TPU v7x, 128 devices: a whole 4x4x4 slice. The times are simulated.
128 devices in a mesh: bx: 8 (over y, core), by: 16 (over z, x).
Axes of the slice: x: 4, y: 4, z: 4, core: 2. Of those that a mesh axis runs over, the one named last changes fastest.
Arguments:
- point_box: int32 [262144, 1], P(('bx', 'by')), may hold values from 0 to 127; in each aligned block of 2048 rows (0 to 2047, 2048 to 4095, ...) at most 32 rows name the same one
- point_offset: int32 [2, 262144], P(None, ('bx', 'by')), may hold values from 0 to 1023
- point_value: float32 [2, 262144], P(None, ('bx', 'by')), may hold values from -0.0625 to 0.0625
- coef: int32 [4], replicated, may hold values from 0 to 31
Outputs:
- weights: float32 [2, 64, 131072], P(None, None, ('bx', 'by'))
Inputs may be any that keep to these rules, and one draw needn't show every extreme that they name: `point_box`: the 2048 points of one device name any one box at most 32 times, a bound that some block reaches.
All inputs are finite; a program needn't handle non-finite values.
Results may differ from a plain program's by a relative error of at most 0.0012.
Values sent between devices are 32-bit elements; how exact they have to be, the bound alone decides.
No kernel may reach another device: no remote copies, remote signals or barrier semaphores. Data moves between devices by JAX's collectives and lax.ppermute only.
A program may use at most 64 MiB of HBM per device.

v0:
```python
import jax
import jax.numpy as jnp
import numpy as np
from jax import lax
from jax.sharding import PartitionSpec as P

N = 16384
ORDER = 8
TGT1 = 32
TGT2 = 32
BLOCK = 256


def from_partner(value, axis, distance):
    return lax.ppermute(value, axis, [(i, i ^ 1 << distance) for i in range(lax.axis_size(axis))])


def node_table():
    counting = np.arange(ORDER) * 1.0
    return 0.5 - 0.5 * np.cos(np.pi * (2.0 * counting + 1.0) / (2.0 * ORDER))


def lagrange(coords):
    nodes = node_table()
    columns = []
    for target in range(ORDER):
        factor = jnp.ones_like(coords)
        for source in range(ORDER):
            if source != target:
                factor = factor * (
                    (coords - float(nodes[source])) * float(1.0 / (nodes[target] - nodes[source]))
                )
        columns.append(factor)
    return jnp.stack(columns, axis=-1)


def child_matrix(side):
    nodes = node_table()
    points = 0.5 * (side + nodes)
    rows_all = []
    for target in range(ORDER):
        factor = np.ones(ORDER)
        for source in range(ORDER):
            if source != target:
                factor = factor * (points - nodes[source]) / (nodes[target] - nodes[source])
        rows_all.append(factor)
    return jnp.asarray(np.stack(rows_all), dtype=jnp.float32)


def phases(tgt_first, tgt_second, freq_first, freq_second, coef):
    scaled = coef.astype(jnp.float32)
    wave = jnp.sin(128.0 * jnp.pi * (tgt_first + tgt_second))
    speed_first = (32.0 + scaled[0] + scaled[1] * wave) / 4096.0
    speed_second = (32.0 + scaled[2] + scaled[3] * wave) / 4096.0
    kfirst = freq_first[:, None]
    ksecond = freq_second[:, None]
    total = (
        tgt_first * kfirst
        + tgt_second * ksecond
        + jnp.sqrt(1.0 + (speed_first * kfirst) ** 2 + (speed_second * ksecond) ** 2)
    )
    fraction = total - jnp.floor(total)
    return (jnp.cos(2.0 * jnp.pi * fraction), jnp.sin(2.0 * jnp.pi * fraction))


def grid_nodes(corner_first, width_first, corner_second, width_second):
    nodes = jnp.asarray(node_table(), dtype=jnp.float32)
    along_first = corner_first + width_first * nodes
    along_second = corner_second + width_second * nodes
    return (
        jnp.broadcast_to(along_first[:, None], (ORDER, ORDER)).reshape(-1),
        jnp.broadcast_to(along_second[None, :], (ORDER, ORDER)).reshape(-1),
    )


def tgt_axis(index, merged, count, boxes):
    code = jnp.zeros((), jnp.int32)
    for bit in range(merged):
        code = code + (index >> bit & 1) * 2 ** (merged - 1 - bit)
    place = jnp.arange(count, dtype=jnp.int32) * 2**merged + code
    return (place.astype(jnp.float32) + 0.5) * (boxes / (N * 2.0**merged))


def centers(index_x, index_y, merged_x, merged_y, boxes_x, boxes_y):
    first = tgt_axis(index_x, merged_x, TGT1, boxes_x)
    second = tgt_axis(index_y, merged_y, TGT2, boxes_y)
    return (
        jnp.broadcast_to(first[:, None], (TGT1, TGT2)).reshape(-1),
        jnp.broadcast_to(second[None, :], (TGT1, TGT2)).reshape(-1),
    )


def leaf_terms(
    columns, corner_first, width_first, corner_second, width_second, tgt_first, tgt_second, coef
):
    cosine, sine = phases(tgt_first, tgt_second, columns[0], columns[1], coef)
    real_in = columns[2][:, None]
    imag_in = columns[3][:, None]
    real_part = cosine * real_in - sine * imag_in
    imag_part = cosine * imag_in + sine * real_in
    basis_first = lagrange((columns[0] - corner_first) / width_first)
    basis_second = lagrange((columns[1] - corner_second) / width_second)
    basis = (basis_first[:, :, None] * basis_second[:, None, :]).reshape(
        columns.shape[1], ORDER * ORDER
    )
    dims = (((0,), (0,)), ((), ()))
    real_sum = lax.dot_general(
        basis, real_part, dims, precision=lax.Precision.HIGHEST, preferred_element_type=jnp.float32
    )
    imag_sum = lax.dot_general(
        basis, imag_part, dims, precision=lax.Precision.HIGHEST, preferred_element_type=jnp.float32
    )
    return (real_sum, imag_sum)


def shift_back(real_sum, imag_sum, node_first, node_second, tgt_first, tgt_second, coef):
    cosine, sine = phases(tgt_first, tgt_second, node_first, node_second, coef)
    return jnp.stack([cosine * real_sum + sine * imag_sum, cosine * imag_sum - sine * real_sum])


def merge_box(
    first_w, second_w, tgt_first, tgt_second, along, corner_d, width_d, corner_o, width_o, coef
):
    spreads = []
    for side, child in ((0, first_w), (1, second_w)):
        start = corner_d + side * width_d
        if along == 1:
            node_first, node_second = grid_nodes(start, width_d, corner_o, width_o)
        else:
            node_first, node_second = grid_nodes(corner_o, width_o, start, width_d)
        cosine, sine = phases(tgt_first, tgt_second, node_first, node_second, coef)
        lifted = jnp.stack(
            [cosine * child[0] - sine * child[1], cosine * child[1] + sine * child[0]]
        )
        lifted = lifted.reshape(2, ORDER, ORDER, -1)
        table = child_matrix(side)
        if along == 1:
            spreads.append(
                jnp.einsum("ts,rsuk->rtuk", table, lifted, precision=lax.Precision.HIGHEST)
            )
        else:
            spreads.append(
                jnp.einsum("us,rtsk->rtuk", table, lifted, precision=lax.Precision.HIGHEST)
            )
    total = (spreads[0] + spreads[1]).reshape(2, ORDER * ORDER, -1)
    if along == 1:
        node_first, node_second = grid_nodes(corner_d, 2.0 * width_d, corner_o, width_o)
    else:
        node_first, node_second = grid_nodes(corner_o, width_o, corner_d, 2.0 * width_d)
    return shift_back(total[0], total[1], node_first, node_second, tgt_first, tgt_second, coef)


def merge_first(holding, partner, index_x, row_y, level, boxes_x, boxes_y, coef):
    width_first = N // boxes_x
    width_second = N // boxes_y
    flag = index_x >> level & 1 == 0
    first_w = jnp.where(flag, holding, partner)
    second_w = jnp.where(flag, partner, holding)
    tgt_first, tgt_second = centers(index_x, row_y, level + 1, level, boxes_x, boxes_y)
    corner_d = ((index_x >> level + 1) * (width_first * 2 ** (level + 1))).astype(jnp.float32)
    corner_o = ((row_y >> level) * (width_second * 2**level)).astype(jnp.float32)
    return merge_box(
        first_w,
        second_w,
        tgt_first,
        tgt_second,
        1,
        corner_d,
        float(width_first * 2**level),
        corner_o,
        float(width_second * 2**level),
        coef,
    )


def merge_second(holding, partner, index_x, index_y, level, boxes_x, boxes_y, coef):
    width_first = N // boxes_x
    width_second = N // boxes_y
    flag = index_y >> level & 1 == 0
    first_w = jnp.where(flag, holding, partner)
    second_w = jnp.where(flag, partner, holding)
    tgt_first, tgt_second = centers(index_x, index_y, level + 1, level + 1, boxes_x, boxes_y)
    corner_d = ((index_y >> level + 1) * (width_second * 2 ** (level + 1))).astype(jnp.float32)
    corner_o = ((index_x >> level + 1) * (width_first * 2 ** (level + 1))).astype(jnp.float32)
    return merge_box(
        first_w,
        second_w,
        tgt_first,
        tgt_second,
        2,
        corner_d,
        float(width_second * 2**level),
        corner_o,
        float(width_first * 2 ** (level + 1)),
        coef,
    )


def pack_slots(box_ids, offsets, values, boxes_y, width_first, width_second, owners, slot_cap):
    ids = box_ids[:, 0]
    onehot = (ids[:, None] == jnp.arange(owners, dtype=jnp.int32)[None, :]).astype(jnp.int32)
    ranks = jnp.sum((jnp.cumsum(onehot, axis=0) - 1) * onehot, axis=1)
    freq_first = (ids // boxes_y * width_first + offsets[0]).astype(jnp.float32)
    freq_second = (ids % boxes_y * width_second + offsets[1]).astype(jnp.float32)
    stacked = jnp.stack([freq_first, freq_second, values[0], values[1]], axis=0)
    slot_of = ids * slot_cap + ranks
    blank = jnp.concatenate(
        [
            jnp.full((2, owners * slot_cap), -1.0, jnp.float32),
            jnp.zeros((2, owners * slot_cap), jnp.float32),
        ],
        axis=0,
    )
    filled = blank.at[:, slot_of].set(stacked)
    return filled.reshape(4, owners, slot_cap).transpose(1, 0, 2).reshape(owners, 4 * slot_cap)


def spread_columns(arrived):
    owners = arrived.shape[0]
    return arrived.reshape(owners, 4, -1).transpose(1, 0, 2).reshape(4, -1)


def trade_first(weights, level):
    return from_partner(weights, "bx", level)


def trade_second(weights, level):
    return from_partner(weights, "by", level)


def on_device(point_box, point_offset, point_value, coef):
    boxes_x = lax.axis_size("bx")
    boxes_y = lax.axis_size("by")
    owners = boxes_x * boxes_y
    slot_cap = 2 * point_box.shape[0] // owners
    width_first = N // boxes_x
    width_second = N // boxes_y
    index_x = lax.axis_index("bx")
    index_y = lax.axis_index("by")
    sent = pack_slots(
        point_box, point_offset, point_value, boxes_y, width_first, width_second, owners, slot_cap
    )
    arrived = lax.all_to_all(sent, ("bx", "by"), split_axis=0, concat_axis=0, tiled=True)
    columns = spread_columns(arrived)
    tgt_first, tgt_second = centers(index_x, index_y, 0, 0, boxes_x, boxes_y)
    slots = columns.shape[1]
    corner_first = (index_x * width_first).astype(jnp.float32)
    corner_second = (index_y * width_second).astype(jnp.float32)
    blocks = slots // BLOCK

    def add_block(number, totals):
        piece = lax.dynamic_slice_in_dim(columns, number * BLOCK, BLOCK, 1)
        real_sum, imag_sum = leaf_terms(
            piece,
            corner_first,
            float(width_first),
            corner_second,
            float(width_second),
            tgt_first,
            tgt_second,
            coef,
        )
        return (totals[0] + real_sum, totals[1] + imag_sum)

    empty = jnp.zeros((ORDER * ORDER, TGT1 * TGT2), jnp.float32)
    real_sum, imag_sum = lax.fori_loop(0, blocks, add_block, (empty, empty))
    node_first, node_second = grid_nodes(
        corner_first, float(width_first), corner_second, float(width_second)
    )
    holding = shift_back(real_sum, imag_sum, node_first, node_second, tgt_first, tgt_second, coef)
    first_level = 0
    for level in range(first_level, 2):
        partner = trade_first(holding, level)
        holding = merge_first(holding, partner, index_x, index_y, level, boxes_x, boxes_y, coef)
        partner = trade_second(holding, level)
        holding = merge_second(holding, partner, index_x, index_y, level, boxes_x, boxes_y, coef)
    return holding


def solution(mesh):
    in_specs = (P(("bx", "by"), None), P(None, ("bx", "by")), P(None, ("bx", "by")), P())
    out_specs = P(None, None, ("bx", "by"))
    return jax.shard_map(
        on_device, mesh=mesh, in_specs=in_specs, out_specs=out_specs, check_vma=False
    )
```

profile of v0, /device:TPU:0, one launch (start us, length us, event | category | flops | bytes accessed | tf_op | source)
XLA Modules:
  0.0 315.2 jit_solution(123902947368702181)
XLA Ops:
  3.1 1.5 copy-done
  4.7 6.4 %scatter_fusion = f32[4,4096]{0,1:T(8,128)S(1)} fusion(f32[4,4096]{0,1:T(8,128)S(1)} %copy-done, s32[2048]{0:T(1024)S(1)} %bitcast.230, f32[2048,4]{1,0:T(8,128)S(1)} %copy.47), kind=kCustom, calls=%fused_computation | custom fusion | bytes 106496 | tf_op jit(solution)/shard_map/scatter | solution.py:214
  13.1 11.6 %all-to-all-start = ((f32[128,1,128]{2,1,0:T(1,128)}), f32[128,1,128]{2,1,0:T(1,128)S(1)}, u32[]{:S(2)}, u32[]{:S(2)}) async-start(f32[128,1,128]{2,1,0:T(1,128)} %copy.49), calls=%async_computation | async-start | bytes 131072 | tf_op jit(solution)/shard_map/all_to_all | solution.py:243
  27.4 1.4 add_multiply_fusion.11
  29.1 5.1 %all-to-all-done = f32[128,1,128]{2,1,0:T(1,128)S(1)} async-done(((f32[128,1,128]{2,1,0:T(1,128)}), f32[128,1,128]{2,1,0:T(1,128)S(1)}, u32[]{:S(2)}, u32[]{:S(2)}) %all-to-all-start) | async-done | bytes 65568 | tf_op jit(solution)/shard_map/all_to_all | solution.py:243
  34.6 213.5 %while.22 = (s32[]{:T(128)}, f32[64,1024]{1,0:T(8,128)S(1)}, f32[64,1024]{1,0:T(8,128)S(1)}, f32[4,4096]{1,0:T(4,128)S(1)}, f32[]{:T(128)}, /*index=5*/f32[]{:T(...) while((s32[]{:T(128)}, f32[64,1024]{1,0:T(8,128)S(1)}, ...), condition=%wide.region_5.6_spmd.clone.clone.clone.clone, body=%wide.region_4.5_spmd.clone.clone.clone.clone.sunk | while | flops 411406848 | bytes 1233722 | solution.py:266
  35.7 1.5 add_multiply_fusion.17
  37.3 5.3 %convolution_add_fusion.9 = f32[64,1024]{1,0:T(8,128)S(1)} fusion(f32[256]{0:T(256)S(1)} %bitcast.238, f32[256]{0:T(256)S(1)} %bitcast.234, f32[1024]{0:T(1024)S(1)} %bitcast.228, f32[1024]{0:T(1024)S(1)} %bitcast.226, f32[256]{0:T(256)S(1)} %bitcast.236, f32[1024]{0:T(1024)S(1)} %mul.9766, f32[256]{0:T(256)S(1)} %bitcast.232, f32[1024]{0:T(1024)S(1)} %mul.9767, ...), kind=kOutput, calls=%fused_computation.5.clone.1 | convolution fusion | flops 205668352 | bytes 561153 | tf_op jit(solution)/shard_map/while/body/eval_jaxpr/dot_general | solution.py:110
  42.6 5.3 %convolution_add_fusion.8 = f32[64,1024]{1,0:T(8,128)S(1)} fusion(f32[256]{0:T(256)S(1)} %bitcast.239, f32[256]{0:T(256)S(1)} %bitcast.235, f32[1024]{0:T(1024)S(1)} %bitcast.229, f32[1024]{0:T(1024)S(1)} %bitcast.227, f32[256]{0:T(256)S(1)} %bitcast.237, f32[1024]{0:T(1024)S(1)} %mul.9766, f32[256]{0:T(256)S(1)} %bitcast.233, f32[1024]{0:T(1024)S(1)} %mul.9767, ...), kind=kOutput, calls=%fused_computation.6.clone.1 | convolution fusion | flops 205668352 | bytes 561153 | tf_op jit(solution)/shard_map/while/body/eval_jaxpr/dot_general | solution.py:107
  49.0 1.5 add_multiply_fusion.17
  50.7 5.3 %convolution_add_fusion.9 = f32[64,1024]{1,0:T(8,128)S(1)} fusion(f32[256]{0:T(256)S(1)} %bitcast.238, f32[256]{0:T(256)S(1)} %bitcast.234, f32[1024]{0:T(1024)S(1)} %bitcast.228, f32[1024]{0:T(1024)S(1)} %bitcast.226, f32[256]{0:T(256)S(1)} %bitcast.236, f32[1024]{0:T(1024)S(1)} %mul.9766, f32[256]{0:T(256)S(1)} %bitcast.232, f32[1024]{0:T(1024)S(1)} %mul.9767, ...), kind=kOutput, calls=%fused_computation.5.clone.1 | convolution fusion | flops 205668352 | bytes 561153 | tf_op jit(solution)/shard_map/while/body/eval_jaxpr/dot_general | solution.py:110
  56.0 5.3 %convolution_add_fusion.8 = f32[64,1024]{1,0:T(8,128)S(1)} fusion(f32[256]{0:T(256)S(1)} %bitcast.239, f32[256]{0:T(256)S(1)} %bitcast.235, f32[1024]{0:T(1024)S(1)} %bitcast.229, f32[1024]{0:T(1024)S(1)} %bitcast.227, f32[256]{0:T(256)S(1)} %bitcast.237, f32[1024]{0:T(1024)S(1)} %mul.9766, f32[256]{0:T(256)S(1)} %bitcast.233, f32[1024]{0:T(1024)S(1)} %mul.9767, ...), kind=kOutput, calls=%fused_computation.6.clone.1 | convolution fusion | flops 205668352 | bytes 561153 | tf_op jit(solution)/shard_map/while/body/eval_jaxpr/dot_general | solution.py:107
  62.3 1.5 add_multiply_fusion.17
  64.0 5.3 %convolution_add_fusion.9 = f32[64,1024]{1,0:T(8,128)S(1)} fusion(f32[256]{0:T(256)S(1)} %bitcast.238, f32[256]{0:T(256)S(1)} %bitcast.234, f32[1024]{0:T(1024)S(1)} %bitcast.228, f32[1024]{0:T(1024)S(1)} %bitcast.226, f32[256]{0:T(256)S(1)} %bitcast.236, f32[1024]{0:T(1024)S(1)} %mul.9766, f32[256]{0:T(256)S(1)} %bitcast.232, f32[1024]{0:T(1024)S(1)} %mul.9767, ...), kind=kOutput, calls=%fused_computation.5.clone.1 | convolution fusion | flops 205668352 | bytes 561153 | tf_op jit(solution)/shard_map/while/body/eval_jaxpr/dot_general | solution.py:110
  69.3 5.3 %convolution_add_fusion.8 = f32[64,1024]{1,0:T(8,128)S(1)} fusion(f32[256]{0:T(256)S(1)} %bitcast.239, f32[256]{0:T(256)S(1)} %bitcast.235, f32[1024]{0:T(1024)S(1)} %bitcast.229, f32[1024]{0:T(1024)S(1)} %bitcast.227, f32[256]{0:T(256)S(1)} %bitcast.237, f32[1024]{0:T(1024)S(1)} %mul.9766, f32[256]{0:T(256)S(1)} %bitcast.233, f32[1024]{0:T(1024)S(1)} %mul.9767, ...), kind=kOutput, calls=%fused_computation.6.clone.1 | convolution fusion | flops 205668352 | bytes 561153 | tf_op jit(solution)/shard_map/while/body/eval_jaxpr/dot_general | solution.py:107
  75.7 1.5 add_multiply_fusion.17
  77.3 5.3 %convolution_add_fusion.9 = f32[64,1024]{1,0:T(8,128)S(1)} fusion(f32[256]{0:T(256)S(1)} %bitcast.238, f32[256]{0:T(256)S(1)} %bitcast.234, f32[1024]{0:T(1024)S(1)} %bitcast.228, f32[1024]{0:T(1024)S(1)} %bitcast.226, f32[256]{0:T(256)S(1)} %bitcast.236, f32[1024]{0:T(1024)S(1)} %mul.9766, f32[256]{0:T(256)S(1)} %bitcast.232, f32[1024]{0:T(1024)S(1)} %mul.9767, ...), kind=kOutput, calls=%fused_computation.5.clone.1 | convolution fusion | flops 205668352 | bytes 561153 | tf_op jit(solution)/shard_map/while/body/eval_jaxpr/dot_general | solution.py:110
  82.6 5.3 %convolution_add_fusion.8 = f32[64,1024]{1,0:T(8,128)S(1)} fusion(f32[256]{0:T(256)S(1)} %bitcast.239, f32[256]{0:T(256)S(1)} %bitcast.235, f32[1024]{0:T(1024)S(1)} %bitcast.229, f32[1024]{0:T(1024)S(1)} %bitcast.227, f32[256]{0:T(256)S(1)} %bitcast.237, f32[1024]{0:T(1024)S(1)} %mul.9766, f32[256]{0:T(256)S(1)} %bitcast.233, f32[1024]{0:T(1024)S(1)} %mul.9767, ...), kind=kOutput, calls=%fused_computation.6.clone.1 | convolution fusion | flops 205668352 | bytes 561153 | tf_op jit(solution)/shard_map/while/body/eval_jaxpr/dot_general | solution.py:107
  89.0 1.5 add_multiply_fusion.17
  90.7 5.3 %convolution_add_fusion.9 = f32[64,1024]{1,0:T(8,128)S(1)} fusion(f32[256]{0:T(256)S(1)} %bitcast.238, f32[256]{0:T(256)S(1)} %bitcast.234, f32[1024]{0:T(1024)S(1)} %bitcast.228, f32[1024]{0:T(1024)S(1)} %bitcast.226, f32[256]{0:T(256)S(1)} %bitcast.236, f32[1024]{0:T(1024)S(1)} %mul.9766, f32[256]{0:T(256)S(1)} %bitcast.232, f32[1024]{0:T(1024)S(1)} %mul.9767, ...), kind=kOutput, calls=%fused_computation.5.clone.1 | convolution fusion | flops 205668352 | bytes 561153 | tf_op jit(solution)/shard_map/while/body/eval_jaxpr/dot_general | solution.py:110
  96.0 5.3 %convolution_add_fusion.8 = f32[64,1024]{1,0:T(8,128)S(1)} fusion(f32[256]{0:T(256)S(1)} %bitcast.239, f32[256]{0:T(256)S(1)} %bitcast.235, f32[1024]{0:T(1024)S(1)} %bitcast.229, f32[1024]{0:T(1024)S(1)} %bitcast.227, f32[256]{0:T(256)S(1)} %bitcast.237, f32[1024]{0:T(1024)S(1)} %mul.9766, f32[256]{0:T(256)S(1)} %bitcast.233, f32[1024]{0:T(1024)S(1)} %mul.9767, ...), kind=kOutput, calls=%fused_computation.6.clone.1 | convolution fusion | flops 205668352 | bytes 561153 | tf_op jit(solution)/shard_map/while/body/eval_jaxpr/dot_general | solution.py:107
  102.3 1.5 add_multiply_fusion.17
  104.0 5.3 %convolution_add_fusion.9 = f32[64,1024]{1,0:T(8,128)S(1)} fusion(f32[256]{0:T(256)S(1)} %bitcast.238, f32[256]{0:T(256)S(1)} %bitcast.234, f32[1024]{0:T(1024)S(1)} %bitcast.228, f32[1024]{0:T(1024)S(1)} %bitcast.226, f32[256]{0:T(256)S(1)} %bitcast.236, f32[1024]{0:T(1024)S(1)} %mul.9766, f32[256]{0:T(256)S(1)} %bitcast.232, f32[1024]{0:T(1024)S(1)} %mul.9767, ...), kind=kOutput, calls=%fused_computation.5.clone.1 | convolution fusion | flops 205668352 | bytes 561153 | tf_op jit(solution)/shard_map/while/body/eval_jaxpr/dot_general | solution.py:110
  109.3 5.3 %convolution_add_fusion.8 = f32[64,1024]{1,0:T(8,128)S(1)} fusion(f32[256]{0:T(256)S(1)} %bitcast.239, f32[256]{0:T(256)S(1)} %bitcast.235, f32[1024]{0:T(1024)S(1)} %bitcast.229, f32[1024]{0:T(1024)S(1)} %bitcast.227, f32[256]{0:T(256)S(1)} %bitcast.237, f32[1024]{0:T(1024)S(1)} %mul.9766, f32[256]{0:T(256)S(1)} %bitcast.233, f32[1024]{0:T(1024)S(1)} %mul.9767, ...), kind=kOutput, calls=%fused_computation.6.clone.1 | convolution fusion | flops 205668352 | bytes 561153 | tf_op jit(solution)/shard_map/while/body/eval_jaxpr/dot_general | solution.py:107
  115.7 1.5 add_multiply_fusion.17
  117.3 5.3 %convolution_add_fusion.9 = f32[64,1024]{1,0:T(8,128)S(1)} fusion(f32[256]{0:T(256)S(1)} %bitcast.238, f32[256]{0:T(256)S(1)} %bitcast.234, f32[1024]{0:T(1024)S(1)} %bitcast.228, f32[1024]{0:T(1024)S(1)} %bitcast.226, f32[256]{0:T(256)S(1)} %bitcast.236, f32[1024]{0:T(1024)S(1)} %mul.9766, f32[256]{0:T(256)S(1)} %bitcast.232, f32[1024]{0:T(1024)S(1)} %mul.9767, ...), kind=kOutput, calls=%fused_computation.5.clone.1 | convolution fusion | flops 205668352 | bytes 561153 | tf_op jit(solution)/shard_map/while/body/eval_jaxpr/dot_general | solution.py:110
  122.6 5.3 %convolution_add_fusion.8 = f32[64,1024]{1,0:T(8,128)S(1)} fusion(f32[256]{0:T(256)S(1)} %bitcast.239, f32[256]{0:T(256)S(1)} %bitcast.235, f32[1024]{0:T(1024)S(1)} %bitcast.229, f32[1024]{0:T(1024)S(1)} %bitcast.227, f32[256]{0:T(256)S(1)} %bitcast.237, f32[1024]{0:T(1024)S(1)} %mul.9766, f32[256]{0:T(256)S(1)} %bitcast.233, f32[1024]{0:T(1024)S(1)} %mul.9767, ...), kind=kOutput, calls=%fused_computation.6.clone.1 | convolution fusion | flops 205668352 | bytes 561153 | tf_op jit(solution)/shard_map/while/body/eval_jaxpr/dot_general | solution.py:107
  129.0 1.5 add_multiply_fusion.17
  130.7 5.3 %convolution_add_fusion.9 = f32[64,1024]{1,0:T(8,128)S(1)} fusion(f32[256]{0:T(256)S(1)} %bitcast.238, f32[256]{0:T(256)S(1)} %bitcast.234, f32[1024]{0:T(1024)S(1)} %bitcast.228, f32[1024]{0:T(1024)S(1)} %bitcast.226, f32[256]{0:T(256)S(1)} %bitcast.236, f32[1024]{0:T(1024)S(1)} %mul.9766, f32[256]{0:T(256)S(1)} %bitcast.232, f32[1024]{0:T(1024)S(1)} %mul.9767, ...), kind=kOutput, calls=%fused_computation.5.clone.1 | convolution fusion | flops 205668352 | bytes 561153 | tf_op jit(solution)/shard_map/while/body/eval_jaxpr/dot_general | solution.py:110
  136.0 5.3 %convolution_add_fusion.8 = f32[64,1024]{1,0:T(8,128)S(1)} fusion(f32[256]{0:T(256)S(1)} %bitcast.239, f32[256]{0:T(256)S(1)} %bitcast.235, f32[1024]{0:T(1024)S(1)} %bitcast.229, f32[1024]{0:T(1024)S(1)} %bitcast.227, f32[256]{0:T(256)S(1)} %bitcast.237, f32[1024]{0:T(1024)S(1)} %mul.9766, f32[256]{0:T(256)S(1)} %bitcast.233, f32[1024]{0:T(1024)S(1)} %mul.9767, ...), kind=kOutput, calls=%fused_computation.6.clone.1 | convolution fusion | flops 205668352 | bytes 561153 | tf_op jit(solution)/shard_map/while/body/eval_jaxpr/dot_general | solution.py:107
  142.3 1.5 add_multiply_fusion.17
  144.0 5.3 %convolution_add_fusion.9 = f32[64,1024]{1,0:T(8,128)S(1)} fusion(f32[256]{0:T(256)S(1)} %bitcast.238, f32[256]{0:T(256)S(1)} %bitcast.234, f32[1024]{0:T(1024)S(1)} %bitcast.228, f32[1024]{0:T(1024)S(1)} %bitcast.226, f32[256]{0:T(256)S(1)} %bitcast.236, f32[1024]{0:T(1024)S(1)} %mul.9766, f32[256]{0:T(256)S(1)} %bitcast.232, f32[1024]{0:T(1024)S(1)} %mul.9767, ...), kind=kOutput, calls=%fused_computation.5.clone.1 | convolution fusion | flops 205668352 | bytes 561153 | tf_op jit(solution)/shard_map/while/body/eval_jaxpr/dot_general | solution.py:110
  149.3 5.3 %convolution_add_fusion.8 = f32[64,1024]{1,0:T(8,128)S(1)} fusion(f32[256]{0:T(256)S(1)} %bitcast.239, f32[256]{0:T(256)S(1)} %bitcast.235, f32[1024]{0:T(1024)S(1)} %bitcast.229, f32[1024]{0:T(1024)S(1)} %bitcast.227, f32[256]{0:T(256)S(1)} %bitcast.237, f32[1024]{0:T(1024)S(1)} %mul.9766, f32[256]{0:T(256)S(1)} %bitcast.233, f32[1024]{0:T(1024)S(1)} %mul.9767, ...), kind=kOutput, calls=%fused_computation.6.clone.1 | convolution fusion | flops 205668352 | bytes 561153 | tf_op jit(solution)/shard_map/while/body/eval_jaxpr/dot_general | solution.py:107
  155.7 1.5 add_multiply_fusion.17
  157.4 5.3 %convolution_add_fusion.9 = f32[64,1024]{1,0:T(8,128)S(1)} fusion(f32[256]{0:T(256)S(1)} %bitcast.238, f32[256]{0:T(256)S(1)} %bitcast.234, f32[1024]{0:T(1024)S(1)} %bitcast.228, f32[1024]{0:T(1024)S(1)} %bitcast.226, f32[256]{0:T(256)S(1)} %bitcast.236, f32[1024]{0:T(1024)S(1)} %mul.9766, f32[256]{0:T(256)S(1)} %bitcast.232, f32[1024]{0:T(1024)S(1)} %mul.9767, ...), kind=kOutput, calls=%fused_computation.5.clone.1 | convolution fusion | flops 205668352 | bytes 561153 | tf_op jit(solution)/shard_map/while/body/eval_jaxpr/dot_general | solution.py:110
  162.7 5.3 %convolution_add_fusion.8 = f32[64,1024]{1,0:T(8,128)S(1)} fusion(f32[256]{0:T(256)S(1)} %bitcast.239, f32[256]{0:T(256)S(1)} %bitcast.235, f32[1024]{0:T(1024)S(1)} %bitcast.229, f32[1024]{0:T(1024)S(1)} %bitcast.227, f32[256]{0:T(256)S(1)} %bitcast.237, f32[1024]{0:T(1024)S(1)} %mul.9766, f32[256]{0:T(256)S(1)} %bitcast.233, f32[1024]{0:T(1024)S(1)} %mul.9767, ...), kind=kOutput, calls=%fused_computation.6.clone.1 | convolution fusion | flops 205668352 | bytes 561153 | tf_op jit(solution)/shard_map/while/body/eval_jaxpr/dot_general | solution.py:107
  169.0 1.5 add_multiply_fusion.17
  170.7 5.3 %convolution_add_fusion.9 = f32[64,1024]{1,0:T(8,128)S(1)} fusion(f32[256]{0:T(256)S(1)} %bitcast.238, f32[256]{0:T(256)S(1)} %bitcast.234, f32[1024]{0:T(1024)S(1)} %bitcast.228, f32[1024]{0:T(1024)S(1)} %bitcast.226, f32[256]{0:T(256)S(1)} %bitcast.236, f32[1024]{0:T(1024)S(1)} %mul.9766, f32[256]{0:T(256)S(1)} %bitcast.232, f32[1024]{0:T(1024)S(1)} %mul.9767, ...), kind=kOutput, calls=%fused_computation.5.clone.1 | convolution fusion | flops 205668352 | bytes 561153 | tf_op jit(solution)/shard_map/while/body/eval_jaxpr/dot_general | solution.py:110
  176.0 5.3 %convolution_add_fusion.8 = f32[64,1024]{1,0:T(8,128)S(1)} fusion(f32[256]{0:T(256)S(1)} %bitcast.239, f32[256]{0:T(256)S(1)} %bitcast.235, f32[1024]{0:T(1024)S(1)} %bitcast.229, f32[1024]{0:T(1024)S(1)} %bitcast.227, f32[256]{0:T(256)S(1)} %bitcast.237, f32[1024]{0:T(1024)S(1)} %mul.9766, f32[256]{0:T(256)S(1)} %bitcast.233, f32[1024]{0:T(1024)S(1)} %mul.9767, ...), kind=kOutput, calls=%fused_computation.6.clone.1 | convolution fusion | flops 205668352 | bytes 561153 | tf_op jit(solution)/shard_map/while/body/eval_jaxpr/dot_general | solution.py:107
  182.3 1.5 add_multiply_fusion.17
  184.0 5.3 %convolution_add_fusion.9 = f32[64,1024]{1,0:T(8,128)S(1)} fusion(f32[256]{0:T(256)S(1)} %bitcast.238, f32[256]{0:T(256)S(1)} %bitcast.234, f32[1024]{0:T(1024)S(1)} %bitcast.228, f32[1024]{0:T(1024)S(1)} %bitcast.226, f32[256]{0:T(256)S(1)} %bitcast.236, f32[1024]{0:T(1024)S(1)} %mul.9766, f32[256]{0:T(256)S(1)} %bitcast.232, f32[1024]{0:T(1024)S(1)} %mul.9767, ...), kind=kOutput, calls=%fused_computation.5.clone.1 | convolution fusion | flops 205668352 | bytes 561153 | tf_op jit(solution)/shard_map/while/body/eval_jaxpr/dot_general | solution.py:110
  189.3 5.3 %convolution_add_fusion.8 = f32[64,1024]{1,0:T(8,128)S(1)} fusion(f32[256]{0:T(256)S(1)} %bitcast.239, f32[256]{0:T(256)S(1)} %bitcast.235, f32[1024]{0:T(1024)S(1)} %bitcast.229, f32[1024]{0:T(1024)S(1)} %bitcast.227, f32[256]{0:T(256)S(1)} %bitcast.237, f32[1024]{0:T(1024)S(1)} %mul.9766, f32[256]{0:T(256)S(1)} %bitcast.233, f32[1024]{0:T(1024)S(1)} %mul.9767, ...), kind=kOutput, calls=%fused_computation.6.clone.1 | convolution fusion | flops 205668352 | bytes 561153 | tf_op jit(solution)/shard_map/while/body/eval_jaxpr/dot_general | solution.py:107
  195.7 1.5 add_multiply_fusion.17
  197.4 5.3 %convolution_add_fusion.9 = f32[64,1024]{1,0:T(8,128)S(1)} fusion(f32[256]{0:T(256)S(1)} %bitcast.238, f32[256]{0:T(256)S(1)} %bitcast.234, f32[1024]{0:T(1024)S(1)} %bitcast.228, f32[1024]{0:T(1024)S(1)} %bitcast.226, f32[256]{0:T(256)S(1)} %bitcast.236, f32[1024]{0:T(1024)S(1)} %mul.9766, f32[256]{0:T(256)S(1)} %bitcast.232, f32[1024]{0:T(1024)S(1)} %mul.9767, ...), kind=kOutput, calls=%fused_computation.5.clone.1 | convolution fusion | flops 205668352 | bytes 561153 | tf_op jit(solution)/shard_map/while/body/eval_jaxpr/dot_general | solution.py:110
  202.7 5.3 %convolution_add_fusion.8 = f32[64,1024]{1,0:T(8,128)S(1)} fusion(f32[256]{0:T(256)S(1)} %bitcast.239, f32[256]{0:T(256)S(1)} %bitcast.235, f32[1024]{0:T(1024)S(1)} %bitcast.229, f32[1024]{0:T(1024)S(1)} %bitcast.227, f32[256]{0:T(256)S(1)} %bitcast.237, f32[1024]{0:T(1024)S(1)} %mul.9766, f32[256]{0:T(256)S(1)} %bitcast.233, f32[1024]{0:T(1024)S(1)} %mul.9767, ...), kind=kOutput, calls=%fused_computation.6.clone.1 | convolution fusion | flops 205668352 | bytes 561153 | tf_op jit(solution)/shard_map/while/body/eval_jaxpr/dot_general | solution.py:107
  209.0 1.5 add_multiply_fusion.17
  210.7 5.3 %convolution_add_fusion.9 = f32[64,1024]{1,0:T(8,128)S(1)} fusion(f32[256]{0:T(256)S(1)} %bitcast.238, f32[256]{0:T(256)S(1)} %bitcast.234, f32[1024]{0:T(1024)S(1)} %bitcast.228, f32[1024]{0:T(1024)S(1)} %bitcast.226, f32[256]{0:T(256)S(1)} %bitcast.236, f32[1024]{0:T(1024)S(1)} %mul.9766, f32[256]{0:T(256)S(1)} %bitcast.232, f32[1024]{0:T(1024)S(1)} %mul.9767, ...), kind=kOutput, calls=%fused_computation.5.clone.1 | convolution fusion | flops 205668352 | bytes 561153 | tf_op jit(solution)/shard_map/while/body/eval_jaxpr/dot_general | solution.py:110
  216.0 5.3 %convolution_add_fusion.8 = f32[64,1024]{1,0:T(8,128)S(1)} fusion(f32[256]{0:T(256)S(1)} %bitcast.239, f32[256]{0:T(256)S(1)} %bitcast.235, f32[1024]{0:T(1024)S(1)} %bitcast.229, f32[1024]{0:T(1024)S(1)} %bitcast.227, f32[256]{0:T(256)S(1)} %bitcast.237, f32[1024]{0:T(1024)S(1)} %mul.9766, f32[256]{0:T(256)S(1)} %bitcast.233, f32[1024]{0:T(1024)S(1)} %mul.9767, ...), kind=kOutput, calls=%fused_computation.6.clone.1 | convolution fusion | flops 205668352 | bytes 561153 | tf_op jit(solution)/shard_map/while/body/eval_jaxpr/dot_general | solution.py:107
  222.3 1.5 add_multiply_fusion.17
  224.0 5.3 %convolution_add_fusion.9 = f32[64,1024]{1,0:T(8,128)S(1)} fusion(f32[256]{0:T(256)S(1)} %bitcast.238, f32[256]{0:T(256)S(1)} %bitcast.234, f32[1024]{0:T(1024)S(1)} %bitcast.228, f32[1024]{0:T(1024)S(1)} %bitcast.226, f32[256]{0:T(256)S(1)} %bitcast.236, f32[1024]{0:T(1024)S(1)} %mul.9766, f32[256]{0:T(256)S(1)} %bitcast.232, f32[1024]{0:T(1024)S(1)} %mul.9767, ...), kind=kOutput, calls=%fused_computation.5.clone.1 | convolution fusion | flops 205668352 | bytes 561153 | tf_op jit(solution)/shard_map/while/body/eval_jaxpr/dot_general | solution.py:110
  229.3 5.3 %convolution_add_fusion.8 = f32[64,1024]{1,0:T(8,128)S(1)} fusion(f32[256]{0:T(256)S(1)} %bitcast.239, f32[256]{0:T(256)S(1)} %bitcast.235, f32[1024]{0:T(1024)S(1)} %bitcast.229, f32[1024]{0:T(1024)S(1)} %bitcast.227, f32[256]{0:T(256)S(1)} %bitcast.237, f32[1024]{0:T(1024)S(1)} %mul.9766, f32[256]{0:T(256)S(1)} %bitcast.233, f32[1024]{0:T(1024)S(1)} %mul.9767, ...), kind=kOutput, calls=%fused_computation.6.clone.1 | convolution fusion | flops 205668352 | bytes 561153 | tf_op jit(solution)/shard_map/while/body/eval_jaxpr/dot_general | solution.py:107
  235.7 1.5 add_multiply_fusion.17
  237.4 5.3 %convolution_add_fusion.9 = f32[64,1024]{1,0:T(8,128)S(1)} fusion(f32[256]{0:T(256)S(1)} %bitcast.238, f32[256]{0:T(256)S(1)} %bitcast.234, f32[1024]{0:T(1024)S(1)} %bitcast.228, f32[1024]{0:T(1024)S(1)} %bitcast.226, f32[256]{0:T(256)S(1)} %bitcast.236, f32[1024]{0:T(1024)S(1)} %mul.9766, f32[256]{0:T(256)S(1)} %bitcast.232, f32[1024]{0:T(1024)S(1)} %mul.9767, ...), kind=kOutput, calls=%fused_computation.5.clone.1 | convolution fusion | flops 205668352 | bytes 561153 | tf_op jit(solution)/shard_map/while/body/eval_jaxpr/dot_general | solution.py:110
  242.7 5.3 %convolution_add_fusion.8 = f32[64,1024]{1,0:T(8,128)S(1)} fusion(f32[256]{0:T(256)S(1)} %bitcast.239, f32[256]{0:T(256)S(1)} %bitcast.235, f32[1024]{0:T(1024)S(1)} %bitcast.229, f32[1024]{0:T(1024)S(1)} %bitcast.227, f32[256]{0:T(256)S(1)} %bitcast.237, f32[1024]{0:T(1024)S(1)} %mul.9766, f32[256]{0:T(256)S(1)} %bitcast.233, f32[1024]{0:T(1024)S(1)} %mul.9767, ...), kind=kOutput, calls=%fused_computation.6.clone.1 | convolution fusion | flops 205668352 | bytes 561153 | tf_op jit(solution)/shard_map/while/body/eval_jaxpr/dot_general | solution.py:107
  250.1 1.3 collective-permute-done
  251.5 2.4 subtract_bitcast_fusion.6
  255.9 1.3 fusion.114
  258.2 13.1 %collective-permute-done.1 = f32[2,64,1024]{2,1,0:T(8,128)S(1)} collective-permute-done((f32[2,64,1024]{2,1,0:T(8,128)S(1)}, f32[2,64,1024]{2,1,0:T(8,128)S(1)}, u32[]{:S(2)}, u32[]{:S(2)}) %collective-permute-start.1) | collective-permute-done | bytes 524320 | tf_op jit(solution)/shard_map/ppermute | solution.py:15
  271.4 2.4 subtract_bitcast_fusion.4
  277.4 12.1 %collective-permute-done.2 = f32[2,64,1024]{2,1,0:T(8,128)S(1)} collective-permute-done((f32[2,64,1024]{2,1,0:T(8,128)S(1)}, f32[2,64,1024]{2,1,0:T(8,128)S(1)}, u32[]{:S(2)}, u32[]{:S(2)}) %collective-permute-start.2) | collective-permute-done | bytes 524320 | tf_op jit(solution)/shard_map/ppermute | solution.py:15
  289.6 2.6 subtract_bitcast_fusion.2
  294.1 1.3 fusion.112
  296.7 12.5 %collective-permute-done.3 = f32[2,64,1024]{2,1,0:T(8,128)S(1)} collective-permute-done((f32[2,64,1024]{2,1,0:T(8,128)S(1)}, f32[2,64,1024]{2,1,0:T(8,128)S(1)}, u32[]{:S(2)}, u32[]{:S(2)}) %collective-permute-start.3) | collective-permute-done | bytes 524320 | tf_op jit(solution)/shard_map/ppermute | solution.py:15
  309.3 2.4 subtract_bitcast_fusion
  (301 shorter events, 41.8 us)
Async XLA Ops:
  1.2 0.7 copy-start.1
  1.3 1.3 copy-start.4
  1.3 1.4 copy-start.5
  3.1 1.6 copy-start
  3.1 22.2 %copy-start.10 = (s32[4]{0:T(128)S(1)}, s32[4]{0:T(128)}, u32[]{:S(2)}) copy-start(s32[4]{0:T(128)} %param.30) | copy-start | bytes 52
  3.1 25.7 %copy-start.8 = (f32[8]{0:T(128)S(1)}, f32[8]{0:T(128)}, u32[]{:S(2)}) copy-start(f32[8]{0:T(128)} %constant.642) | copy-start | bytes 100
  3.1 25.7 %copy-start.9 = (f32[8]{0:T(128)S(1)}, f32[8]{0:T(128)}, u32[]{:S(2)}) copy-start(f32[8]{0:T(128)} %constant.643) | copy-start | bytes 100
  13.1 21.1 %all-to-all-start = ((f32[128,1,128]{2,1,0:T(1,128)}), f32[128,1,128]{2,1,0:T(1,128)S(1)}, u32[]{:S(2)}, u32[]{:S(2)}) async-start(f32[128,1,128]{2,1,0:T(1,128)} %copy.49), calls=%async_computation | async-start | bytes 131072 | tf_op jit(solution)/shard_map/all_to_all | solution.py:243
  248.1 1.8 copy-start.6
  248.2 1.8 copy-start.7
  249.4 2.0 collective-permute-start
  251.5 3.1 copy-start.3
  254.0 1.2 copy-start.2
  257.2 14.0 %collective-permute-start.1 = (f32[2,64,1024]{2,1,0:T(8,128)S(1)}, f32[2,64,1024]{2,1,0:T(8,128)S(1)}, u32[]{:S(2)}, u32[]{:S(2)}) collective-permute-start(f32[2,64,1024]{2,1,0:T(8,128)S(1)} %pad_maximum_fusion.1), channel_id=1, source_target_pairs={{0,1},{1,0},{2,3},{3,2},{4,5},{5,4},{6,7},{7,6},{8,9},{9,8},{10,11... | collective-permute-start | bytes 1572872 | tf_op jit(solution)/shard_map/ppermute | solution.py:15
  276.3 13.2 %collective-permute-start.2 = (f32[2,64,1024]{2,1,0:T(8,128)S(1)}, f32[2,64,1024]{2,1,0:T(8,128)S(1)}, u32[]{:S(2)}, u32[]{:S(2)}) collective-permute-start(f32[2,64,1024]{2,1,0:T(8,128)S(1)} %pad_maximum_fusion.2), channel_id=1, source_target_pairs={{0,32},{16,48},{32,0},{48,16},{64,96},{80,112},{96,64},{112,80},{1... | collective-permute-start | bytes 1572872 | tf_op jit(solution)/shard_map/ppermute | solution.py:15
  295.4 13.8 %collective-permute-start.3 = (f32[2,64,1024]{2,1,0:T(8,128)S(1)}, f32[2,64,1024]{2,1,0:T(8,128)S(1)}, u32[]{:S(2)}, u32[]{:S(2)}) collective-permute-start(f32[2,64,1024]{2,1,0:T(8,128)S(1)} %pad_maximum_fusion.3), channel_id=1, source_target_pairs={{0,2},{1,3},{2,0},{3,1},{4,6},{5,7},{6,4},{7,5},{8,10},{9,11},{10,... | collective-permute-start | bytes 1572872 | tf_op jit(solution)/shard_map/ppermute | solution.py:15
where the time goes:
time: 320 us; the launch traced here: 315 us
  matrix products  174 us (54%)
  other arithmetic  47.2 us (15%)
  waiting for transfers between devices  44.1 us (14%)
  local copies, waits for them, and re-layouts  32.8 us (10%)
  starting transfers between devices  14 us (4%)
    dot_general x16, matrix products, leaf_terms(): lax.dot_general(basis, real_part, dims, precision=lax.Precision.HIGHEST,...  84.6 us
    dot_general x16, matrix products, leaf_terms(): lax.dot_general(basis, imag_part, dims, precision=lax.Precision.HIGHEST,...  84.6 us
    ppermute x4, waiting for transfers between devices, from_partner(): lax.ppermute(value, axis, [(i, i ^ 1 << distance) for i in range(lax.axis...  39.1 us
    div x17, other arithmetic, phases(): speed_first = (32.0 + scaled[0] + scaled[1] * wave) / 4096.0  24.7 us
    all_to_all x1, starting transfers between devices, on_device(): lax.all_to_all(sent, ('bx', 'by'), split_axis=0, concat_axis=0, tiled=True)  11.6 us
    slice x17, local copies, waits for them, and re-layouts, phases(): speed_first = (32.0 + scaled[0] + scaled[1] * wave) / 4096.0  11.1 us
    another operation x4, other arithmetic, merge_box(): jnp.stack([cosine * child[0] - sine * child[1], cosine * child[1] + sine...  9.92 us
  transfers between devices with their start and end apart: 5, of which 5 were waited for; matrix products, arithmetic and copies ran while one was open for 1% of the time, Pallas kernels for 0%

commit v1 on v0

v1 whole, which is shorter than its diff:
```python
import functools
import math

import jax
import jax.numpy as jnp
import numpy as np
from jax import lax
from jax.experimental import pallas as pl
from jax.experimental.pallas import tpu as pltpu
from jax.sharding import PartitionSpec as P

N = 16384
ORDER = 8
TGT = 32
CAP = 32
NODES = ORDER * ORDER
TARGETS = TGT * TGT
F32 = jnp.float32
BF16 = jnp.bfloat16

SIN_C = (3.1415925798055824, -5.167706866167939, 2.550031193519312, -0.5980441939121666, 0.07721838615746283)
COS_C = (0.9999999532476086, -4.934792830619651, 4.058411352862725, -1.3318765680816773, 0.21968961109948903)


def node_table():
    counting = np.arange(ORDER) * 1.0
    return 0.5 - 0.5 * np.cos(np.pi * (2.0 * counting + 1.0) / (2.0 * ORDER))


def child_matrix(side):
    nodes = node_table()
    points = 0.5 * (side + nodes)
    rows = []
    for target in range(ORDER):
        factor = np.ones(ORDER)
        for source in range(ORDER):
            if source != target:
                factor = factor * (points - nodes[source]) / (nodes[target] - nodes[source])
        rows.append(factor)
    return np.stack(rows)


def merge_tables(along):
    eye = np.eye(ORDER)
    both = []
    for bit in range(2):
        parts = []
        for side in (bit, 1 - bit):
            matrix = child_matrix(side)
            parts.append(np.kron(matrix, eye) if along == 1 else np.kron(eye, matrix))
        full = np.concatenate(parts, axis=1)
        high = full.astype(np.float32).astype(BF16)
        low = (full - high.astype(np.float64)).astype(np.float32).astype(BF16)
        top = np.concatenate([high, high], axis=1)
        bottom = np.concatenate([low, np.zeros_like(low)], axis=1)
        both.append(np.concatenate([top, bottom], axis=0))
    return np.stack(both)


def horner(coefs, x):
    total = coefs[-1]
    for c in coefs[-2::-1]:
        total = total * x + c
    return total


def turn(phase):
    r = phase - jnp.floor(phase + 0.5)
    x = r * r
    sine = horner(SIN_C, x) * r
    cosine = horner(COS_C, x)
    twice = sine + sine
    return 1.0 - twice * sine, twice * cosine


def split(x):
    high = x.astype(BF16)
    return high, (x - high.astype(F32)).astype(BF16)


def iota(shape, axis):
    return lax.broadcasted_iota(jnp.int32, shape, axis)


def nt(a, b):
    return lax.dot_general(a, b, (((1,), (1,)), ((), ())), preferred_element_type=F32)


def pack_body(box_ref, off_ref, val_ref, out_ref):
    blocks = box_ref.shape[0]
    row = iota((128, 128), 0)
    row2 = iota((128, 256), 0)
    col2 = iota((128, 256), 1)
    prefix = jnp.where((row2 < col2) | (col2 >= 128), 1.0, 0.0).astype(BF16)
    same = [row == box_ref[b : b + 1, :] for b in range(blocks)]
    ones = [jnp.where(m, 1.0, 0.0).astype(BF16) for m in same]
    counts = jnp.dot(jnp.concatenate(ones, axis=0), prefix, preferred_element_type=F32)
    slots = iota((CAP, 128), 0).astype(F32)
    carry = jnp.zeros((128, 128), F32)
    wide = []
    for b in range(blocks):
        part = counts[b * 128 : (b + 1) * 128]
        rank = jnp.sum(jnp.where(same[b], part[:, :128] + carry, 0.0), axis=0, keepdims=True)
        carry = carry + part[:, 128:]
        hit = slots == rank
        cols = slice(b * 128, (b + 1) * 128)
        values = [off_ref[0:1, cols].astype(F32), off_ref[1:2, cols].astype(F32), val_ref[0:1, cols], val_ref[1:2, cols]]
        pieces = [[], [], []]
        for v in values:
            rest = v
            for piece in pieces:
                top = rest.astype(BF16).astype(F32)
                rest = rest - top
                piece.append(jnp.where(hit, top, 0.0).astype(BF16))
        wide.append(jnp.concatenate([x for piece in pieces for x in piece], axis=0))
    total = nt(jnp.concatenate(ones, axis=1), jnp.concatenate(wide, axis=1))
    out_ref[...] = total[:, :128] + total[:, 128:256] + total[:, 256:]


def pack(box, offsets, values):
    return pl.pallas_call(
        pack_body,
        out_shape=jax.ShapeDtypeStruct((128, 4 * CAP), F32),
        in_specs=[pl.BlockSpec(memory_space=pltpu.VMEM)] * 3,
        out_specs=pl.BlockSpec(memory_space=pltpu.VMEM),
        name="pack",
    )(box, offsets, values)


def basis_rows(tau):
    nodes = node_table()
    which = iota((ORDER, 128), 0)
    total = None
    for step in range(1, ORDER):
        other = jnp.zeros((ORDER, 128), F32)
        scale = jnp.zeros((ORDER, 128), F32)
        for t in range(ORDER):
            s = (t + step) % ORDER
            other = jnp.where(which == t, float(nodes[s]), other)
            scale = jnp.where(which == t, float(1.0 / (nodes[t] - nodes[s])), scale)
        factor = (tau - other) * scale
        total = factor if total is None else total * factor
    return total


def leaf_body(info_ref, rx_ref, out_ref, xt_ref, q_ref, r_ref, l_ref, acc_ref):
    width_first, width_second = float(N // 8), float(N // 16)
    corner_first = info_ref[4].astype(F32) * width_first
    corner_second = info_ref[5].astype(F32) * width_second
    xt_ref[...] = rx_ref[...].T
    acc_ref[...] = jnp.zeros_like(acc_ref)

    order = iota((TGT, 128), 0)
    klass = (order % 16) * 2 + order // 16
    _, wave = turn((klass.astype(F32) + 1.5) * (1.0 / 32.0))
    speed_first = (32.0 + info_ref[0].astype(F32) + info_ref[1].astype(F32) * wave) * (1.0 / 4096.0)
    speed_second = (32.0 + info_ref[2].astype(F32) + info_ref[3].astype(F32) * wave) * (1.0 / 4096.0)
    lin_second = (iota((TGT, 128), 0) * 4 + 34).astype(F32)
    power = iota((16, 128), 0).astype(F32)

    def slot(s, lane):
        off_first = xt_ref[pl.ds(s, 1), :]
        off_second = xt_ref[pl.ds(CAP + s, 1), :]
        real_in = xt_ref[pl.ds(2 * CAP + s, 1), :]
        imag_in = xt_ref[pl.ds(3 * CAP + s, 1), :]
        first = off_first + corner_first
        second = off_second + corner_second
        a = speed_first * first
        b = speed_second * second
        root = jnp.sqrt(1.0 + a * a + b * b)
        root = root - jnp.floor(root)
        along = lin_second * second
        for eps in range(2):
            part = root[eps * 16 : eps * 16 + 16]
            lin = (along + first * (2.0 * eps + 1.0)) * (1.0 / 4096.0)
            lin = lin - jnp.floor(lin)
            cosine, sine = turn(lin + jnp.concatenate([part, part], axis=0))
            q_ref[2 * eps] = cosine
            q_ref[2 * eps + 1] = sine
        cosine, sine = turn(power * ((first - second) * (1.0 / 1024.0)))
        z_real = cosine * real_in - sine * imag_in
        z_imag = cosine * imag_in + sine * real_in
        cols = slice(lane * 128, lane * 128 + 128)
        low_cols = slice(256 + lane * 128, 256 + lane * 128 + 128)
        for up in range(16):
            zr = z_real[up : up + 1]
            zi = z_imag[up : up + 1]
            for eps in range(2):
                qr = q_ref[2 * eps, up : up + 16, :]
                qi = q_ref[2 * eps + 1, up : up + 16, :]
                for part, value in enumerate((qr * zr - qi * zi, qr * zi + qi * zr)):
                    high, low = split(value)
                    base = part * 512 + (2 * up + eps) * 16
                    r_ref[base : base + 16, cols] = high
                    r_ref[base : base + 16, low_cols] = low
        first_rows = basis_rows(off_first * (1.0 / width_first))
        second_rows = basis_rows(off_second * (1.0 / width_second))
        for part, value in enumerate(turn(second * (1.0 / 128.0))):
            scaled = second_rows * value
            for t in range(0, ORDER, 2):
                pair = jnp.concatenate([first_rows[t : t + 1] * scaled, first_rows[t + 1 : t + 2] * scaled], axis=0)
                high, low = split(pair)
                base = part * NODES + t * ORDER
                l_ref[base : base + 16, cols] = high
                l_ref[128 + base : 128 + base + 16, cols] = low

    def step(i, carry):
        slot(2 * i, 0)
        slot(2 * i + 1, 1)
        right = l_ref[...]
        for m in range(4):
            rows = slice(m * 256, m * 256 + 256)
            acc_ref[rows, :] += nt(r_ref[rows, :256], right) + nt(r_ref[rows, 256:], right)
        return carry

    lax.fori_loop(0, CAP // 2, step, 0)

    for m in range(4):
        blocks = []
        for part in range(2):
            rows = slice(part * 512 + m * 128, part * 512 + m * 128 + 128)
            blocks.append((acc_ref[rows, :128] + acc_ref[rows, 128:]).T)
        (cr, sr), (ci, si) = [(x[:NODES], x[NODES:]) for x in blocks]
        low_cols = slice(m * 128, m * 128 + 128)
        high_cols = slice(512 + m * 128, 512 + m * 128 + 128)
        out_ref[:NODES, low_cols] = cr + si
        out_ref[NODES:, low_cols] = ci - sr
        out_ref[:NODES, high_cols] = cr - si
        out_ref[NODES:, high_cols] = ci + sr


def leaf(info, arrived):
    return pl.pallas_call(
        leaf_body,
        out_shape=jax.ShapeDtypeStruct((2 * NODES, TARGETS), F32),
        in_specs=[pl.BlockSpec(memory_space=pltpu.SMEM), pl.BlockSpec(memory_space=pltpu.VMEM)],
        out_specs=pl.BlockSpec(memory_space=pltpu.VMEM),
        scratch_shapes=[
            pltpu.VMEM((128, 128), F32),
            pltpu.VMEM((4, TGT, 128), F32),
            pltpu.VMEM((1024, 512), BF16),
            pltpu.VMEM((256, 256), BF16),
            pltpu.VMEM((1024, 256), F32),
        ],
        name="leaf",
    )(info, arrived)


def place(index, merged):
    code = jnp.int32(0)
    for bit in range(merged):
        code = code + ((index >> bit) & 1) * 2 ** (merged - 1 - bit)
    return (code.astype(F32) + 0.5) * (1.0 / 2.0**merged)


def node_columns(shape):
    nodes = node_table()
    row = iota(shape, 0)
    first = jnp.zeros(shape, F32)
    second = jnp.zeros(shape, F32)
    for t in range(ORDER):
        first = jnp.where(row // ORDER == t, float(nodes[t]), first)
        second = jnp.where(row % ORDER == t, float(nodes[t]), second)
    return first, second


def speeds(info_ref, klass, place_first, place_second):
    _, wave = turn((klass + (place_first + 2.0 * place_second)) * (1.0 / 32.0))
    one = (32.0 + info_ref[0].astype(F32) + info_ref[1].astype(F32) * wave) * (1.0 / 4096.0)
    two = (32.0 + info_ref[2].astype(F32) + info_ref[3].astype(F32) * wave) * (1.0 / 4096.0)
    return one, two


def root_of(speed, first, second):
    a = speed[0] * first
    b = speed[1] * second
    return jnp.sqrt(1.0 + a * a + b * b)


LEVELS = ((1, 0), (2, 0), (1, 1), (2, 1))


def tables_body(info_ref, gamma_ref, last_ref):
    index_x = info_ref[4]
    index_y = info_ref[5]
    z_first, z_second = node_columns((NODES, 128))
    for tile in range(4):
        lane = iota((1, 128), 1)
        u = tile * 8 + lane // 16
        v = lane % 16
        klass = ((u + 2 * v) % TGT).astype(F32)
        cols = slice(tile * 128, tile * 128 + 128)
        merged = [0, 0]
        for number, (along, level) in enumerate(LEVELS):
            before = list(merged)
            merged[along - 1] += 1
            old = [place(index_x, before[0]), place(index_y, before[1])]
            new = [place(index_x, merged[0]), place(index_y, merged[1])]
            speed_old = speeds(info_ref, klass, *old)
            speed_new = speeds(info_ref, klass, *new)
            index_d = index_x if along == 1 else index_y
            bit = (index_d >> level) & 1
            for who in range(2):
                side = bit if who == 0 else 1 - bit
                child_first = index_x >> before[0]
                child_second = index_y >> before[1]
                if along == 1:
                    child_first = (index_x >> merged[0]) * 2 + side
                else:
                    child_second = (index_y >> merged[1]) * 2 + side
                width_first = float(N // 8 * 2 ** before[0])
                width_second = float(N // 16 * 2 ** before[1])
                first = child_first.astype(F32) * width_first + width_first * z_first
                second = child_second.astype(F32) * width_second + width_second * z_second
                if along == 1:
                    moved = first * ((new[0] - old[0]) * (1.0 / 2048.0))
                else:
                    moved = second * ((new[1] - old[1]) * (1.0 / 1024.0))
                phase = root_of(speed_new, first, second) - root_of(speed_old, first, second) + moved
                cosine, sine = turn(phase)
                gamma_ref[number, who, :NODES, cols] = cosine
                gamma_ref[number, who, NODES:, cols] = sine
        width_first = float(N // 8 * 4)
        width_second = float(N // 16 * 4)
        first = (index_x >> 2).astype(F32) * width_first + width_first * z_first
        second = (index_y >> 2).astype(F32) * width_second + width_second * z_second
        new = [place(index_x, 2), place(index_y, 2)]
        root = root_of(speeds(info_ref, klass, *new), first, second)
        root = root - jnp.floor(root)
        at_first = first * ((u.astype(F32) + new[0]) * (1.0 / 2048.0))
        at_first = at_first - jnp.floor(at_first) + root
        for half in range(2):
            at_second = second * ((v.astype(F32) + (16.0 * half + new[1])) * (1.0 / 1024.0))
            cosine, sine = turn(at_first + at_second)
            wide = slice(half * 512 + tile * 128, half * 512 + tile * 128 + 128)
            last_ref[:NODES, wide] = cosine
            last_ref[NODES:, wide] = sine


def tables(info):
    return pl.pallas_call(
        tables_body,
        out_shape=(
            jax.ShapeDtypeStruct((4, 2, 2 * NODES, 512), F32),
            jax.ShapeDtypeStruct((2 * NODES, TARGETS), F32),
        ),
        in_specs=[pl.BlockSpec(memory_space=pltpu.SMEM)],
        out_specs=[pl.BlockSpec(memory_space=pltpu.VMEM)] * 2,
        name="tables",
    )(info)


def merge_body(number, info_ref, own_ref, other_ref, gamma_ref, mix_ref, *rest):
    along, level = LEVELS[number]
    final = number == 3
    out_ref = rest[-1]
    index_d = info_ref[4] if along == 1 else info_ref[5]
    bit = (index_d >> level) & 1
    left = mix_ref[bit]

    def combined(cols, gcols):
        reals, imags = [], []
        for who, ref in ((0, own_ref), (1, other_ref)):
            gr = gamma_ref[number, who, :NODES, gcols]
            gi = gamma_ref[number, who, NODES:, gcols]
            xr = ref[:NODES, cols]
            xi = ref[NODES:, cols]
            reals.append(split(gr * xr - gi * xi))
            imags.append(split(gr * xi + gi * xr))
        out = []
        for parts in (reals, imags):
            right = jnp.concatenate([parts[0][0], parts[1][0], parts[0][1], parts[1][1]], axis=0)
            both = jnp.dot(left, right, preferred_element_type=F32)
            out.append(both[:NODES] + both[NODES:])
        return out

    if not final:
        for tile in range(4):
            cols = slice(tile * 256, tile * 256 + 256)
            gcols = slice((tile % 2) * 256, (tile % 2) * 256 + 256)
            real, imag = combined(cols, gcols)
            out_ref[:NODES, cols] = real
            out_ref[NODES:, cols] = imag
        return
    last_ref = rest[0]
    source = iota((256, 256), 0)
    target = iota((256, 256), 1)
    wanted = ((target // 16) % 2) * 128 + (target // 32) * 16 + target % 16
    order = jnp.where(source == wanted, 1.0, 0.0).astype(BF16)
    for tile in range(4):
        halves = []
        for half in range(2):
            cols = slice(half * 512 + tile * 128, half * 512 + tile * 128 + 128)
            real, imag = combined(cols, slice(tile * 128, tile * 128 + 128))
            cosine = last_ref[:NODES, cols]
            sine = last_ref[NODES:, cols]
            halves.append(jnp.concatenate([cosine * real + sine * imag, cosine * imag - sine * real], axis=0))
        value = jnp.concatenate(halves, axis=1)
        high = value.astype(BF16)
        value = value - high.astype(F32)
        mid, low = split(value)
        moved = jnp.dot(jnp.concatenate([high, mid, low], axis=0), order, preferred_element_type=F32)
        moved = moved[:128] + moved[128:256] + moved[256:]
        out_ref[0, :, tile * 256 : tile * 256 + 256] = moved[:NODES]
        out_ref[1, :, tile * 256 : tile * 256 + 256] = moved[NODES:]


def merge(number, info, own, other, gamma, last):
    final = number == 3
    args = [info, own, other, gamma, jnp.asarray(merge_tables(LEVELS[number][0]))]
    if final:
        args.append(last)
    shape = (2, NODES, TARGETS) if final else (2 * NODES, TARGETS)
    return pl.pallas_call(
        functools.partial(merge_body, number),
        out_shape=jax.ShapeDtypeStruct(shape, F32),
        in_specs=[pl.BlockSpec(memory_space=pltpu.SMEM)] + [pl.BlockSpec(memory_space=pltpu.VMEM)] * (len(args) - 1),
        out_specs=pl.BlockSpec(memory_space=pltpu.VMEM),
        name="merge_%d" % number,
    )(*args)


def swap(value, along, level):
    axis = "bx" if along == 1 else "by"
    return lax.ppermute(value, axis, [(i, i ^ 1 << level) for i in range(lax.axis_size(axis))])


def on_device(point_box, point_offset, point_value, coef):
    owners = lax.axis_size("bx") * lax.axis_size("by")
    place_on = jnp.stack([lax.axis_index("bx"), lax.axis_index("by")]).astype(jnp.int32)
    info = jnp.concatenate([coef, place_on])
    sent = pack(point_box.reshape(-1, 128), point_offset, point_value)
    arrived = lax.all_to_all(sent.reshape(owners, 1, -1), ("bx", "by"), split_axis=0, concat_axis=0, tiled=True)
    gamma, last = tables(info)
    holding = leaf(info, arrived.reshape(owners, -1))
    for number, (along, level) in enumerate(LEVELS):
        holding = merge(number, info, holding, swap(holding, along, level), gamma, last)
    return holding


def solution(mesh):
    in_specs = (P(("bx", "by"), None), P(None, ("bx", "by")), P(None, ("bx", "by")), P())
    out_specs = P(None, None, ("bx", "by"))
    return jax.shard_map(on_device, mesh=mesh, in_specs=in_specs, out_specs=out_specs, check_vma=False)
```

time: 320 us -> 102 us (0.32); the launches traced: 315 us -> 102 us
  matrix products: 174 us -> 0 us
  other arithmetic: 47.2 us -> 1.26 us
  Pallas kernels: 0 us -> 34.6 us
  local copies, waits for them, and re-layouts: 32.8 us -> 3.84 us
  waiting for transfers between devices: 44.1 us -> 48.8 us
    dot_general x40 -> x0, matrix products: 174 us -> none  [the longest x16 84.6 us: leaf_terms(): lax.dot_general(basis, real_part, dims, precision=lax.Precision.HIGHEST,...]
    pallas_call x0 -> x7, Pallas kernels: none -> 34.6 us  [the longest x1 14.1 us: leaf(): pl.pallas_call(leaf_body, out_shape=jax.ShapeDtypeStruct((2 * NODES, TARG...]
    div x17 -> x0, other arithmetic: 24.7 us -> none  [phases(): speed_first = (32.0 + scaled[0] + scaled[1] * wave) / 4096.0]
    another operation x13 -> x0, other arithmetic: 12.6 us -> none  [the longest x4 9.92 us: merge_box(): jnp.stack([cosine * child[0] - sine * child[1], cosine * child[1] + sine...]
    slice x19 -> x0, local copies, waits for them, and re-layouts: 11.2 us -> none  [the longest x17 11.1 us: phases(): speed_first = (32.0 + scaled[0] + scaled[1] * wave) / 4096.0]
    scatter x1 -> x0, local copies, waits for them, and re-layouts: 6.36 us -> none  [pack_slots(): filled = blank.at[:, slot_of].set(stacked)]
    add x22 -> x0, other arithmetic: 6.27 us -> none  [the longest x4 5.12 us: shift_back(): cosine * real_sum + sine * imag_sum]
    mul x53 -> x0, local copies, waits for them, and re-layouts: 4 us -> none  [the longest x27 2.02 us: phases(): tgt_second * ksecond]
  transfers between devices with their start and end apart: 5 -> 5, of which waited for: 5 -> 4; matrix products, arithmetic and copies ran while one was open for 1% -> 1% of each run, Pallas kernels for 0% -> 4%
where the time goes in v1:
time: 102 us
  waiting for transfers between devices  48.8 us (48%)
  Pallas kernels  34.6 us (34%)
  starting transfers between devices  13.2 us (13%)
  local copies, waits for them, and re-layouts  3.84 us (4%)
  other arithmetic  1.26 us (1%)
    ppermute x4, waiting for transfers between devices, swap(): lax.ppermute(value, axis, [(i, i ^ 1 << level) for i in range(lax.axis_si...  40.6 us
    pallas_call x1, Pallas kernels, leaf(): pl.pallas_call(leaf_body, out_shape=jax.ShapeDtypeStruct((2 * NODES, TARG...  14.1 us
    pallas_call x4, Pallas kernels, merge(): pl.pallas_call(functools.partial(merge_body, number), out_shape=jax.Shape...  13.6 us
    all_to_all x1, starting transfers between devices, on_device(): lax.all_to_all(sent.reshape(owners, 1, -1), ('bx', 'by'), split_axis=0, c...  11.1 us
    all_to_all x1, waiting for transfers between devices, on_device(): lax.all_to_all(sent.reshape(owners, 1, -1), ('bx', 'by'), split_axis=0, c...  8.14 us
    pallas_call x1, Pallas kernels, tables(): pl.pallas_call(tables_body, out_shape=(jax.ShapeDtypeStruct((4, 2, 2 * NO...  4.46 us
    unnamed x10, local copies, waits for them, and re-layouts  3.84 us
    pallas_call x1, Pallas kernels, pack(): pl.pallas_call(pack_body, out_shape=jax.ShapeDtypeStruct((128, 4 * CAP),...  2.44 us
  transfers between devices with their start and end apart: 5, of which 4 were waited for; matrix products, arithmetic and copies ran while one was open for 1% of the time, Pallas kernels for 4%

profile of v1, /device:TPU:0, one launch (start us, length us, event | category | flops | bytes accessed | tf_op | source)
XLA Modules:
  0.0 101.7 jit_solution(6093107008065063352)
XLA Ops:
  0.0 2.4 %pack.1 = f32[128,128]{1,0:T(8,128)} custom-call(s32[16,128]{1,0:T(8,128)} %bitcast.9, s32[2,2048]{1,0:T(2,128)} %off_ref.1, f32[2,2048]{1,0:T(2,128)} %val_ref.1), custom_call_target="tpu_custom_call" | custom-call | tf_op jit(solution)/shard_map/pack/pallas_call | solution.py:121
  2.4 11.1 %all-to-all-start = ((f32[128,1,128]{2,1,0:T(1,128)}), f32[128,1,128]{2,1,0:T(1,128)S(1)}, u32[]{:S(2)}, u32[]{:S(2)}) async-start(f32[128,1,128]{2,1,0:T(1,128)} %bitcast.7), calls=%async_computation | async-start | bytes 131072 | tf_op jit(solution)/shard_map/all_to_all | solution.py:433
  13.6 1.3 %pad_add_fusion.info_ref = s32[6]{0:T(128)} fusion(s32[1]{0:T(128)} %bitcast.1, s32[1]{0:T(128)} %bitcast, s32[4]{0:T(128)} %param.11), kind=kLoop, calls=%fused_computation | loop fusion | flops 12 | bytes 48 | tf_op jit(solution)/shard_map/concatenate | solution.py:431
  14.9 8.1 %all-to-all-done = f32[128,1,128]{2,1,0:T(1,128)S(1)} async-done(((f32[128,1,128]{2,1,0:T(1,128)}), f32[128,1,128]{2,1,0:T(1,128)S(1)}, u32[]{:S(2)}, u32[]{:S(2)}) %all-to-all-start) | async-done | bytes 65568 | tf_op jit(solution)/shard_map/all_to_all | solution.py:433
  23.0 0.0 copy-start.4
  23.0 0.6 copy-done.4
  23.6 14.1 %leaf.1.own_ref = f32[128,1024]{1,0:T(8,128)} custom-call(s32[6]{0:T(128)} %pad_add_fusion.info_ref, f32[128,128]{1,0:T(8,128)} %bitcast.8), custom_call_target="tpu_custom_call" | custom-call | tf_op jit(solution)/shard_map/leaf/pallas_call | solution.py:233
  37.7 0.0 collective-permute-start
  37.7 4.5 %tables.1 = (f32[4,2,128,512]{3,2,1,0:T(8,128)}, f32[128,1024]{1,0:T(8,128)}) custom-call(s32[6]{0:T(128)} %pad_add_fusion.info_ref), custom_call_target="tpu_custom_call" | custom-call | tf_op jit(solution)/shard_map/tables/pallas_call | solution.py:341
  42.2 0.0 collective-permute-done.other_ref
  42.2 0.0 copy-start.1
  42.2 0.8 copy-done.1
  43.0 3.2 %merge_0.1.own_ref = f32[128,1024]{1,0:T(8,128)} custom-call(s32[6]{0:T(128)} %pad_add_fusion.info_ref, f32[128,1024]{1,0:T(8,128)} %leaf.1.own_ref, f32[128,1024]{1,0:T(8,128)} %copy-done.1, f32[4,2,128,512]{3,2,1,0:T(8,128)} %get-tuple-element.7.gamma_ref, bf16[2,128,256]{2,1,0:T(8,128)(2,1)} %constant.13.clone.mix_ref), custom_call_target="tpu_custom_call" | custom-call | tf_op jit(solution)/shard_map/merge_0/pallas_call | solution.py:414
  46.2 0.6 collective-permute-start.1
  46.8 14.0 %collective-permute-done.1.other_ref = f32[128,1024]{1,0:T(8,128)S(1)} collective-permute-done((f32[128,1024]{1,0:T(8,128)}, f32[128,1024]{1,0:T(8,128)S(1)}, u32[]{:S(2)}, u32[]{:S(2)}) %collective-permute-start.1) | collective-permute-done | bytes 524320 | tf_op jit(solution)/shard_map/ppermute | solution.py:425
  60.7 0.0 copy-start.3
  60.7 0.8 copy-done.3
  61.5 3.2 %merge_1.1.own_ref = f32[128,1024]{1,0:T(8,128)} custom-call(s32[6]{0:T(128)} %pad_add_fusion.info_ref, f32[128,1024]{1,0:T(8,128)} %merge_0.1.own_ref, f32[128,1024]{1,0:T(8,128)} %copy-done.3, f32[4,2,128,512]{3,2,1,0:T(8,128)} %get-tuple-element.7.gamma_ref, bf16[2,128,256]{2,1,0:T(8,128)(2,1)} %constant.14.clone.mix_ref), custom_call_target="tpu_custom_call" | custom-call | tf_op jit(solution)/shard_map/merge_1/pallas_call | solution.py:414
  64.7 0.6 collective-permute-start.2
  65.3 13.1 %collective-permute-done.2.other_ref = f32[128,1024]{1,0:T(8,128)S(1)} collective-permute-done((f32[128,1024]{1,0:T(8,128)}, f32[128,1024]{1,0:T(8,128)S(1)}, u32[]{:S(2)}, u32[]{:S(2)}) %collective-permute-start.2) | collective-permute-done | bytes 524320 | tf_op jit(solution)/shard_map/ppermute | solution.py:425
  78.5 0.0 copy-start.2
  78.5 0.8 copy-done.2
  79.3 3.2 %merge_2.1.own_ref = f32[128,1024]{1,0:T(8,128)} custom-call(s32[6]{0:T(128)} %pad_add_fusion.info_ref, f32[128,1024]{1,0:T(8,128)} %merge_1.1.own_ref, f32[128,1024]{1,0:T(8,128)} %copy-done.2, f32[4,2,128,512]{3,2,1,0:T(8,128)} %get-tuple-element.7.gamma_ref, bf16[2,128,256]{2,1,0:T(8,128)(2,1)} %constant.13.clone.mix_ref), custom_call_target="tpu_custom_call" | custom-call | tf_op jit(solution)/shard_map/merge_2/pallas_call | solution.py:414
  82.4 0.9 collective-permute-start.3
  83.3 13.5 %collective-permute-done.3.other_ref = f32[128,1024]{1,0:T(8,128)S(1)} collective-permute-done((f32[128,1024]{1,0:T(8,128)}, f32[128,1024]{1,0:T(8,128)S(1)}, u32[]{:S(2)}, u32[]{:S(2)}) %collective-permute-start.3) | collective-permute-done | bytes 524320 | tf_op jit(solution)/shard_map/ppermute | solution.py:425
  96.8 0.0 copy-start
  96.8 0.8 copy-done
  97.6 4.1 %merge_3.1 = f32[2,64,1024]{2,1,0:T(8,128)} custom-call(s32[6]{0:T(128)} %pad_add_fusion.info_ref, f32[128,1024]{1,0:T(8,128)} %merge_2.1.own_ref, f32[128,1024]{1,0:T(8,128)} %copy-done, f32[4,2,128,512]{3,2,1,0:T(8,128)} %get-tuple-element.7.gamma_ref, bf16[2,128,256]{2,1,0:T(8,128)(2,1)} %constant.14.clone.mix_ref, f32[128,1024]{1,0:T(8,128)} %get-tuple-element.8.rest_0_), custom_call_target="tpu_custom_call" | custom-call | tf_op jit(solution)/shard_map/merge_3/pallas_call | solution.py:414
Async XLA Ops:
  2.4 20.6 %all-to-all-start = ((f32[128,1,128]{2,1,0:T(1,128)}), f32[128,1,128]{2,1,0:T(1,128)S(1)}, u32[]{:S(2)}, u32[]{:S(2)}) async-start(f32[128,1,128]{2,1,0:T(1,128)} %bitcast.7), calls=%async_computation | async-start | bytes 131072 | tf_op jit(solution)/shard_map/all_to_all | solution.py:433
  23.0 0.6 copy-start.4
  37.7 4.5 %collective-permute-start = (f32[128,1024]{1,0:T(8,128)}, f32[128,1024]{1,0:T(8,128)S(1)}, u32[]{:S(2)}, u32[]{:S(2)}) collective-permute-start(f32[128,1024]{1,0:T(8,128)} %leaf.1.own_ref), channel_id=1, source_target_pairs={{0,16},{16,0},{32,48},{48,32},{64,80},{80,64},{96,112},{112,96},{1... | collective-permute-start | bytes 1572872 | tf_op jit(solution)/shard_map/ppermute | solution.py:425
  42.2 0.8 copy-start.1
  46.2 14.5 %collective-permute-start.1 = (f32[128,1024]{1,0:T(8,128)}, f32[128,1024]{1,0:T(8,128)S(1)}, u32[]{:S(2)}, u32[]{:S(2)}) collective-permute-start(f32[128,1024]{1,0:T(8,128)} %merge_0.1.own_ref), channel_id=1, source_target_pairs={{0,1},{1,0},{2,3},{3,2},{4,5},{5,4},{6,7},{7,6},{8,9},{9,8},{10,11... | collective-permute-start | bytes 1572872 | tf_op jit(solution)/shard_map/ppermute | solution.py:425
  60.7 0.8 copy-start.3
  64.7 13.8 %collective-permute-start.2 = (f32[128,1024]{1,0:T(8,128)}, f32[128,1024]{1,0:T(8,128)S(1)}, u32[]{:S(2)}, u32[]{:S(2)}) collective-permute-start(f32[128,1024]{1,0:T(8,128)} %merge_1.1.own_ref), channel_id=1, source_target_pairs={{0,32},{16,48},{32,0},{48,16},{64,96},{80,112},{96,64},{112,80},{1... | collective-permute-start | bytes 1572872 | tf_op jit(solution)/shard_map/ppermute | solution.py:425
  78.5 0.8 copy-start.2
  82.4 14.4 %collective-permute-start.3 = (f32[128,1024]{1,0:T(8,128)}, f32[128,1024]{1,0:T(8,128)S(1)}, u32[]{:S(2)}, u32[]{:S(2)}) collective-permute-start(f32[128,1024]{1,0:T(8,128)} %merge_2.1.own_ref), channel_id=1, source_target_pairs={{0,2},{1,3},{2,0},{3,1},{4,6},{5,7},{6,4},{7,5},{8,10},{9,11},{10,... | collective-permute-start | bytes 1572872 | tf_op jit(solution)/shard_map/ppermute | solution.py:425
  96.8 0.8 copy-start

commit v2 on v1

--- a/solution.py
+++ b/solution.py
@@ -123,7 +123,7 @@
         out_shape=jax.ShapeDtypeStruct((128, 4 * CAP), F32),
         in_specs=[pl.BlockSpec(memory_space=pltpu.VMEM)] * 3,
         out_specs=pl.BlockSpec(memory_space=pltpu.VMEM),
-        name="pack",
+        name="pack", compiler_params=pltpu.CompilerParams(vmem_limit_bytes=8 << 20),
     )(box, offsets, values)
 
 
@@ -242,7 +242,7 @@
             pltpu.VMEM((256, 256), BF16),
             pltpu.VMEM((1024, 256), F32),
         ],
-        name="leaf",
+        name="leaf", compiler_params=pltpu.CompilerParams(vmem_limit_bytes=16 << 20),
     )(info, arrived)
 
 
@@ -346,7 +346,7 @@
         ),
         in_specs=[pl.BlockSpec(memory_space=pltpu.SMEM)],
         out_specs=[pl.BlockSpec(memory_space=pltpu.VMEM)] * 2,
-        name="tables",
+        name="tables", compiler_params=pltpu.CompilerParams(vmem_limit_bytes=16 << 20),
     )(info)
 
 
@@ -416,7 +416,7 @@
         out_shape=jax.ShapeDtypeStruct(shape, F32),
         in_specs=[pl.BlockSpec(memory_space=pltpu.SMEM)] + [pl.BlockSpec(memory_space=pltpu.VMEM)] * (len(args) - 1),
         out_specs=pl.BlockSpec(memory_space=pltpu.VMEM),
-        name="merge_%d" % number,
+        name="merge_%d" % number, compiler_params=pltpu.CompilerParams(vmem_limit_bytes=16 << 20),
     )(*args)
 
 

time: 102 us -> 89.4 us (0.88)
  Pallas kernels: 34.6 us -> 23.1 us
    pallas_call x4, Pallas kernels: 13.6 us -> 5.46 us  [merge(): pl.pallas_call(functools.partial(merge_body, number), out_shape=jax.Shape...]
    pallas_call x1, Pallas kernels: 4.46 us -> 2.89 us  [tables(): pl.pallas_call(tables_body, out_shape=(jax.ShapeDtypeStruct((4, 2, 2 * NO...]
    pallas_call x1, Pallas kernels: 14.1 us -> 13 us  [leaf(): pl.pallas_call(leaf_body, out_shape=jax.ShapeDtypeStruct((2 * NODES, TARG...]
  transfers between devices with their start and end apart: 5 -> 5, of which waited for: 4 -> 4; matrix products, arithmetic and copies ran while one was open for 1% -> 1% of each run, Pallas kernels for 4% -> 3%
where the time goes in v2:
time: 89.4 us; the launch traced here: 89.1 us
  waiting for transfers between devices  48.6 us (54%)
  Pallas kernels  23.1 us (26%)
  starting transfers between devices  13.5 us (15%)
  local copies, waits for them, and re-layouts  3.03 us (3%)
    ppermute x4, waiting for transfers between devices, swap(): lax.ppermute(value, axis, [(i, i ^ 1 << level) for i in range(lax.axis_si...  40 us
    pallas_call x1, Pallas kernels, leaf(): pl.pallas_call(leaf_body, out_shape=jax.ShapeDtypeStruct((2 * NODES, TARG...  13 us
    all_to_all x1, starting transfers between devices, on_device(): lax.all_to_all(sent.reshape(owners, 1, -1), ('bx', 'by'), split_axis=0, c...  11.1 us
    all_to_all x1, waiting for transfers between devices, on_device(): lax.all_to_all(sent.reshape(owners, 1, -1), ('bx', 'by'), split_axis=0, c...  8.67 us
    pallas_call x4, Pallas kernels, merge(): pl.pallas_call(functools.partial(merge_body, number), out_shape=jax.Shape...  5.46 us
    unnamed x10, local copies, waits for them, and re-layouts  3.03 us
    pallas_call x1, Pallas kernels, tables(): pl.pallas_call(tables_body, out_shape=(jax.ShapeDtypeStruct((4, 2, 2 * NO...  2.89 us
    ppermute x4, starting transfers between devices, swap(): lax.ppermute(value, axis, [(i, i ^ 1 << level) for i in range(lax.axis_si...  2.38 us
  transfers between devices with their start and end apart: 5, of which 4 were waited for; matrix products, arithmetic and copies ran while one was open for 1% of the time, Pallas kernels for 3%

profile of v2, /device:TPU:0, one launch (start us, length us, event | category | flops | bytes accessed | tf_op | source)
XLA Modules:
  0.0 89.1 jit_solution(5713586724287607726)
XLA Ops:
  0.0 0.0 copy-start.2
  0.0 0.7 copy-done.2
  0.7 0.0 copy-start.3
  0.7 0.7 copy-done.3
  1.4 0.0 copy-start.4
  1.4 0.7 copy-done.4
  2.1 1.7 %pack.1 = f32[128,128]{1,0:T(8,128)} custom-call(s32[16,128]{1,0:T(8,128)S(1)} %bitcast.8, s32[2,2048]{1,0:T(2,128)S(1)} %copy-done.2, f32[2,2048]{1,0:T(2,128)S(1)} %copy-done.3), custom_call_target="tpu_custom_call" | custom-call | tf_op jit(solution)/shard_map/pack/pallas_call | solution.py:121
  3.8 11.1 %all-to-all-start = ((f32[128,1,128]{2,1,0:T(1,128)}), f32[128,1,128]{2,1,0:T(1,128)S(1)}, u32[]{:S(2)}, u32[]{:S(2)}) async-start(f32[128,1,128]{2,1,0:T(1,128)} %bitcast.4), calls=%async_computation | async-start | bytes 131072 | tf_op jit(solution)/shard_map/all_to_all | solution.py:433
  15.0 0.7 pad_add_fusion.info_ref
  15.7 8.7 %all-to-all-done = f32[128,1,128]{2,1,0:T(1,128)S(1)} async-done(((f32[128,1,128]{2,1,0:T(1,128)}), f32[128,1,128]{2,1,0:T(1,128)S(1)}, u32[]{:S(2)}, u32[]{:S(2)}) %all-to-all-start) | async-done | bytes 65568 | tf_op jit(solution)/shard_map/all_to_all | solution.py:433
  24.4 0.0 copy-start
  24.4 13.0 %leaf.1.own_ref = f32[128,1024]{1,0:T(8,128)S(1)} custom-call(s32[6]{0:T(128)S(1)} %pad_add_fusion.info_ref, f32[128,128]{1,0:T(8,128)S(1)} %bitcast.7), custom_call_target="tpu_custom_call" | custom-call | tf_op jit(solution)/shard_map/leaf/pallas_call | solution.py:233
  37.4 0.1 collective-permute-start
  37.5 2.9 %tables.1 = (f32[4,2,128,512]{3,2,1,0:T(8,128)S(1)}, f32[128,1024]{1,0:T(8,128)S(1)}) custom-call(s32[6]{0:T(128)S(1)} %pad_add_fusion.info_ref), custom_call_target="tpu_custom_call" | custom-call | tf_op jit(solution)/shard_map/tables/pallas_call | solution.py:341
  40.4 0.0 collective-permute-done.other_ref
  40.4 0.0 copy-start.1
  40.4 0.9 %copy-done.1 = bf16[2,128,256]{2,1,0:T(8,128)(2,1)S(1)} copy-done((bf16[2,128,256]{2,1,0:T(8,128)(2,1)S(1)}, bf16[2,128,256]{2,1,0:T(8,128)(2,1)}, u32[]{:S(2)}) %copy-start.1) | copy-done | bytes 131096
  41.3 1.0 %merge_0.1.own_ref = f32[128,1024]{1,0:T(8,128)S(1)} custom-call(s32[6]{0:T(128)S(1)} %pad_add_fusion.info_ref, f32[128,1024]{1,0:T(8,128)S(1)} %leaf.1.own_ref, f32[128,1024]{1,0:T(8,128)S(1)} %collective-permute-done.other_ref, f32[4,2,128,512]{3,2,1,0:T(8,128)S(1)} %get-tuple-element.7.gamma_ref, bf16[2,128,256]{2,1,0:T(8,128)(2,1)S(1)} %copy-done.1), custom_call_target="tpu_custom_call" | custom-call | tf_op jit(solution)/shard_map/merge_0/pallas_call | solution.py:414
  42.3 0.7 collective-permute-start.1
  42.9 13.7 %collective-permute-done.1.other_ref = f32[128,1024]{1,0:T(8,128)S(1)} collective-permute-done((f32[128,1024]{1,0:T(8,128)S(1)}, f32[128,1024]{1,0:T(8,128)S(1)}, u32[]{:S(2)}, u32[]{:S(2)}) %collective-permute-start.1) | collective-permute-done | bytes 524320 | tf_op jit(solution)/shard_map/ppermute | solution.py:425
  56.7 0.0 copy-done
  56.7 1.0 %merge_1.1.own_ref = f32[128,1024]{1,0:T(8,128)S(1)} custom-call(s32[6]{0:T(128)S(1)} %pad_add_fusion.info_ref, f32[128,1024]{1,0:T(8,128)S(1)} %merge_0.1.own_ref, f32[128,1024]{1,0:T(8,128)S(1)} %collective-permute-done.1.other_ref, f32[4,2,128,512]{3,2,1,0:T(8,128)S(1)} %get-tuple-element.7.gamma_ref, bf16[2,128,256]{2,1,0:T(8,128)(2,1)S(1)} %copy-done), custom_call_target="tpu_custom_call" | custom-call | tf_op jit(solution)/shard_map/merge_1/pallas_call | solution.py:414
  57.7 0.7 collective-permute-start.2
  58.4 12.9 %collective-permute-done.2.other_ref = f32[128,1024]{1,0:T(8,128)S(1)} collective-permute-done((f32[128,1024]{1,0:T(8,128)S(1)}, f32[128,1024]{1,0:T(8,128)S(1)}, u32[]{:S(2)}, u32[]{:S(2)}) %collective-permute-start.2) | collective-permute-done | bytes 524320 | tf_op jit(solution)/shard_map/ppermute | solution.py:425
  71.3 1.0 %merge_2.1.own_ref = f32[128,1024]{1,0:T(8,128)S(1)} custom-call(s32[6]{0:T(128)S(1)} %pad_add_fusion.info_ref, f32[128,1024]{1,0:T(8,128)S(1)} %merge_1.1.own_ref, f32[128,1024]{1,0:T(8,128)S(1)} %collective-permute-done.2.other_ref, f32[4,2,128,512]{3,2,1,0:T(8,128)S(1)} %get-tuple-element.7.gamma_ref, bf16[2,128,256]{2,1,0:T(8,128)(2,1)S(1)} %copy-done.1), custom_call_target="tpu_custom_call" | custom-call | tf_op jit(solution)/shard_map/merge_2/pallas_call | solution.py:414
  72.3 0.9 %collective-permute-start.3 = (f32[128,1024]{1,0:T(8,128)S(1)}, f32[128,1024]{1,0:T(8,128)S(1)}, u32[]{:S(2)}, u32[]{:S(2)}) collective-permute-start(f32[128,1024]{1,0:T(8,128)S(1)} %merge_2.1.own_ref), channel_id=1, source_target_pairs={{0,2},{1,3},{2,0},{3,1},{4,6},{5,7},{6,4},{7,5},{8,10},{9,11},{10,... | collective-permute-start | bytes 1572872 | tf_op jit(solution)/shard_map/ppermute | solution.py:425
  73.2 13.3 %collective-permute-done.3.other_ref = f32[128,1024]{1,0:T(8,128)S(1)} collective-permute-done((f32[128,1024]{1,0:T(8,128)S(1)}, f32[128,1024]{1,0:T(8,128)S(1)}, u32[]{:S(2)}, u32[]{:S(2)}) %collective-permute-start.3) | collective-permute-done | bytes 524320 | tf_op jit(solution)/shard_map/ppermute | solution.py:425
  86.5 2.6 %merge_3.1 = f32[2,64,1024]{2,1,0:T(8,128)} custom-call(s32[6]{0:T(128)S(1)} %pad_add_fusion.info_ref, f32[128,1024]{1,0:T(8,128)S(1)} %merge_2.1.own_ref, f32[128,1024]{1,0:T(8,128)S(1)} %collective-permute-done.3.other_ref, f32[4,2,128,512]{3,2,1,0:T(8,128)S(1)} %get-tuple-element.7.gamma_ref, bf16[2,128,256]{2,1,0:T(8,128)(2,1)S(1)} %copy-done, ...), custom_call_target="tpu_custom_call" | custom-call | tf_op jit(solution)/shard_map/merge_3/pallas_call | solution.py:414
Async XLA Ops:
  0.0 0.7 copy-start.2
  0.7 0.7 copy-start.3
  1.4 0.7 copy-start.4
  3.8 20.6 %all-to-all-start = ((f32[128,1,128]{2,1,0:T(1,128)}), f32[128,1,128]{2,1,0:T(1,128)S(1)}, u32[]{:S(2)}, u32[]{:S(2)}) async-start(f32[128,1,128]{2,1,0:T(1,128)} %bitcast.4), calls=%async_computation | async-start | bytes 131072 | tf_op jit(solution)/shard_map/all_to_all | solution.py:433
  24.4 32.3 %copy-start = (bf16[2,128,256]{2,1,0:T(8,128)(2,1)S(1)}, bf16[2,128,256]{2,1,0:T(8,128)(2,1)}, u32[]{:S(2)}) copy-start(bf16[2,128,256]{2,1,0:T(8,128)(2,1)} %constant.14.clone.mix_ref) | copy-start | bytes 393220
  37.4 3.0 %collective-permute-start = (f32[128,1024]{1,0:T(8,128)S(1)}, f32[128,1024]{1,0:T(8,128)S(1)}, u32[]{:S(2)}, u32[]{:S(2)}) collective-permute-start(f32[128,1024]{1,0:T(8,128)S(1)} %leaf.1.own_ref), channel_id=1, source_target_pairs={{0,16},{16,0},{32,48},{48,32},{64,80},{80,64},{96,112},{112,96},{1... | collective-permute-start | bytes 1572872 | tf_op jit(solution)/shard_map/ppermute | solution.py:425
  40.4 0.9 %copy-start.1 = (bf16[2,128,256]{2,1,0:T(8,128)(2,1)S(1)}, bf16[2,128,256]{2,1,0:T(8,128)(2,1)}, u32[]{:S(2)}) copy-start(bf16[2,128,256]{2,1,0:T(8,128)(2,1)} %constant.13.clone.mix_ref) | copy-start | bytes 393220
  42.3 14.4 %collective-permute-start.1 = (f32[128,1024]{1,0:T(8,128)S(1)}, f32[128,1024]{1,0:T(8,128)S(1)}, u32[]{:S(2)}, u32[]{:S(2)}) collective-permute-start(f32[128,1024]{1,0:T(8,128)S(1)} %merge_0.1.own_ref), channel_id=1, source_target_pairs={{0,1},{1,0},{2,3},{3,2},{4,5},{5,4},{6,7},{7,6},{8,9},{9,8},{10,11... | collective-permute-start | bytes 1572872 | tf_op jit(solution)/shard_map/ppermute | solution.py:425
  57.7 13.6 %collective-permute-start.2 = (f32[128,1024]{1,0:T(8,128)S(1)}, f32[128,1024]{1,0:T(8,128)S(1)}, u32[]{:S(2)}, u32[]{:S(2)}) collective-permute-start(f32[128,1024]{1,0:T(8,128)S(1)} %merge_1.1.own_ref), channel_id=1, source_target_pairs={{0,32},{16,48},{32,0},{48,16},{64,96},{80,112},{96,64},{112,80},{1... | collective-permute-start | bytes 1572872 | tf_op jit(solution)/shard_map/ppermute | solution.py:425
  72.3 14.2 %collective-permute-start.3 = (f32[128,1024]{1,0:T(8,128)S(1)}, f32[128,1024]{1,0:T(8,128)S(1)}, u32[]{:S(2)}, u32[]{:S(2)}) collective-permute-start(f32[128,1024]{1,0:T(8,128)S(1)} %merge_2.1.own_ref), channel_id=1, source_target_pairs={{0,2},{1,3},{2,0},{3,1},{4,6},{5,7},{6,4},{7,5},{8,10},{9,11},{10,... | collective-permute-start | bytes 1572872 | tf_op jit(solution)/shard_map/ppermute | solution.py:425

commit v3 on v1

--- a/solution.py
+++ b/solution.py
@@ -13,6 +13,10 @@
 ORDER = 8
 TGT = 32
 CAP = 32
+CHUNKS = 4
+GROUPS = 4 // CHUNKS
+LANES = 256 * GROUPS
+STEP = 8
 NODES = ORDER * ORDER
 TARGETS = TGT * TGT
 F32 = jnp.float32
@@ -76,6 +80,17 @@
 def split(x):
     high = x.astype(BF16)
     return high, (x - high.astype(F32)).astype(BF16)
+
+
+def cost(micros):
+    return pl.CostEstimate(flops=0, bytes_accessed=int(micros * 3.7e6), transcendentals=0)
+
+
+def vmem(count):
+    return [pl.BlockSpec(memory_space=pltpu.VMEM)] * count
+
+
+SMALL = pltpu.CompilerParams(vmem_limit_bytes=12 << 20)
 
 
 def iota(shape, axis):
@@ -124,6 +139,7 @@
         in_specs=[pl.BlockSpec(memory_space=pltpu.VMEM)] * 3,
         out_specs=pl.BlockSpec(memory_space=pltpu.VMEM),
         name="pack",
+        cost_estimate=cost(2.0),
     )(box, offsets, values)
 
 
@@ -143,12 +159,11 @@
     return total
 
 
-def leaf_body(info_ref, rx_ref, out_ref, xt_ref, q_ref, r_ref, l_ref, acc_ref):
+def prepare_body(info_ref, rx_ref, l_ref, q_ref, z_ref, xt_ref):
     width_first, width_second = float(N // 8), float(N // 16)
     corner_first = info_ref[4].astype(F32) * width_first
     corner_second = info_ref[5].astype(F32) * width_second
     xt_ref[...] = rx_ref[...].T
-    acc_ref[...] = jnp.zeros_like(acc_ref)
 
     order = iota((TGT, 128), 0)
     klass = (order % 16) * 2 + order // 16
@@ -158,11 +173,11 @@
     lin_second = (iota((TGT, 128), 0) * 4 + 34).astype(F32)
     power = iota((16, 128), 0).astype(F32)
 
-    def slot(s, lane):
-        off_first = xt_ref[pl.ds(s, 1), :]
-        off_second = xt_ref[pl.ds(CAP + s, 1), :]
-        real_in = xt_ref[pl.ds(2 * CAP + s, 1), :]
-        imag_in = xt_ref[pl.ds(3 * CAP + s, 1), :]
+    for s in range(CAP):
+        off_first = xt_ref[s : s + 1, :]
+        off_second = xt_ref[CAP + s : CAP + s + 1, :]
+        real_in = xt_ref[2 * CAP + s : 2 * CAP + s + 1, :]
+        imag_in = xt_ref[3 * CAP + s : 3 * CAP + s + 1, :]
         first = off_first + corner_first
         second = off_second + corner_second
         a = speed_first * first
@@ -175,24 +190,12 @@
             lin = (along + first * (2.0 * eps + 1.0)) * (1.0 / 4096.0)
             lin = lin - jnp.floor(lin)
             cosine, sine = turn(lin + jnp.concatenate([part, part], axis=0))
-            q_ref[2 * eps] = cosine
-            q_ref[2 * eps + 1] = sine
+            q_ref[s, 2 * eps] = cosine
+            q_ref[s, 2 * eps + 1] = sine
         cosine, sine = turn(power * ((first - second) * (1.0 / 1024.0)))
-        z_real = cosine * real_in - sine * imag_in
-        z_imag = cosine * imag_in + sine * real_in
-        cols = slice(lane * 128, lane * 128 + 128)
-        low_cols = slice(256 + lane * 128, 256 + lane * 128 + 128)
-        for up in range(16):
-            zr = z_real[up : up + 1]
-            zi = z_imag[up : up + 1]
-            for eps in range(2):
-                qr = q_ref[2 * eps, up : up + 16, :]
-                qi = q_ref[2 * eps + 1, up : up + 16, :]
-                for part, value in enumerate((qr * zr - qi * zi, qr * zi + qi * zr)):
-                    high, low = split(value)
-                    base = part * 512 + (2 * up + eps) * 16
-                    r_ref[base : base + 16, cols] = high
-                    r_ref[base : base + 16, low_cols] = low
+        z_ref[s, 0] = cosine * real_in - sine * imag_in
+        z_ref[s, 1] = cosine * imag_in + sine * real_in
+        cols = slice(s * 128, s * 128 + 128)
         first_rows = basis_rows(off_first * (1.0 / width_first))
         second_rows = basis_rows(off_second * (1.0 / width_second))
         for part, value in enumerate(turn(second * (1.0 / 128.0))):
@@ -204,46 +207,87 @@
                 l_ref[base : base + 16, cols] = high
                 l_ref[128 + base : 128 + base + 16, cols] = low
 
-    def step(i, carry):
-        slot(2 * i, 0)
-        slot(2 * i + 1, 1)
-        right = l_ref[...]
-        for m in range(4):
-            rows = slice(m * 256, m * 256 + 256)
-            acc_ref[rows, :] += nt(r_ref[rows, :256], right) + nt(r_ref[rows, 256:], right)
-        return carry
-
-    lax.fori_loop(0, CAP // 2, step, 0)
-
-    for m in range(4):
+
+def prepare(info, arrived):
+    return pl.pallas_call(
+        prepare_body,
+        out_shape=(
+            jax.ShapeDtypeStruct((256, CAP * 128), BF16),
+            jax.ShapeDtypeStruct((CAP, 4, TGT, 128), F32),
+            jax.ShapeDtypeStruct((CAP, 2, 16, 128), F32),
+        ),
+        in_specs=[pl.BlockSpec(memory_space=pltpu.SMEM)] + vmem(1),
+        out_specs=vmem(3),
+        scratch_shapes=[pltpu.VMEM((128, 128), F32)],
+        name="prepare",
+        compiler_params=SMALL,
+        cost_estimate=cost(2.0),
+    )(info, arrived)
+
+
+def leaf_body(chunk, l_ref, q_ref, z_ref, out_ref, ra_ref, rb_ref, acc_ref):
+    half = STEP * 128
+
+    def build(step, r_ref):
+        for j in range(STEP):
+            s = step * STEP + j
+            cols = slice(j * 128, j * 128 + 128)
+            low_cols = slice(half + j * 128, half + j * 128 + 128)
+            for local in range(4 * GROUPS):
+                up = chunk * 4 * GROUPS + local
+                zr = z_ref[s, 0, up : up + 1, :]
+                zi = z_ref[s, 1, up : up + 1, :]
+                for eps in range(2):
+                    qr = q_ref[s, 2 * eps, up : up + 16, :]
+                    qi = q_ref[s, 2 * eps + 1, up : up + 16, :]
+                    for part, value in enumerate((qr * zr - qi * zi, qr * zi + qi * zr)):
+                        high, low = split(value)
+                        base = (local // 4) * 256 + part * 128 + (2 * (local % 4) + eps) * 16
+                        r_ref[base : base + 16, cols] = high
+                        r_ref[base : base + 16, low_cols] = low
+
+    steps = CAP // STEP
+    build(0, ra_ref)
+    for step in range(steps):
+        now, later = (ra_ref, rb_ref) if step % 2 == 0 else (rb_ref, ra_ref)
+        if step + 1 < steps:
+            build(step + 1, later)
+        right = l_ref[:, step * half : step * half + half]
+        product = nt(now[...], jnp.concatenate([right, right], axis=1))
+        if step == 0:
+            acc_ref[...] = product
+        else:
+            acc_ref[...] += product
+
+    for g in range(GROUPS):
         blocks = []
         for part in range(2):
-            rows = slice(part * 512 + m * 128, part * 512 + m * 128 + 128)
+            rows = slice(g * 256 + part * 128, g * 256 + part * 128 + 128)
             blocks.append((acc_ref[rows, :128] + acc_ref[rows, 128:]).T)
         (cr, sr), (ci, si) = [(x[:NODES], x[NODES:]) for x in blocks]
-        low_cols = slice(m * 128, m * 128 + 128)
-        high_cols = slice(512 + m * 128, 512 + m * 128 + 128)
+        low_cols = slice(g * 256, g * 256 + 128)
+        high_cols = slice(g * 256 + 128, g * 256 + 256)
         out_ref[:NODES, low_cols] = cr + si
         out_ref[NODES:, low_cols] = ci - sr
         out_ref[:NODES, high_cols] = cr - si
         out_ref[NODES:, high_cols] = ci + sr
 
 
-def leaf(info, arrived):
+def leaf(chunk, prepared):
     return pl.pallas_call(
-        leaf_body,
-        out_shape=jax.ShapeDtypeStruct((2 * NODES, TARGETS), F32),
-        in_specs=[pl.BlockSpec(memory_space=pltpu.SMEM), pl.BlockSpec(memory_space=pltpu.VMEM)],
-        out_specs=pl.BlockSpec(memory_space=pltpu.VMEM),
+        functools.partial(leaf_body, chunk),
+        out_shape=jax.ShapeDtypeStruct((2 * NODES, LANES), F32),
+        in_specs=vmem(3),
+        out_specs=vmem(1)[0],
         scratch_shapes=[
-            pltpu.VMEM((128, 128), F32),
-            pltpu.VMEM((4, TGT, 128), F32),
-            pltpu.VMEM((1024, 512), BF16),
-            pltpu.VMEM((256, 256), BF16),
-            pltpu.VMEM((1024, 256), F32),
+            pltpu.VMEM((LANES, STEP * 256), BF16),
+            pltpu.VMEM((LANES, STEP * 256), BF16),
+            pltpu.VMEM((LANES, 256), F32),
         ],
-        name="leaf",
-    )(info, arrived)
+        name="leaf_%d" % chunk,
+        compiler_params=SMALL,
+        cost_estimate=cost(2.5 * GROUPS),
+    )(*prepared)
 
 
 def place(index, merged):
@@ -280,7 +324,7 @@
 LEVELS = ((1, 0), (2, 0), (1, 1), (2, 1))
 
 
-def tables_body(info_ref, gamma_ref, last_ref):
+def tables_body(numbers, with_last, info_ref, *out_refs):
     index_x = info_ref[4]
     index_y = info_ref[5]
     z_first, z_second = node_columns((NODES, 128))
@@ -294,6 +338,9 @@
         for number, (along, level) in enumerate(LEVELS):
             before = list(merged)
             merged[along - 1] += 1
+            if number not in numbers:
+                continue
+            gamma_ref = out_refs[numbers.index(number)]
             old = [place(index_x, before[0]), place(index_y, before[1])]
             new = [place(index_x, merged[0]), place(index_y, merged[1])]
             speed_old = speeds(info_ref, klass, *old)
@@ -318,8 +365,11 @@
                     moved = second * ((new[1] - old[1]) * (1.0 / 1024.0))
                 phase = root_of(speed_new, first, second) - root_of(speed_old, first, second) + moved
                 cosine, sine = turn(phase)
-                gamma_ref[number, who, :NODES, cols] = cosine
-                gamma_ref[number, who, NODES:, cols] = sine
+                gamma_ref[who, :NODES, cols] = cosine
+                gamma_ref[who, NODES:, cols] = sine
+        if not with_last:
+            continue
+        last_ref = out_refs[-1]
         width_first = float(N // 8 * 4)
         width_second = float(N // 16 * 4)
         first = (index_x >> 2).astype(F32) * width_first + width_first * z_first
@@ -332,91 +382,117 @@
         for half in range(2):
             at_second = second * ((v.astype(F32) + (16.0 * half + new[1])) * (1.0 / 1024.0))
             cosine, sine = turn(at_first + at_second)
-            wide = slice(half * 512 + tile * 128, half * 512 + tile * 128 + 128)
+            wide = slice(tile * 256 + half * 128, tile * 256 + half * 128 + 128)
             last_ref[:NODES, wide] = cosine
             last_ref[NODES:, wide] = sine
 
 
-def tables(info):
+def tables(info, numbers, with_last=False):
+    shapes = [jax.ShapeDtypeStruct((2, 2 * NODES, 512), F32)] * len(numbers)
+    if with_last:
+        shapes.append(jax.ShapeDtypeStruct((2 * NODES, TARGETS), F32))
     return pl.pallas_call(
-        tables_body,
-        out_shape=(
-            jax.ShapeDtypeStruct((4, 2, 2 * NODES, 512), F32),
-            jax.ShapeDtypeStruct((2 * NODES, TARGETS), F32),
-        ),
+        functools.partial(tables_body, numbers, with_last),
+        out_shape=tuple(shapes),
         in_specs=[pl.BlockSpec(memory_space=pltpu.SMEM)],
-        out_specs=[pl.BlockSpec(memory_space=pltpu.VMEM)] * 2,
-        name="tables",
+        out_specs=vmem(len(shapes)),
+        name="tables_" + "".join(str(n) for n in numbers),
+        compiler_params=SMALL,
+        cost_estimate=cost(0.6 * len(numbers) + 0.6 * with_last),
     )(info)
 
 
-def merge_body(number, info_ref, own_ref, other_ref, gamma_ref, mix_ref, *rest):
-    along, level = LEVELS[number]
-    final = number == 3
-    out_ref = rest[-1]
-    index_d = info_ref[4] if along == 1 else info_ref[5]
-    bit = (index_d >> level) & 1
-    left = mix_ref[bit]
-
-    def combined(cols, gcols):
+def combined(number, group, left, own_ref, other_ref, gamma_ref, chunk):
+    tile = chunk * GROUPS + group
+    gcols = slice(tile * 128, tile * 128 + 128)
+    sides = [[], []]
+    for half in range(2):
+        cols = slice(group * 256 + half * 128, group * 256 + half * 128 + 128)
         reals, imags = [], []
         for who, ref in ((0, own_ref), (1, other_ref)):
-            gr = gamma_ref[number, who, :NODES, gcols]
-            gi = gamma_ref[number, who, NODES:, gcols]
+            gr = gamma_ref[who, :NODES, gcols]
+            gi = gamma_ref[who, NODES:, gcols]
             xr = ref[:NODES, cols]
             xi = ref[NODES:, cols]
             reals.append(split(gr * xr - gi * xi))
             imags.append(split(gr * xi + gi * xr))
-        out = []
-        for parts in (reals, imags):
-            right = jnp.concatenate([parts[0][0], parts[1][0], parts[0][1], parts[1][1]], axis=0)
-            both = jnp.dot(left, right, preferred_element_type=F32)
-            out.append(both[:NODES] + both[NODES:])
-        return out
-
-    if not final:
-        for tile in range(4):
-            cols = slice(tile * 256, tile * 256 + 256)
-            gcols = slice((tile % 2) * 256, (tile % 2) * 256 + 256)
-            real, imag = combined(cols, gcols)
-            out_ref[:NODES, cols] = real
-            out_ref[NODES:, cols] = imag
-        return
-    last_ref = rest[0]
+        for side, parts in zip(sides, (reals, imags)):
+            side.append(jnp.concatenate([parts[0][0], parts[1][0], parts[0][1], parts[1][1]], axis=0))
+    out = []
+    for side in sides:
+        both = jnp.dot(left, jnp.concatenate(side, axis=1), preferred_element_type=F32)
+        out.append(both[:NODES] + both[NODES:])
+    return out
+
+
+def merge_body(number, chunk, info_ref, own_ref, other_ref, gamma_ref, mix_ref, out_ref):
+    along, level = LEVELS[number]
+    index_d = info_ref[4] if along == 1 else info_ref[5]
+    left = mix_ref[(index_d >> level) & 1]
+    for group in range(GROUPS):
+        real, imag = combined(number, group, left, own_ref, other_ref, gamma_ref, chunk)
+        cols = slice(group * 256, group * 256 + 256)
+        out_ref[:NODES, cols] = real
+        out_ref[NODES:, cols] = imag
+
+
+def merge(number, chunk, info, own, other, gamma):
+    return pl.pallas_call(
+        functools.partial(merge_body, number, chunk),
+        out_shape=jax.ShapeDtypeStruct((2 * NODES, LANES), F32),
+        in_specs=[pl.BlockSpec(memory_space=pltpu.SMEM)] + vmem(4),
+        out_specs=vmem(1)[0],
+        name="merge_%d_%d" % (number, chunk),
+        compiler_params=SMALL,
+        cost_estimate=cost(0.4 * GROUPS),
+    )(info, own, other, gamma, jnp.asarray(merge_tables(LEVELS[number][0])))
+
+
+def finish_body(chunk, info_ref, own_ref, other_ref, gamma_ref, mix_ref, last_ref, *rest):
+    number = 3
+    out_ref, wide_ref, sem = rest[-3:]
+    left = mix_ref[(info_ref[5] >> 1) & 1]
     source = iota((256, 256), 0)
     target = iota((256, 256), 1)
     wanted = ((target // 16) % 2) * 128 + (target // 32) * 16 + target % 16
     order = jnp.where(source == wanted, 1.0, 0.0).astype(BF16)
-    for tile in range(4):
-        halves = []
-        for half in range(2):
-            cols = slice(half * 512 + tile * 128, half * 512 + tile * 128 + 128)
-            real, imag = combined(cols, slice(tile * 128, tile * 128 + 128))
-            cosine = last_ref[:NODES, cols]
-            sine = last_ref[NODES:, cols]
-            halves.append(jnp.concatenate([cosine * real + sine * imag, cosine * imag - sine * real], axis=0))
-        value = jnp.concatenate(halves, axis=1)
+    for group in range(GROUPS):
+        real, imag = combined(number, group, left, own_ref, other_ref, gamma_ref, chunk)
+        tile = chunk * GROUPS + group
+        cols = slice(tile * 256, tile * 256 + 256)
+        cosine = last_ref[:NODES, cols]
+        sine = last_ref[NODES:, cols]
+        value = jnp.concatenate([cosine * real + sine * imag, cosine * imag - sine * real], axis=0)
         high = value.astype(BF16)
         value = value - high.astype(F32)
         mid, low = split(value)
         moved = jnp.dot(jnp.concatenate([high, mid, low], axis=0), order, preferred_element_type=F32)
         moved = moved[:128] + moved[128:256] + moved[256:]
-        out_ref[0, :, tile * 256 : tile * 256 + 256] = moved[:NODES]
-        out_ref[1, :, tile * 256 : tile * 256 + 256] = moved[NODES:]
-
-
-def merge(number, info, own, other, gamma, last):
-    final = number == 3
-    args = [info, own, other, gamma, jnp.asarray(merge_tables(LEVELS[number][0]))]
-    if final:
-        args.append(last)
-    shape = (2, NODES, TARGETS) if final else (2 * NODES, TARGETS)
+        wide_ref[0, :, group * 256 : group * 256 + 256] = moved[:NODES]
+        wide_ref[1, :, group * 256 : group * 256 + 256] = moved[NODES:]
+    copy = pltpu.make_async_copy(wide_ref, out_ref.at[:, :, chunk * LANES : chunk * LANES + LANES], sem)
+    copy.start()
+    copy.wait()
+
+
+def finish(chunk, info, own, other, gamma, last, sofar):
+    args = [info, own, other, gamma, jnp.asarray(merge_tables(2)), last]
+    specs = [pl.BlockSpec(memory_space=pltpu.SMEM)] + vmem(5)
+    aliases = {}
+    if sofar is not None:
+        aliases = {len(args): 0}
+        args.append(sofar)
+        specs.append(pl.BlockSpec(memory_space=pl.ANY))
     return pl.pallas_call(
-        functools.partial(merge_body, number),
-        out_shape=jax.ShapeDtypeStruct(shape, F32),
-        in_specs=[pl.BlockSpec(memory_space=pltpu.SMEM)] + [pl.BlockSpec(memory_space=pltpu.VMEM)] * (len(args) - 1),
-        out_specs=pl.BlockSpec(memory_space=pltpu.VMEM),
-        name="merge_%d" % number,
+        functools.partial(finish_body, chunk),
+        out_shape=jax.ShapeDtypeStruct((2, NODES, TARGETS), F32),
+        in_specs=specs,
+        out_specs=pl.BlockSpec(memory_space=pl.ANY),
+        scratch_shapes=[pltpu.VMEM((2, NODES, LANES), F32), pltpu.SemaphoreType.DMA],
+        input_output_aliases=aliases,
+        name="finish_%d" % chunk,
+        compiler_params=SMALL,
+        cost_estimate=cost(0.8 * GROUPS),
     )(*args)
 
 
@@ -431,11 +507,18 @@
     info = jnp.concatenate([coef, place_on])
     sent = pack(point_box.reshape(-1, 128), point_offset, point_value)
     arrived = lax.all_to_all(sent.reshape(owners, 1, -1), ("bx", "by"), split_axis=0, concat_axis=0, tiled=True)
-    gamma, last = tables(info)
-    holding = leaf(info, arrived.reshape(owners, -1))
-    for number, (along, level) in enumerate(LEVELS):
-        holding = merge(number, info, holding, swap(holding, along, level), gamma, last)
-    return holding
+    prepared = prepare(info, arrived.reshape(owners, -1))
+    gammas = list(tables(info, (0, 1)))
+    *late, last = tables(info, (2, 3), True)
+    gammas += late
+    chunks = range(CHUNKS)
+    holding = [leaf(c, prepared) for c in chunks]
+    for number in range(3):
+        holding = [merge(number, c, info, holding[c], swap(holding[c], *LEVELS[number]), gammas[number]) for c in chunks]
+    out = None
+    for c in chunks:
+        out = finish(c, info, holding[c], swap(holding[c], *LEVELS[3]), gammas[3], last, out)
+    return out
 
 
 def solution(mesh):

time: 102 us -> 75 us (0.74)
  waiting for transfers between devices: 48.8 us -> 11.7 us
  starting transfers between devices: 13.2 us -> 27.6 us
  local copies, waits for them, and re-layouts: 3.84 us -> 0.01 us
    ppermute x4 -> x16, waiting for transfers between devices: 40.6 us -> 3.01 us  [swap(): lax.ppermute(value, axis, [(i, i ^ 1 << level) for i in range(lax.axis_si...]
    ppermute x4 -> x16, starting transfers between devices: 2.07 us -> 16.5 us  [swap(): lax.ppermute(value, axis, [(i, i ^ 1 << level) for i in range(lax.axis_si...]
    unnamed x10 -> x4, local copies, waits for them, and re-layouts: 3.84 us -> 0.01 us
    pallas_call x6 -> x23, Pallas kernels: 32.2 us -> 31.8 us  [the longest x4 9.74 us: leaf(): pl.pallas_call(functools.partial(leaf_body, chunk), out_shape=jax.ShapeDt...]
  transfers between devices with their start and end apart: 5 -> 17, of which waited for: 4 -> 5; matrix products, arithmetic and copies ran while one was open for 1% -> 1% of each run, Pallas kernels for 4% -> 33%
where the time goes in v3:
time: 75 us; the launch traced here: 74.7 us
  Pallas kernels  34.3 us (46%)
  starting transfers between devices  27.6 us (37%)
  waiting for transfers between devices  11.7 us (16%)
    ppermute x16, starting transfers between devices, swap(): lax.ppermute(value, axis, [(i, i ^ 1 << level) for i in range(lax.axis_si...  16.5 us
    all_to_all x1, starting transfers between devices, on_device(): lax.all_to_all(sent.reshape(owners, 1, -1), ('bx', 'by'), split_axis=0, c...  11.1 us
    pallas_call x4, Pallas kernels, leaf(): pl.pallas_call(functools.partial(leaf_body, chunk), out_shape=jax.ShapeDt...  9.74 us
    pallas_call x12, Pallas kernels, merge(): pl.pallas_call(functools.partial(merge_body, number, chunk), out_shape=ja...  9 us
    all_to_all x1, waiting for transfers between devices, on_device(): lax.all_to_all(sent.reshape(owners, 1, -1), ('bx', 'by'), split_axis=0, c...  8.67 us
    pallas_call x4, Pallas kernels, finish(): pl.pallas_call(functools.partial(finish_body, chunk), out_shape=jax.Shape...  6.4 us
    pallas_call x2, Pallas kernels, tables(): pl.pallas_call(functools.partial(tables_body, numbers, with_last), out_sh...  3.53 us
    pallas_call x1, Pallas kernels, prepare(): pl.pallas_call(prepare_body, out_shape=(jax.ShapeDtypeStruct((256, CAP *...  3.19 us
  transfers between devices with their start and end apart: 17, of which 5 were waited for; matrix products, arithmetic and copies ran while one was open for 1% of the time, Pallas kernels for 33%

profile of v3, /device:TPU:0, one launch (start us, length us, event | category | flops | bytes accessed | tf_op | source)
XLA Modules:
  0.0 74.7 jit_solution(4218777742265219602)
XLA Ops:
  0.0 2.4 %pack.1 = f32[128,128]{1,0:T(8,128)} custom-call(s32[16,128]{1,0:T(8,128)} %bitcast.9, s32[2,2048]{1,0:T(2,128)} %off_ref.1, f32[2,2048]{1,0:T(2,128)} %val_ref.1), custom_call_target="tpu_custom_call" | custom-call | bytes 7400000 | tf_op jit(solution)/shard_map/pack/pallas_call | solution.py:136
  2.4 11.1 %all-to-all-start = ((f32[128,1,128]{2,1,0:T(1,128)}), f32[128,1,128]{2,1,0:T(1,128)S(1)}, u32[]{:S(2)}, u32[]{:S(2)}) async-start(f32[128,1,128]{2,1,0:T(1,128)} %bitcast.8), calls=%async_computation | async-start | bytes 131072 | tf_op jit(solution)/shard_map/all_to_all | solution.py:509
  13.6 0.7 pad_add_fusion.info_ref
  14.3 8.7 %all-to-all-done = f32[128,1,128]{2,1,0:T(1,128)S(1)} async-done(((f32[128,1,128]{2,1,0:T(1,128)}), f32[128,1,128]{2,1,0:T(1,128)S(1)}, u32[]{:S(2)}, u32[]{:S(2)}) %all-to-all-start) | async-done | bytes 65568 | tf_op jit(solution)/shard_map/all_to_all | solution.py:509
  23.0 3.2 %prepare.1 = (bf16[256,4096]{1,0:T(8,128)(2,1)S(1)}, f32[32,4,32,128]{3,2,1,0:T(8,128)S(1)}, f32[32,2,16,128]{3,2,1,0:T(8,128)S(1)}) custom-call(s32[6]{0:T(128)S(1)} %pad_add_fusion.info_ref, f32[128,128]{1,0:T(8,128)S(1)} %bitcast.7), custom_call_target="tpu_custom_call" | custom-call | bytes 7400000 | tf_op jit(solution)/shard_map/prepare/pallas_call | solution.py:212
  26.2 2.4 %leaf_0.1.own_ref = f32[128,256]{1,0:T(8,128)S(1)} custom-call(bf16[256,4096]{1,0:T(8,128)(2,1)S(1)} %get-tuple-element.13.l_ref, f32[32,4,32,128]{3,2,1,0:T(8,128)S(1)} %get-tuple-element.14.q_ref, f32[32,2,16,128]{3,2,1,0:T(8,128)S(1)} %get-tuple-element.15.z_ref), custom_call_target="tpu_custom_call" | custom-call | bytes 9250000 | tf_op jit(solution)/shard_map/leaf_0/pallas_call | solution.py:277
  28.6 0.1 collective-permute-start.12
  28.7 2.4 %leaf_1.1.own_ref = f32[128,256]{1,0:T(8,128)S(1)} custom-call(bf16[256,4096]{1,0:T(8,128)(2,1)S(1)} %get-tuple-element.13.l_ref, f32[32,4,32,128]{3,2,1,0:T(8,128)S(1)} %get-tuple-element.14.q_ref, f32[32,2,16,128]{3,2,1,0:T(8,128)S(1)} %get-tuple-element.15.z_ref), custom_call_target="tpu_custom_call" | custom-call | bytes 9250000 | tf_op jit(solution)/shard_map/leaf_1/pallas_call | solution.py:277
  31.2 0.6 collective-permute-start.8
  31.7 2.4 %leaf_2.1.own_ref = f32[128,256]{1,0:T(8,128)S(1)} custom-call(bf16[256,4096]{1,0:T(8,128)(2,1)S(1)} %get-tuple-element.13.l_ref, f32[32,4,32,128]{3,2,1,0:T(8,128)S(1)} %get-tuple-element.14.q_ref, f32[32,2,16,128]{3,2,1,0:T(8,128)S(1)} %get-tuple-element.15.z_ref), custom_call_target="tpu_custom_call" | custom-call | bytes 9250000 | tf_op jit(solution)/shard_map/leaf_2/pallas_call | solution.py:277
  34.2 0.0 copy-start
  34.2 0.3 collective-permute-start.4
  34.5 2.4 %leaf_3.1.own_ref = f32[128,256]{1,0:T(8,128)S(1)} custom-call(bf16[256,4096]{1,0:T(8,128)(2,1)S(1)} %get-tuple-element.13.l_ref, f32[32,4,32,128]{3,2,1,0:T(8,128)S(1)} %get-tuple-element.14.q_ref, f32[32,2,16,128]{3,2,1,0:T(8,128)S(1)} %get-tuple-element.15.z_ref), custom_call_target="tpu_custom_call" | custom-call | bytes 9250000 | tf_op jit(solution)/shard_map/leaf_3/pallas_call | solution.py:277
  36.9 0.6 collective-permute-start
  37.5 1.6 %tables_01.1 = (f32[2,128,512]{2,1,0:T(8,128)S(1)}, f32[2,128,512]{2,1,0:T(8,128)S(1)}) custom-call(s32[6]{0:T(128)S(1)} %pad_add_fusion.info_ref), custom_call_target="tpu_custom_call" | custom-call | bytes 4440000 | tf_op jit(solution)/shard_map/tables_01/pallas_call | solution.py:394
  39.1 0.0 collective-permute-done.12.other_ref
  39.1 0.0 copy-done
  39.1 0.0 copy-start.1
  39.1 0.7 %merge_0_0.1.own_ref = f32[128,256]{1,0:T(8,128)S(1)} custom-call(s32[6]{0:T(128)S(1)} %pad_add_fusion.info_ref, f32[128,256]{1,0:T(8,128)S(1)} %leaf_0.1.own_ref, f32[128,256]{1,0:T(8,128)S(1)} %collective-permute-done.12.other_ref, f32[2,128,512]{2,1,0:T(8,128)S(1)} %get-tuple-element.16.gamma_ref, bf16[2,128,256]{2,1,0:T(8,128)(2,1)S(1)} %copy-done), custom_call_target="tpu_custom_call" | custom-call | bytes 1480000 | tf_op jit(solution)/shard_map/merge_0_0/pallas_call | solution.py:440
  39.9 0.7 collective-permute-start.13
  40.5 0.0 collective-permute-done.8.other_ref
  40.5 0.8 %merge_0_1.1.own_ref = f32[128,256]{1,0:T(8,128)S(1)} custom-call(s32[6]{0:T(128)S(1)} %pad_add_fusion.info_ref, f32[128,256]{1,0:T(8,128)S(1)} %leaf_1.1.own_ref, f32[128,256]{1,0:T(8,128)S(1)} %collective-permute-done.8.other_ref, f32[2,128,512]{2,1,0:T(8,128)S(1)} %get-tuple-element.16.gamma_ref, bf16[2,128,256]{2,1,0:T(8,128)(2,1)S(1)} %copy-done), custom_call_target="tpu_custom_call" | custom-call | bytes 1480000 | tf_op jit(solution)/shard_map/merge_0_1/pallas_call | solution.py:440
  41.3 1.5 %collective-permute-start.9 = (f32[128,256]{1,0:T(8,128)S(1)}, f32[128,256]{1,0:T(8,128)S(1)}, u32[]{:S(2)}, u32[]{:S(2)}) collective-permute-start(f32[128,256]{1,0:T(8,128)S(1)} %merge_0_1.1.own_ref), channel_id=1, source_target_pairs={{0,1},{1,0},{2,3},{3,2},{4,5},{5,4},{6,7},{7,6},{8,9},{9,8},{10,11... | collective-permute-start | bytes 393224 | tf_op jit(solution)/shard_map/ppermute | solution.py:501
  42.8 0.0 collective-permute-done.4.other_ref
  42.8 0.8 %merge_0_2.1.own_ref = f32[128,256]{1,0:T(8,128)S(1)} custom-call(s32[6]{0:T(128)S(1)} %pad_add_fusion.info_ref, f32[128,256]{1,0:T(8,128)S(1)} %leaf_2.1.own_ref, f32[128,256]{1,0:T(8,128)S(1)} %collective-permute-done.4.other_ref, f32[2,128,512]{2,1,0:T(8,128)S(1)} %get-tuple-element.16.gamma_ref, bf16[2,128,256]{2,1,0:T(8,128)(2,1)S(1)} %copy-done), custom_call_target="tpu_custom_call" | custom-call | bytes 1480000 | tf_op jit(solution)/shard_map/merge_0_2/pallas_call | solution.py:440
  43.6 0.7 collective-permute-start.5
  44.2 0.0 collective-permute-done.other_ref
  44.2 0.8 %merge_0_3.1.own_ref = f32[128,256]{1,0:T(8,128)S(1)} custom-call(s32[6]{0:T(128)S(1)} %pad_add_fusion.info_ref, f32[128,256]{1,0:T(8,128)S(1)} %leaf_3.1.own_ref, f32[128,256]{1,0:T(8,128)S(1)} %collective-permute-done.other_ref, f32[2,128,512]{2,1,0:T(8,128)S(1)} %get-tuple-element.16.gamma_ref, bf16[2,128,256]{2,1,0:T(8,128)(2,1)S(1)} %copy-done), custom_call_target="tpu_custom_call" | custom-call | bytes 1480000 | tf_op jit(solution)/shard_map/merge_0_3/pallas_call | solution.py:440
  45.0 1.5 %collective-permute-start.1 = (f32[128,256]{1,0:T(8,128)S(1)}, f32[128,256]{1,0:T(8,128)S(1)}, u32[]{:S(2)}, u32[]{:S(2)}) collective-permute-start(f32[128,256]{1,0:T(8,128)S(1)} %merge_0_3.1.own_ref), channel_id=1, source_target_pairs={{0,1},{1,0},{2,3},{3,2},{4,5},{5,4},{6,7},{7,6},{8,9},{9,8},{10,11... | collective-permute-start | bytes 393224 | tf_op jit(solution)/shard_map/ppermute | solution.py:501
  46.5 0.0 collective-permute-done.13.other_ref
  46.5 0.0 copy-done.1
  46.5 0.7 merge_1_0.1.own_ref
  47.3 0.7 collective-permute-start.14
  48.0 1.1 %collective-permute-done.9.other_ref = f32[128,256]{1,0:T(8,128)S(1)} collective-permute-done((f32[128,256]{1,0:T(8,128)S(1)}, f32[128,256]{1,0:T(8,128)S(1)}, u32[]{:S(2)}, u32[]{:S(2)}) %collective-permute-start.9) | collective-permute-done | bytes 131104 | tf_op jit(solution)/shard_map/ppermute | solution.py:501
  49.1 0.8 %merge_1_1.1.own_ref = f32[128,256]{1,0:T(8,128)S(1)} custom-call(s32[6]{0:T(128)S(1)} %pad_add_fusion.info_ref, f32[128,256]{1,0:T(8,128)S(1)} %merge_0_1.1.own_ref, f32[128,256]{1,0:T(8,128)S(1)} %collective-permute-done.9.other_ref, f32[2,128,512]{2,1,0:T(8,128)S(1)} %get-tuple-element.17.gamma_ref, bf16[2,128,256]{2,1,0:T(8,128)(2,1)S(1)} %copy-done.1), custom_call_target="tpu_custom_call" | custom-call | bytes 1480000 | tf_op jit(solution)/shard_map/merge_1_1/pallas_call | solution.py:440
  49.9 0.7 collective-permute-start.10
  50.6 1.3 %collective-permute-done.5.other_ref = f32[128,256]{1,0:T(8,128)S(1)} collective-permute-done((f32[128,256]{1,0:T(8,128)S(1)}, f32[128,256]{1,0:T(8,128)S(1)}, u32[]{:S(2)}, u32[]{:S(2)}) %collective-permute-start.5) | collective-permute-done | bytes 131104 | tf_op jit(solution)/shard_map/ppermute | solution.py:501
  51.9 0.8 %merge_1_2.1.own_ref = f32[128,256]{1,0:T(8,128)S(1)} custom-call(s32[6]{0:T(128)S(1)} %pad_add_fusion.info_ref, f32[128,256]{1,0:T(8,128)S(1)} %merge_0_2.1.own_ref, f32[128,256]{1,0:T(8,128)S(1)} %collective-permute-done.5.other_ref, f32[2,128,512]{2,1,0:T(8,128)S(1)} %get-tuple-element.17.gamma_ref, bf16[2,128,256]{2,1,0:T(8,128)(2,1)S(1)} %copy-done.1), custom_call_target="tpu_custom_call" | custom-call | bytes 1480000 | tf_op jit(solution)/shard_map/merge_1_2/pallas_call | solution.py:440
  52.7 0.7 collective-permute-start.6
  53.4 0.4 collective-permute-done.1.other_ref
  53.8 0.8 %merge_1_3.1.own_ref = f32[128,256]{1,0:T(8,128)S(1)} custom-call(s32[6]{0:T(128)S(1)} %pad_add_fusion.info_ref, f32[128,256]{1,0:T(8,128)S(1)} %merge_0_3.1.own_ref, f32[128,256]{1,0:T(8,128)S(1)} %collective-permute-done.1.other_ref, f32[2,128,512]{2,1,0:T(8,128)S(1)} %get-tuple-element.17.gamma_ref, bf16[2,128,256]{2,1,0:T(8,128)(2,1)S(1)} %copy-done.1), custom_call_target="tpu_custom_call" | custom-call | bytes 1480000 | tf_op jit(solution)/shard_map/merge_1_3/pallas_call | solution.py:440
  54.6 1.1 %collective-permute-start.2 = (f32[128,256]{1,0:T(8,128)S(1)}, f32[128,256]{1,0:T(8,128)S(1)}, u32[]{:S(2)}, u32[]{:S(2)}) collective-permute-start(f32[128,256]{1,0:T(8,128)S(1)} %merge_1_3.1.own_ref), channel_id=1, source_target_pairs={{0,32},{16,48},{32,0},{48,16},{64,96},{80,112},{96,64},{112,80},{1... | collective-permute-start | bytes 393224 | tf_op jit(solution)/shard_map/ppermute | solution.py:501
  55.6 1.9 %tables_23.1 = (f32[2,128,512]{2,1,0:T(8,128)S(1)}, f32[2,128,512]{2,1,0:T(8,128)S(1)}, f32[128,1024]{1,0:T(8,128)S(1)}) custom-call(s32[6]{0:T(128)S(1)} %pad_add_fusion.info_ref), custom_call_target="tpu_custom_call" | custom-call | bytes 6659999 | tf_op jit(solution)/shard_map/tables_23/pallas_call | solution.py:394
  57.6 0.0 collective-permute-done.14.other_ref
  57.6 0.7 %merge_2_0.1.own_ref = f32[128,256]{1,0:T(8,128)S(1)} custom-call(s32[6]{0:T(128)S(1)} %pad_add_fusion.info_ref, f32[128,256]{1,0:T(8,128)S(1)} %merge_1_0.1.own_ref, f32[128,256]{1,0:T(8,128)S(1)} %collective-permute-done.14.other_ref, f32[2,128,512]{2,1,0:T(8,128)S(1)} %get-tuple-element.18.gamma_ref, bf16[2,128,256]{2,1,0:T(8,128)(2,1)S(1)} %copy-done), custom_call_target="tpu_custom_call" | custom-call | bytes 1480000 | tf_op jit(solution)/shard_map/merge_2_0/pallas_call | solution.py:440
  58.3 0.7 collective-permute-start.15
  59.1 0.0 collective-permute-done.10.other_ref
  59.1 0.8 %merge_2_1.1.own_ref = f32[128,256]{1,0:T(8,128)S(1)} custom-call(s32[6]{0:T(128)S(1)} %pad_add_fusion.info_ref, f32[128,256]{1,0:T(8,128)S(1)} %merge_1_1.1.own_ref, f32[128,256]{1,0:T(8,128)S(1)} %collective-permute-done.10.other_ref, f32[2,128,512]{2,1,0:T(8,128)S(1)} %get-tuple-element.18.gamma_ref, bf16[2,128,256]{2,1,0:T(8,128)(2,1)S(1)} %copy-done), custom_call_target="tpu_custom_call" | custom-call | bytes 1480000 | tf_op jit(solution)/shard_map/merge_2_1/pallas_call | solution.py:440
  59.8 2.9 %collective-permute-start.11 = (f32[128,256]{1,0:T(8,128)S(1)}, f32[128,256]{1,0:T(8,128)S(1)}, u32[]{:S(2)}, u32[]{:S(2)}) collective-permute-start(f32[128,256]{1,0:T(8,128)S(1)} %merge_2_1.1.own_ref), channel_id=1, source_target_pairs={{0,2},{1,3},{2,0},{3,1},{4,6},{5,7},{6,4},{7,5},{8,10},{9,11},{10,... | collective-permute-start | bytes 393224 | tf_op jit(solution)/shard_map/ppermute | solution.py:501
  62.8 0.0 collective-permute-done.6.other_ref
  62.8 0.8 %merge_2_2.1.own_ref = f32[128,256]{1,0:T(8,128)S(1)} custom-call(s32[6]{0:T(128)S(1)} %pad_add_fusion.info_ref, f32[128,256]{1,0:T(8,128)S(1)} %merge_1_2.1.own_ref, f32[128,256]{1,0:T(8,128)S(1)} %collective-permute-done.6.other_ref, f32[2,128,512]{2,1,0:T(8,128)S(1)} %get-tuple-element.18.gamma_ref, bf16[2,128,256]{2,1,0:T(8,128)(2,1)S(1)} %copy-done), custom_call_target="tpu_custom_call" | custom-call | bytes 1480000 | tf_op jit(solution)/shard_map/merge_2_2/pallas_call | solution.py:440
  63.5 0.7 collective-permute-start.7
  64.3 0.0 collective-permute-done.2.other_ref
  64.3 0.8 %merge_2_3.1.own_ref = f32[128,256]{1,0:T(8,128)S(1)} custom-call(s32[6]{0:T(128)S(1)} %pad_add_fusion.info_ref, f32[128,256]{1,0:T(8,128)S(1)} %merge_1_3.1.own_ref, f32[128,256]{1,0:T(8,128)S(1)} %collective-permute-done.2.other_ref, f32[2,128,512]{2,1,0:T(8,128)S(1)} %get-tuple-element.18.gamma_ref, bf16[2,128,256]{2,1,0:T(8,128)(2,1)S(1)} %copy-done), custom_call_target="tpu_custom_call" | custom-call | bytes 1480000 | tf_op jit(solution)/shard_map/merge_2_3/pallas_call | solution.py:440
  65.1 2.9 %collective-permute-start.3 = (f32[128,256]{1,0:T(8,128)S(1)}, f32[128,256]{1,0:T(8,128)S(1)}, u32[]{:S(2)}, u32[]{:S(2)}) collective-permute-start(f32[128,256]{1,0:T(8,128)S(1)} %merge_2_3.1.own_ref), channel_id=1, source_target_pairs={{0,2},{1,3},{2,0},{3,1},{4,6},{5,7},{6,4},{7,5},{8,10},{9,11},{10,... | collective-permute-start | bytes 393224 | tf_op jit(solution)/shard_map/ppermute | solution.py:501
  68.0 0.0 collective-permute-done.15.other_ref
  68.0 1.6 %finish_0.1.rest_0_ = f32[2,64,1024]{2,1,0:T(8,128)} custom-call(s32[6]{0:T(128)S(1)} %pad_add_fusion.info_ref, f32[128,256]{1,0:T(8,128)S(1)} %merge_2_0.1.own_ref, f32[128,256]{1,0:T(8,128)S(1)} %collective-permute-done.15.other_ref, f32[2,128,512]{2,1,0:T(8,128)S(1)} %get-tuple-element.19.gamma_ref, bf16[2,128,256]{2,1,0:T(8,128)(2,1)S(1)} %copy-done.1, ...), custom_call_target="tpu_custom_call" | custom-call | bytes 2960000 | tf_op jit(solution)/shard_map/finish_0/pallas_call | solution.py:486
  69.6 0.0 collective-permute-done.11.other_ref
  69.6 1.6 %finish_1.1.rest_0_ = f32[2,64,1024]{2,1,0:T(8,128)} custom-call(s32[6]{0:T(128)S(1)} %pad_add_fusion.info_ref, f32[128,256]{1,0:T(8,128)S(1)} %merge_2_1.1.own_ref, f32[128,256]{1,0:T(8,128)S(1)} %collective-permute-done.11.other_ref, f32[2,128,512]{2,1,0:T(8,128)S(1)} %get-tuple-element.19.gamma_ref, ...), custom_call_target="tpu_custom_call", output_to_operand_aliasing={{}: (6, {})} | custom-call | bytes 2960000 | tf_op jit(solution)/shard_map/finish_1/pallas_call | solution.py:486
  71.2 0.1 collective-permute-done.7.other_ref
  71.4 1.6 %finish_2.1.rest_0_ = f32[2,64,1024]{2,1,0:T(8,128)} custom-call(s32[6]{0:T(128)S(1)} %pad_add_fusion.info_ref, f32[128,256]{1,0:T(8,128)S(1)} %merge_2_2.1.own_ref, f32[128,256]{1,0:T(8,128)S(1)} %collective-permute-done.7.other_ref, f32[2,128,512]{2,1,0:T(8,128)S(1)} %get-tuple-element.19.gamma_ref, ...), custom_call_target="tpu_custom_call", output_to_operand_aliasing={{}: (6, {})} | custom-call | bytes 2960000 | tf_op jit(solution)/shard_map/finish_2/pallas_call | solution.py:486
  73.0 0.0 collective-permute-done.3.other_ref
  73.0 1.6 %finish_3.1 = f32[2,64,1024]{2,1,0:T(8,128)} custom-call(s32[6]{0:T(128)S(1)} %pad_add_fusion.info_ref, f32[128,256]{1,0:T(8,128)S(1)} %merge_2_3.1.own_ref, f32[128,256]{1,0:T(8,128)S(1)} %collective-permute-done.3.other_ref, f32[2,128,512]{2,1,0:T(8,128)S(1)} %get-tuple-element.19.gamma_ref, ...), custom_call_target="tpu_custom_call", output_to_operand_aliasing={{}: (6, {})} | custom-call | bytes 2960000 | tf_op jit(solution)/shard_map/finish_3/pallas_call | solution.py:486
Async XLA Ops:
  2.4 20.6 %all-to-all-start = ((f32[128,1,128]{2,1,0:T(1,128)}), f32[128,1,128]{2,1,0:T(1,128)S(1)}, u32[]{:S(2)}, u32[]{:S(2)}) async-start(f32[128,1,128]{2,1,0:T(1,128)} %bitcast.8), calls=%async_computation | async-start | bytes 131072 | tf_op jit(solution)/shard_map/all_to_all | solution.py:509
  28.6 10.5 %collective-permute-start.12 = (f32[128,256]{1,0:T(8,128)S(1)}, f32[128,256]{1,0:T(8,128)S(1)}, u32[]{:S(2)}, u32[]{:S(2)}) collective-permute-start(f32[128,256]{1,0:T(8,128)S(1)} %leaf_0.1.own_ref), channel_id=1, source_target_pairs={{0,16},{16,0},{32,48},{48,32},{64,80},{80,64},{96,112},{112,96},{1... | collective-permute-start | bytes 393224 | tf_op jit(solution)/shard_map/ppermute | solution.py:501
  31.2 9.4 %collective-permute-start.8 = (f32[128,256]{1,0:T(8,128)S(1)}, f32[128,256]{1,0:T(8,128)S(1)}, u32[]{:S(2)}, u32[]{:S(2)}) collective-permute-start(f32[128,256]{1,0:T(8,128)S(1)} %leaf_1.1.own_ref), channel_id=1, source_target_pairs={{0,16},{16,0},{32,48},{48,32},{64,80},{80,64},{96,112},{112,96},{1... | collective-permute-start | bytes 393224 | tf_op jit(solution)/shard_map/ppermute | solution.py:501
  34.2 4.9 %copy-start = (bf16[2,128,256]{2,1,0:T(8,128)(2,1)S(1)}, bf16[2,128,256]{2,1,0:T(8,128)(2,1)}, u32[]{:S(2)}) copy-start(bf16[2,128,256]{2,1,0:T(8,128)(2,1)} %constant.13.clone.mix_ref) | copy-start | bytes 393220
  34.2 8.6 %collective-permute-start.4 = (f32[128,256]{1,0:T(8,128)S(1)}, f32[128,256]{1,0:T(8,128)S(1)}, u32[]{:S(2)}, u32[]{:S(2)}) collective-permute-start(f32[128,256]{1,0:T(8,128)S(1)} %leaf_2.1.own_ref), channel_id=1, source_target_pairs={{0,16},{16,0},{32,48},{48,32},{64,80},{80,64},{96,112},{112,96},{1... | collective-permute-start | bytes 393224 | tf_op jit(solution)/shard_map/ppermute | solution.py:501
  36.9 7.3 %collective-permute-start = (f32[128,256]{1,0:T(8,128)S(1)}, f32[128,256]{1,0:T(8,128)S(1)}, u32[]{:S(2)}, u32[]{:S(2)}) collective-permute-start(f32[128,256]{1,0:T(8,128)S(1)} %leaf_3.1.own_ref), channel_id=1, source_target_pairs={{0,16},{16,0},{32,48},{48,32},{64,80},{80,64},{96,112},{112,96},{1... | collective-permute-start | bytes 393224 | tf_op jit(solution)/shard_map/ppermute | solution.py:501
  39.1 7.4 %copy-start.1 = (bf16[2,128,256]{2,1,0:T(8,128)(2,1)S(1)}, bf16[2,128,256]{2,1,0:T(8,128)(2,1)}, u32[]{:S(2)}) copy-start(bf16[2,128,256]{2,1,0:T(8,128)(2,1)} %constant.14.clone.mix_ref) | copy-start | bytes 393220
  39.9 6.7 %collective-permute-start.13 = (f32[128,256]{1,0:T(8,128)S(1)}, f32[128,256]{1,0:T(8,128)S(1)}, u32[]{:S(2)}, u32[]{:S(2)}) collective-permute-start(f32[128,256]{1,0:T(8,128)S(1)} %merge_0_0.1.own_ref), channel_id=1, source_target_pairs={{0,1},{1,0},{2,3},{3,2},{4,5},{5,4},{6,7},{7,6},{8,9},{9,8},{10,11... | collective-permute-start | bytes 393224 | tf_op jit(solution)/shard_map/ppermute | solution.py:501
  41.3 7.8 %collective-permute-start.9 = (f32[128,256]{1,0:T(8,128)S(1)}, f32[128,256]{1,0:T(8,128)S(1)}, u32[]{:S(2)}, u32[]{:S(2)}) collective-permute-start(f32[128,256]{1,0:T(8,128)S(1)} %merge_0_1.1.own_ref), channel_id=1, source_target_pairs={{0,1},{1,0},{2,3},{3,2},{4,5},{5,4},{6,7},{7,6},{8,9},{9,8},{10,11... | collective-permute-start | bytes 393224 | tf_op jit(solution)/shard_map/ppermute | solution.py:501
  43.6 8.3 %collective-permute-start.5 = (f32[128,256]{1,0:T(8,128)S(1)}, f32[128,256]{1,0:T(8,128)S(1)}, u32[]{:S(2)}, u32[]{:S(2)}) collective-permute-start(f32[128,256]{1,0:T(8,128)S(1)} %merge_0_2.1.own_ref), channel_id=1, source_target_pairs={{0,1},{1,0},{2,3},{3,2},{4,5},{5,4},{6,7},{7,6},{8,9},{9,8},{10,11... | collective-permute-start | bytes 393224 | tf_op jit(solution)/shard_map/ppermute | solution.py:501
  45.0 8.8 %collective-permute-start.1 = (f32[128,256]{1,0:T(8,128)S(1)}, f32[128,256]{1,0:T(8,128)S(1)}, u32[]{:S(2)}, u32[]{:S(2)}) collective-permute-start(f32[128,256]{1,0:T(8,128)S(1)} %merge_0_3.1.own_ref), channel_id=1, source_target_pairs={{0,1},{1,0},{2,3},{3,2},{4,5},{5,4},{6,7},{7,6},{8,9},{9,8},{10,11... | collective-permute-start | bytes 393224 | tf_op jit(solution)/shard_map/ppermute | solution.py:501
  47.3 10.3 %collective-permute-start.14 = (f32[128,256]{1,0:T(8,128)S(1)}, f32[128,256]{1,0:T(8,128)S(1)}, u32[]{:S(2)}, u32[]{:S(2)}) collective-permute-start(f32[128,256]{1,0:T(8,128)S(1)} %merge_1_0.1.own_ref), channel_id=1, source_target_pairs={{0,32},{16,48},{32,0},{48,16},{64,96},{80,112},{96,64},{112,80},{1... | collective-permute-start | bytes 393224 | tf_op jit(solution)/shard_map/ppermute | solution.py:501
  49.9 9.2 %collective-permute-start.10 = (f32[128,256]{1,0:T(8,128)S(1)}, f32[128,256]{1,0:T(8,128)S(1)}, u32[]{:S(2)}, u32[]{:S(2)}) collective-permute-start(f32[128,256]{1,0:T(8,128)S(1)} %merge_1_1.1.own_ref), channel_id=1, source_target_pairs={{0,32},{16,48},{32,0},{48,16},{64,96},{80,112},{96,64},{112,80},{1... | collective-permute-start | bytes 393224 | tf_op jit(solution)/shard_map/ppermute | solution.py:501
  52.7 10.1 %collective-permute-start.6 = (f32[128,256]{1,0:T(8,128)S(1)}, f32[128,256]{1,0:T(8,128)S(1)}, u32[]{:S(2)}, u32[]{:S(2)}) collective-permute-start(f32[128,256]{1,0:T(8,128)S(1)} %merge_1_2.1.own_ref), channel_id=1, source_target_pairs={{0,32},{16,48},{32,0},{48,16},{64,96},{80,112},{96,64},{112,80},{1... | collective-permute-start | bytes 393224 | tf_op jit(solution)/shard_map/ppermute | solution.py:501
  54.6 9.7 %collective-permute-start.2 = (f32[128,256]{1,0:T(8,128)S(1)}, f32[128,256]{1,0:T(8,128)S(1)}, u32[]{:S(2)}, u32[]{:S(2)}) collective-permute-start(f32[128,256]{1,0:T(8,128)S(1)} %merge_1_3.1.own_ref), channel_id=1, source_target_pairs={{0,32},{16,48},{32,0},{48,16},{64,96},{80,112},{96,64},{112,80},{1... | collective-permute-start | bytes 393224 | tf_op jit(solution)/shard_map/ppermute | solution.py:501
  58.3 9.7 %collective-permute-start.15 = (f32[128,256]{1,0:T(8,128)S(1)}, f32[128,256]{1,0:T(8,128)S(1)}, u32[]{:S(2)}, u32[]{:S(2)}) collective-permute-start(f32[128,256]{1,0:T(8,128)S(1)} %merge_2_0.1.own_ref), channel_id=1, source_target_pairs={{0,2},{1,3},{2,0},{3,1},{4,6},{5,7},{6,4},{7,5},{8,10},{9,11},{10,... | collective-permute-start | bytes 393224 | tf_op jit(solution)/shard_map/ppermute | solution.py:501
  59.8 9.8 %collective-permute-start.11 = (f32[128,256]{1,0:T(8,128)S(1)}, f32[128,256]{1,0:T(8,128)S(1)}, u32[]{:S(2)}, u32[]{:S(2)}) collective-permute-start(f32[128,256]{1,0:T(8,128)S(1)} %merge_2_1.1.own_ref), channel_id=1, source_target_pairs={{0,2},{1,3},{2,0},{3,1},{4,6},{5,7},{6,4},{7,5},{8,10},{9,11},{10,... | collective-permute-start | bytes 393224 | tf_op jit(solution)/shard_map/ppermute | solution.py:501
  63.5 7.8 %collective-permute-start.7 = (f32[128,256]{1,0:T(8,128)S(1)}, f32[128,256]{1,0:T(8,128)S(1)}, u32[]{:S(2)}, u32[]{:S(2)}) collective-permute-start(f32[128,256]{1,0:T(8,128)S(1)} %merge_2_2.1.own_ref), channel_id=1, source_target_pairs={{0,2},{1,3},{2,0},{3,1},{4,6},{5,7},{6,4},{7,5},{8,10},{9,11},{10,... | collective-permute-start | bytes 393224 | tf_op jit(solution)/shard_map/ppermute | solution.py:501
  65.1 7.9 %collective-permute-start.3 = (f32[128,256]{1,0:T(8,128)S(1)}, f32[128,256]{1,0:T(8,128)S(1)}, u32[]{:S(2)}, u32[]{:S(2)}) collective-permute-start(f32[128,256]{1,0:T(8,128)S(1)} %merge_2_3.1.own_ref), channel_id=1, source_target_pairs={{0,2},{1,3},{2,0},{3,1},{4,6},{5,7},{6,4},{7,5},{8,10},{9,11},{10,... | collective-permute-start | bytes 393224 | tf_op jit(solution)/shard_map/ppermute | solution.py:501

commit v4 on v3

v4 whole, which is shorter than its diff:
```python
import functools
import math

import jax
import jax.numpy as jnp
import numpy as np
from jax import lax
from jax.experimental import pallas as pl
from jax.experimental.pallas import tpu as pltpu
from jax.sharding import PartitionSpec as P

N = 16384
ORDER = 8
TGT = 32
CAP = 32
CHUNKS = ((0, 2), (2, 2))
STEP = 8
NODES = ORDER * ORDER
TARGETS = TGT * TGT
F32 = jnp.float32
BF16 = jnp.bfloat16

SIN_C = (3.1415925798055824, -5.167706866167939, 2.550031193519312, -0.5980441939121666, 0.07721838615746283)
COS_C = (0.9999999532476086, -4.934792830619651, 4.058411352862725, -1.3318765680816773, 0.21968961109948903)


def node_table():
    counting = np.arange(ORDER) * 1.0
    return 0.5 - 0.5 * np.cos(np.pi * (2.0 * counting + 1.0) / (2.0 * ORDER))


def child_matrix(side):
    nodes = node_table()
    points = 0.5 * (side + nodes)
    rows = []
    for target in range(ORDER):
        factor = np.ones(ORDER)
        for source in range(ORDER):
            if source != target:
                factor = factor * (points - nodes[source]) / (nodes[target] - nodes[source])
        rows.append(factor)
    return np.stack(rows)


def merge_tables(along):
    eye = np.eye(ORDER)
    both = []
    for bit in range(2):
        parts = []
        for side in (bit, 1 - bit):
            matrix = child_matrix(side)
            parts.append(np.kron(matrix, eye) if along == 1 else np.kron(eye, matrix))
        full = np.concatenate(parts, axis=1)
        high = full.astype(np.float32).astype(BF16)
        low = (full - high.astype(np.float64)).astype(np.float32).astype(BF16)
        top = np.concatenate([high, high], axis=1)
        bottom = np.concatenate([low, np.zeros_like(low)], axis=1)
        both.append(np.concatenate([top, bottom], axis=0))
    return np.stack(both)


def horner(coefs, x):
    total = coefs[-1]
    for c in coefs[-2::-1]:
        total = total * x + c
    return total


def turn(phase):
    r = phase - jnp.floor(phase + 0.5)
    x = r * r
    sine = horner(SIN_C, x) * r
    cosine = horner(COS_C, x)
    twice = sine + sine
    return 1.0 - twice * sine, twice * cosine


def split(x):
    high = x.astype(BF16)
    return high, (x - high.astype(F32)).astype(BF16)


def cost(micros):
    return pl.CostEstimate(flops=0, bytes_accessed=int(micros * 3.7e6), transcendentals=0)


def vmem(count):
    return [pl.BlockSpec(memory_space=pltpu.VMEM)] * count


def anywhere(count):
    return [pl.BlockSpec(memory_space=pl.ANY)] * count


SMALL = pltpu.CompilerParams(vmem_limit_bytes=12 << 20)


def iota(shape, axis):
    return lax.broadcasted_iota(jnp.int32, shape, axis)


def nt(a, b):
    return lax.dot_general(a, b, (((1,), (1,)), ((), ())), preferred_element_type=F32)


def pack_body(box_ref, off_ref, val_ref, out_ref):
    blocks = box_ref.shape[0]
    row = iota((128, 128), 0)
    row2 = iota((128, 256), 0)
    col2 = iota((128, 256), 1)
    prefix = jnp.where((row2 < col2) | (col2 >= 128), 1.0, 0.0).astype(BF16)
    same = [row == box_ref[b : b + 1, :] for b in range(blocks)]
    ones = [jnp.where(m, 1.0, 0.0).astype(BF16) for m in same]
    counts = jnp.dot(jnp.concatenate(ones, axis=0), prefix, preferred_element_type=F32)
    slots = iota((CAP, 128), 0).astype(F32)
    carry = jnp.zeros((128, 128), F32)
    wide = []
    for b in range(blocks):
        part = counts[b * 128 : (b + 1) * 128]
        rank = jnp.sum(jnp.where(same[b], part[:, :128] + carry, 0.0), axis=0, keepdims=True)
        carry = carry + part[:, 128:]
        hit = slots == rank
        cols = slice(b * 128, (b + 1) * 128)
        values = [off_ref[0:1, cols].astype(F32), off_ref[1:2, cols].astype(F32), val_ref[0:1, cols], val_ref[1:2, cols]]
        pieces = [[], [], []]
        for v in values:
            rest = v
            for piece in pieces:
                top = rest.astype(BF16).astype(F32)
                rest = rest - top
                piece.append(jnp.where(hit, top, 0.0).astype(BF16))
        wide.append(jnp.concatenate([x for piece in pieces for x in piece], axis=0))
    total = nt(jnp.concatenate(ones, axis=1), jnp.concatenate(wide, axis=1))
    out_ref[...] = total[:, :128] + total[:, 128:256] + total[:, 256:]


def pack(box, offsets, values):
    return pl.pallas_call(
        pack_body,
        out_shape=jax.ShapeDtypeStruct((128, 4 * CAP), F32),
        in_specs=[pl.BlockSpec(memory_space=pltpu.VMEM)] * 3,
        out_specs=pl.BlockSpec(memory_space=pltpu.VMEM),
        name="pack",
        cost_estimate=cost(2.0),
    )(box, offsets, values)


def basis_rows(tau):
    nodes = node_table()
    which = iota((ORDER, 128), 0)
    total = None
    for step in range(1, ORDER):
        other = jnp.zeros((ORDER, 128), F32)
        scale = jnp.zeros((ORDER, 128), F32)
        for t in range(ORDER):
            s = (t + step) % ORDER
            other = jnp.where(which == t, float(nodes[s]), other)
            scale = jnp.where(which == t, float(1.0 / (nodes[t] - nodes[s])), scale)
        factor = (tau - other) * scale
        total = factor if total is None else total * factor
    return total


def prepare_body(info_ref, rx_ref, *rest):
    l_ref, q_ref, z_ref, xt_ref, trig_ref = rest[-5:]
    width_first, width_second = float(N // 8), float(N // 16)
    corner_first = info_ref[4].astype(F32) * width_first
    corner_second = info_ref[5].astype(F32) * width_second
    xt_ref[...] = rx_ref[...].T

    order = iota((TGT, 128), 0)
    klass = (order % 16) * 2 + order // 16
    _, wave = turn((klass.astype(F32) + 1.5) * (1.0 / 32.0))
    speed_first = (32.0 + info_ref[0].astype(F32) + info_ref[1].astype(F32) * wave) * (1.0 / 4096.0)
    speed_second = (32.0 + info_ref[2].astype(F32) + info_ref[3].astype(F32) * wave) * (1.0 / 4096.0)
    lin_first = (order // 16 * 2 + 1).astype(F32) * (1.0 / 4096.0)
    lin_second = (order % 16 * 4 + 34).astype(F32) * (1.0 / 4096.0)
    power = iota((16, 128), 0).astype(F32) * (1.0 / 1024.0)

    second_all = xt_ref[CAP : 2 * CAP, :] + corner_second
    cosine, sine = turn(second_all * (1.0 / 128.0))
    trig_ref[0] = cosine
    trig_ref[1] = sine
    trig_ref[2] = 1.0 - 2.0 * sine * sine
    trig_ref[3] = 2.0 * cosine * sine

    for s in range(CAP):
        off_first = xt_ref[s : s + 1, :]
        off_second = xt_ref[CAP + s : CAP + s + 1, :]
        real_in = xt_ref[2 * CAP + s : 2 * CAP + s + 1, :]
        imag_in = xt_ref[3 * CAP + s : 3 * CAP + s + 1, :]
        wrap_real = trig_ref[2, s : s + 1, :]
        wrap_imag = trig_ref[3, s : s + 1, :]
        first = off_first + corner_first
        second = off_second + corner_second
        a = speed_first * first
        b = speed_second * second
        root = jnp.sqrt(1.0 + a * a + b * b)
        root = root - jnp.floor(root)
        lin = lin_first * first + lin_second * second
        cosine, sine = turn(root + (lin - jnp.floor(lin)))
        more_cosine = cosine * wrap_real - sine * wrap_imag
        more_sine = cosine * wrap_imag + sine * wrap_real
        for eps in range(2):
            rows = slice(eps * 16, eps * 16 + 16)
            q_ref[s, 2 * eps, :16] = cosine[rows]
            q_ref[s, 2 * eps, 16:] = more_cosine[rows]
            q_ref[s, 2 * eps + 1, :16] = sine[rows]
            q_ref[s, 2 * eps + 1, 16:] = more_sine[rows]
        cosine, sine = turn(power * (first - second))
        z_ref[s, 0] = cosine * real_in - sine * imag_in
        z_ref[s, 1] = cosine * imag_in + sine * real_in
        cols = slice(s * 128, s * 128 + 128)
        first_rows = basis_rows(off_first * (1.0 / width_first))
        second_rows = basis_rows(off_second * (1.0 / width_second))
        for part in range(2):
            scaled = second_rows * trig_ref[part, s : s + 1, :]
            for t in range(0, ORDER, 2):
                pair = jnp.concatenate([first_rows[t : t + 1] * scaled, first_rows[t + 1 : t + 2] * scaled], axis=0)
                high, low = split(pair)
                base = part * NODES + t * ORDER
                l_ref[base : base + 16, cols] = high
                l_ref[128 + base : 128 + base + 16, cols] = low


def prepare(info, arrived, after):
    return pl.pallas_call(
        prepare_body,
        out_shape=(
            jax.ShapeDtypeStruct((256, CAP * 128), BF16),
            jax.ShapeDtypeStruct((CAP, 4, TGT, 128), F32),
            jax.ShapeDtypeStruct((CAP, 2, 16, 128), F32),
        ),
        in_specs=[pl.BlockSpec(memory_space=pltpu.SMEM)] + vmem(1) + anywhere(len(after)),
        out_specs=vmem(3),
        scratch_shapes=[pltpu.VMEM((128, 128), F32), pltpu.VMEM((4, CAP, 128), F32)],
        name="prepare",
        compiler_params=SMALL,
        cost_estimate=cost(2.0),
    )(info, arrived, *after)


def leaf_body(chunk, l_ref, q_ref, z_ref, *rest):
    start, groups = chunk
    out_ref, ra_ref, rb_ref, acc_ref = rest[-4:]
    half = STEP * 128

    def build(step, r_ref):
        for j in range(STEP):
            s = step * STEP + j
            cols = slice(j * 128, j * 128 + 128)
            low_cols = slice(half + j * 128, half + j * 128 + 128)
            for local in range(4 * groups):
                up = start * 4 + local
                zr = z_ref[s, 0, up : up + 1, :]
                zi = z_ref[s, 1, up : up + 1, :]
                for eps in range(2):
                    qr = q_ref[s, 2 * eps, up : up + 16, :]
                    qi = q_ref[s, 2 * eps + 1, up : up + 16, :]
                    for part, value in enumerate((qr * zr - qi * zi, qr * zi + qi * zr)):
                        high, low = split(value)
                        base = (local // 4) * 256 + part * 128 + (2 * (local % 4) + eps) * 16
                        r_ref[base : base + 16, cols] = high
                        r_ref[base : base + 16, low_cols] = low

    steps = CAP // STEP
    build(0, ra_ref)
    for step in range(steps):
        now, later = (ra_ref, rb_ref) if step % 2 == 0 else (rb_ref, ra_ref)
        if step + 1 < steps:
            build(step + 1, later)
        right = l_ref[:, step * half : step * half + half]
        product = nt(now[...], jnp.concatenate([right, right], axis=1))
        if step == 0:
            acc_ref[...] = product
        else:
            acc_ref[...] += product

    for g in range(groups):
        blocks = []
        for part in range(2):
            rows = slice(g * 256 + part * 128, g * 256 + part * 128 + 128)
            blocks.append((acc_ref[rows, :128] + acc_ref[rows, 128:]).T)
        (cr, sr), (ci, si) = [(x[:NODES], x[NODES:]) for x in blocks]
        low_cols = slice(g * 256, g * 256 + 128)
        high_cols = slice(g * 256 + 128, g * 256 + 256)
        out_ref[:NODES, low_cols] = cr + si
        out_ref[NODES:, low_cols] = ci - sr
        out_ref[:NODES, high_cols] = cr - si
        out_ref[NODES:, high_cols] = ci + sr


def leaf(chunk, prepared, after):
    lanes = 256 * chunk[1]
    return pl.pallas_call(
        functools.partial(leaf_body, chunk),
        out_shape=jax.ShapeDtypeStruct((2 * NODES, lanes), F32),
        in_specs=vmem(3) + anywhere(len(after)),
        out_specs=vmem(1)[0],
        scratch_shapes=[
            pltpu.VMEM((lanes, STEP * 256), BF16),
            pltpu.VMEM((lanes, STEP * 256), BF16),
            pltpu.VMEM((lanes, 256), F32),
        ],
        name="leaf_%d" % chunk[0],
        compiler_params=SMALL,
        cost_estimate=cost(2.3 * chunk[1]),
    )(*prepared, *after)


def place(index, merged):
    code = jnp.int32(0)
    for bit in range(merged):
        code = code + ((index >> bit) & 1) * 2 ** (merged - 1 - bit)
    return (code.astype(F32) + 0.5) * (1.0 / 2.0**merged)


def node_columns(shape):
    nodes = node_table()
    row = iota(shape, 0)
    first = jnp.zeros(shape, F32)
    second = jnp.zeros(shape, F32)
    for t in range(ORDER):
        first = jnp.where(row // ORDER == t, float(nodes[t]), first)
        second = jnp.where(row % ORDER == t, float(nodes[t]), second)
    return first, second


def speeds(info_ref, klass, at):
    _, wave = turn((klass + at) * (1.0 / 32.0))
    one = (32.0 + info_ref[0].astype(F32) + info_ref[1].astype(F32) * wave) * (1.0 / 4096.0)
    two = (32.0 + info_ref[2].astype(F32) + info_ref[3].astype(F32) * wave) * (1.0 / 4096.0)
    return one, two


def root_of(speed, first, second):
    a = speed[0] * first
    b = speed[1] * second
    return jnp.sqrt(1.0 + a * a + b * b)


LEVELS = ((1, 0), (2, 0), (1, 1), (2, 1))


def exact(x):
    high = x.astype(BF16)
    mid, low = split(x - high.astype(F32))
    return jnp.concatenate([high, mid, low], axis=0)


def spread(values, out_ref, columns):
    klass = iota((TGT * 4, 512), 0)
    lane = iota((TGT * 4, 512), 1)
    pick = jnp.where(klass == (lane // 16 + 2 * (lane % 16)) % TGT + TGT * columns, 1.0, 0.0).astype(BF16)
    moved = jnp.dot(values, pick, preferred_element_type=F32)
    rows = 2 * NODES
    out_ref[...] = moved[:rows] + moved[rows : 2 * rows] + moved[2 * rows :]


def tables_body(pair, info_ref, mix_first_ref, mix_second_ref, *rest):
    gamma_refs = [rest[-5 + k] for k in range(4)] if pair == 0 else [rest[-4 + k] for k in range(4)]
    index_x = info_ref[4]
    index_y = info_ref[5]
    z_first, z_second = node_columns((NODES, 128))
    lane = iota((1, 128), 1)
    klass = (lane % TGT).astype(F32)
    which = lane // TGT
    quads = [[], [], [], [], []]
    merged = [0, 0]
    for number, (along, level) in enumerate(LEVELS):
        before = list(merged)
        merged[along - 1] += 1
        if number // 2 != pair:
            continue
        old = [place(index_x, before[0]), place(index_y, before[1])]
        new = [place(index_x, merged[0]), place(index_y, merged[1])]
        index_d = index_x if along == 1 else index_y
        bit = (index_d >> level) & 1
        for who in range(2):
            side = bit if who == 0 else 1 - bit
            child_first = index_x >> before[0]
            child_second = index_y >> before[1]
            if along == 1:
                child_first = (index_x >> merged[0]) * 2 + side
            else:
                child_second = (index_y >> merged[1]) * 2 + side
            width_first = float(N // 8 * 2 ** before[0])
            width_second = float(N // 16 * 2 ** before[1])
            quads[0].append((child_first.astype(F32) * width_first, width_first))
            quads[1].append((child_second.astype(F32) * width_second, width_second))
            quads[2].append((old[0] + 2.0 * old[1], 0.0))
            quads[3].append((new[0] + 2.0 * new[1], 0.0))
            quads[4].append(((new[0] - old[0]) * (1.0 / 2048.0), (new[1] - old[1]) * (1.0 / 1024.0)))

    def lanes(values):
        out = jnp.zeros((1, 128), F32) + values[0]
        for k in range(1, 4):
            out = jnp.where(which == k, values[k], out)
        return out

    (first_at, first_width), (second_at, second_width), (old_at, _), (new_at, _), (move_first, move_second) = [
        (lanes([q[0] for q in quad]), lanes([q[1] for q in quad])) for quad in quads
    ]
    first = first_at + first_width * z_first
    second = second_at + second_width * z_second
    moved = first * move_first + second * move_second
    phase = root_of(speeds(info_ref, klass, new_at), first, second) - root_of(speeds(info_ref, klass, old_at), first, second)
    values = exact(jnp.concatenate(turn(phase + moved), axis=0))
    for k in range(4):
        spread(values, gamma_refs[k], k)
    if pair == 0:
        mix_ref = rest[-1]
        for number, (along, level) in enumerate(LEVELS):
            index_d = index_x if along == 1 else index_y
            mix_ref[number] = (mix_first_ref if along == 1 else mix_second_ref)[(index_d >> level) & 1]


def tables(info, pair, after=()):
    shapes = [jax.ShapeDtypeStruct((2 * NODES, 512), F32)] * 4
    if pair == 0:
        shapes.append(jax.ShapeDtypeStruct((4, 128, 256), BF16))
    return pl.pallas_call(
        functools.partial(tables_body, pair),
        out_shape=tuple(shapes),
        in_specs=[pl.BlockSpec(memory_space=pltpu.SMEM)] + vmem(2) + anywhere(len(after)),
        out_specs=vmem(len(shapes)),
        name="tables_%d" % pair,
        compiler_params=SMALL,
        cost_estimate=cost(0.8),
    )(info, jnp.asarray(merge_tables(1)), jnp.asarray(merge_tables(2)), *after)


def last_body(info_ref, *rest):
    last_ref, order_ref = rest[-2:]
    index_x = info_ref[4]
    index_y = info_ref[5]
    z_first, z_second = node_columns((NODES, 128))
    width_first = float(N // 8 * 4)
    width_second = float(N // 16 * 4)
    first = (index_x >> 2).astype(F32) * width_first + width_first * z_first
    second = (index_y >> 2).astype(F32) * width_second + width_second * z_second
    new = [place(index_x, 2), place(index_y, 2)]
    lane = iota((1, 128), 1)
    v = lane % 16
    for tile in range(4):
        u = tile * 8 + lane // 16
        klass = ((u + 2 * v) % TGT).astype(F32)
        root = root_of(speeds(info_ref, klass, new[0] + 2.0 * new[1]), first, second)
        root = root - jnp.floor(root)
        at_first = first * ((u.astype(F32) + new[0]) * (1.0 / 2048.0))
        at_first = at_first - jnp.floor(at_first) + root
        for half in range(2):
            at_second = second * ((v.astype(F32) + (16.0 * half + new[1])) * (1.0 / 1024.0))
            cosine, sine = turn(at_first + at_second)
            wide = slice(tile * 256 + half * 128, tile * 256 + half * 128 + 128)
            last_ref[:NODES, wide] = cosine
            last_ref[NODES:, wide] = sine
    source = iota((256, 256), 0)
    target = iota((256, 256), 1)
    wanted = ((target // 16) % 2) * 128 + (target // 32) * 16 + target % 16
    order_ref[...] = jnp.where(source == wanted, 1.0, 0.0).astype(BF16)


def last_tables(info, after):
    return pl.pallas_call(
        last_body,
        out_shape=(jax.ShapeDtypeStruct((2 * NODES, TARGETS), F32), jax.ShapeDtypeStruct((256, 256), BF16)),
        in_specs=[pl.BlockSpec(memory_space=pltpu.SMEM)] + anywhere(len(after)),
        out_specs=vmem(2),
        name="last",
        compiler_params=SMALL,
        cost_estimate=cost(0.8),
    )(info, *after)


def combined(start, group, left, own_ref, other_ref, gamma_refs):
    gcols = slice((start + group) * 128, (start + group) * 128 + 128)
    sides = [[], []]
    for half in range(2):
        cols = slice(group * 256 + half * 128, group * 256 + half * 128 + 128)
        reals, imags = [], []
        for gamma_ref, ref in zip(gamma_refs, (own_ref, other_ref)):
            gr = gamma_ref[:NODES, gcols]
            gi = gamma_ref[NODES:, gcols]
            xr = ref[:NODES, cols]
            xi = ref[NODES:, cols]
            reals.append(split(gr * xr - gi * xi))
            imags.append(split(gr * xi + gi * xr))
        for side, parts in zip(sides, (reals, imags)):
            side.append(jnp.concatenate([parts[0][0], parts[1][0], parts[0][1], parts[1][1]], axis=0))
    out = []
    for side in sides:
        both = jnp.dot(left, jnp.concatenate(side, axis=1), preferred_element_type=F32)
        out.append(both[:NODES] + both[NODES:])
    return out


def merge_body(number, chunk, own_ref, other_ref, gamma_own_ref, gamma_other_ref, mix_ref, *rest):
    start, groups = chunk
    out_ref = rest[-1]
    left = mix_ref[number]
    for group in range(groups):
        real, imag = combined(start, group, left, own_ref, other_ref, (gamma_own_ref, gamma_other_ref))
        cols = slice(group * 256, group * 256 + 256)
        out_ref[:NODES, cols] = real
        out_ref[NODES:, cols] = imag


def merge(number, chunk, own, other, gammas, mix, after=()):
    return pl.pallas_call(
        functools.partial(merge_body, number, chunk),
        out_shape=jax.ShapeDtypeStruct((2 * NODES, 256 * chunk[1]), F32),
        in_specs=vmem(5) + anywhere(len(after)),
        out_specs=vmem(1)[0],
        name="merge_%d_%d" % (number, chunk[0]),
        compiler_params=SMALL,
        cost_estimate=cost(0.2 + 0.2 * chunk[1]),
    )(own, other, *gammas, mix, *after)


def finish_body(chunk, own_ref, other_ref, gamma_own_ref, gamma_other_ref, mix_ref, last_ref, order_ref, *rest):
    start, groups = chunk
    out_ref, wide_ref, sem = rest[-3:]
    left = mix_ref[3]
    for group in range(groups):
        real, imag = combined(start, group, left, own_ref, other_ref, (gamma_own_ref, gamma_other_ref))
        tile = start + group
        cols = slice(tile * 256, tile * 256 + 256)
        cosine = last_ref[:NODES, cols]
        sine = last_ref[NODES:, cols]
        value = jnp.concatenate([cosine * real + sine * imag, cosine * imag - sine * real], axis=0)
        moved = jnp.dot(exact(value), order_ref[...], preferred_element_type=F32)
        moved = moved[:128] + moved[128:256] + moved[256:]
        wide_ref[0, :, group * 256 : group * 256 + 256] = moved[:NODES]
        wide_ref[1, :, group * 256 : group * 256 + 256] = moved[NODES:]
    copy = pltpu.make_async_copy(wide_ref, out_ref.at[:, :, start * 256 : (start + groups) * 256], sem)
    copy.start()
    copy.wait()


def finish(chunk, own, other, gammas, mix, lasts, sofar):
    args = [own, other, *gammas, mix, *lasts]
    specs = vmem(7)
    aliases = {}
    if sofar is not None:
        aliases = {len(args): 0}
        args.append(sofar)
        specs = specs + anywhere(1)
    return pl.pallas_call(
        functools.partial(finish_body, chunk),
        out_shape=jax.ShapeDtypeStruct((2, NODES, TARGETS), F32),
        in_specs=specs,
        out_specs=anywhere(1)[0],
        scratch_shapes=[pltpu.VMEM((2, NODES, 256 * chunk[1]), F32), pltpu.SemaphoreType.DMA],
        input_output_aliases=aliases,
        name="finish_%d" % chunk[0],
        compiler_params=SMALL,
        cost_estimate=cost(0.7 + 0.3 * chunk[1]),
    )(*args)


def swap(value, along, level):
    axis = "bx" if along == 1 else "by"
    return lax.ppermute(value, axis, [(i, i ^ 1 << level) for i in range(lax.axis_size(axis))])


def on_device(point_box, point_offset, point_value, coef):
    owners = lax.axis_size("bx") * lax.axis_size("by")
    place_on = jnp.stack([lax.axis_index("bx"), lax.axis_index("by")]).astype(jnp.int32)
    info = jnp.concatenate([coef, place_on])
    sent = pack(point_box.reshape(-1, 128), point_offset, point_value)
    arrived = lax.all_to_all(sent.reshape(owners, 1, -1), ("bx", "by"), split_axis=0, concat_axis=0, tiled=True)
    *gammas, mix = tables(info, 0)
    prepared = prepare(info, arrived.reshape(owners, -1), (mix,))
    leaf_a = leaf(CHUNKS[0], prepared, ())
    other = swap(leaf_a, *LEVELS[0])
    first = merge(0, CHUNKS[0], leaf_a, other, gammas[:2], mix)
    leaf_b = leaf(CHUNKS[1], prepared, (leaf_a,))
    gammas += tables(info, 1, (leaf_b,))
    second = merge(0, CHUNKS[1], leaf_b, swap(leaf_b, *LEVELS[0]), gammas[:2], mix, (gammas[4],))
    holding = [first, second]
    lasts = last_tables(info, (second,))
    for number in (1, 2):
        pair = gammas[2 * number : 2 * number + 2]
        holding = [merge(number, c, x, swap(x, *LEVELS[number]), pair, mix) for c, x in zip(CHUNKS, holding)]
    out = None
    for c, x in zip(CHUNKS, holding):
        out = finish(c, x, swap(x, *LEVELS[3]), gammas[6:], mix, lasts, out)
    return out


def solution(mesh):
    in_specs = (P(("bx", "by"), None), P(None, ("bx", "by")), P(None, ("bx", "by")), P())
    out_specs = P(None, None, ("bx", "by"))
    return jax.shard_map(on_device, mesh=mesh, in_specs=in_specs, out_specs=out_specs, check_vma=False)
```

time: 75 us -> 67.4 us (0.90)
  waiting for transfers between devices: 11.7 us -> 24.9 us
  Pallas kernels: 34.3 us -> 21.6 us
  starting transfers between devices: 27.6 us -> 17.8 us
  local copies, waits for them, and re-layouts: 0.01 us -> 1.82 us
    ppermute x16 -> x8, waiting for transfers between devices: 3.01 us -> 19.3 us  [swap(): lax.ppermute(value, axis, [(i, i ^ 1 << level) for i in range(lax.axis_si...]
    ppermute x16 -> x8, starting transfers between devices: 16.5 us -> 6.68 us  [swap(): lax.ppermute(value, axis, [(i, i ^ 1 << level) for i in range(lax.axis_si...]
    pallas_call x12 -> x6, Pallas kernels: 9 us -> 1.71 us  [merge(): pl.pallas_call(functools.partial(merge_body, number, chunk), out_shape=ja...]
    pallas_call x4 -> x2, Pallas kernels: 6.4 us -> 2.53 us  [finish(): pl.pallas_call(functools.partial(finish_body, chunk), out_shape=jax.Shape...]
    all_to_all x1, waiting for transfers between devices: 8.67 us -> 5.64 us  [on_device(): lax.all_to_all(sent.reshape(owners, 1, -1), ('bx', 'by'), split_axis=0, c...]
    unnamed x4 -> x8, local copies, waits for them, and re-layouts: 0.01 us -> 1.82 us
    pallas_call x4 -> x2, Pallas kernels: 9.74 us -> 8.87 us  [leaf(): pl.pallas_call(functools.partial(leaf_body, chunk), out_shape=jax.ShapeDt...]
    pallas_call x2 -> x3, Pallas kernels: 3.53 us -> 3.4 us  [the longest x2 2.44 us: tables(): pl.pallas_call(functools.partial(tables_body, pair), out_shape=tuple(shap...]
  transfers between devices with their start and end apart: 17 -> 9, of which waited for: 5 -> 7; matrix products, arithmetic and copies ran while one was open for 1% -> 1% of each run, Pallas kernels for 33% -> 16%
where the time goes in v4:
time: 67.4 us; the launch traced here: 67.1 us
  waiting for transfers between devices  24.9 us (37%)
  Pallas kernels  21.6 us (32%)
  starting transfers between devices  17.8 us (26%)
  local copies, waits for them, and re-layouts  1.82 us (3%)
  other arithmetic  0.73 us (1%)
    ppermute x8, waiting for transfers between devices, swap(): lax.ppermute(value, axis, [(i, i ^ 1 << level) for i in range(lax.axis_si...  19.3 us
    all_to_all x1, starting transfers between devices, on_device(): lax.all_to_all(sent.reshape(owners, 1, -1), ('bx', 'by'), split_axis=0, c...  11.1 us
    pallas_call x2, Pallas kernels, leaf(): pl.pallas_call(functools.partial(leaf_body, chunk), out_shape=jax.ShapeDt...  8.87 us
    ppermute x8, starting transfers between devices, swap(): lax.ppermute(value, axis, [(i, i ^ 1 << level) for i in range(lax.axis_si...  6.68 us
    all_to_all x1, waiting for transfers between devices, on_device(): lax.all_to_all(sent.reshape(owners, 1, -1), ('bx', 'by'), split_axis=0, c...  5.64 us
    pallas_call x1, Pallas kernels, prepare(): pl.pallas_call(prepare_body, out_shape=(jax.ShapeDtypeStruct((256, CAP *...  2.62 us
    pallas_call x2, Pallas kernels, finish(): pl.pallas_call(functools.partial(finish_body, chunk), out_shape=jax.Shape...  2.53 us
    pallas_call x2, Pallas kernels, tables(): pl.pallas_call(functools.partial(tables_body, pair), out_shape=tuple(shap...  2.44 us
  transfers between devices with their start and end apart: 9, of which 7 were waited for; matrix products, arithmetic and copies ran while one was open for 1% of the time, Pallas kernels for 16%

profile of v4, /device:TPU:0, one launch (start us, length us, event | category | flops | bytes accessed | tf_op | source)
XLA Modules:
  0.0 67.1 jit_solution(8879918530596695876)
XLA Ops:
  0.0 2.4 %pack.1 = f32[128,128]{1,0:T(8,128)} custom-call(s32[16,128]{1,0:T(8,128)} %bitcast.9, s32[2,2048]{1,0:T(2,128)} %off_ref.1, f32[2,2048]{1,0:T(2,128)} %val_ref.1), custom_call_target="tpu_custom_call" | custom-call | bytes 7400000 | tf_op jit(solution)/shard_map/pack/pallas_call | solution.py:138
  2.4 11.1 %all-to-all-start = ((f32[128,1,128]{2,1,0:T(1,128)}), f32[128,1,128]{2,1,0:T(1,128)S(1)}, u32[]{:S(2)}, u32[]{:S(2)}) async-start(f32[128,1,128]{2,1,0:T(1,128)} %bitcast.8), calls=%async_computation | async-start | bytes 131072 | tf_op jit(solution)/shard_map/all_to_all | solution.py:572
  13.6 0.7 %pad_add_fusion.info_ref = s32[6]{0:T(128)S(1)} fusion(s32[1]{0:T(128)} %bitcast.1, s32[1]{0:T(128)} %bitcast, s32[4]{0:T(128)} %param.11), kind=kLoop, calls=%fused_computation | loop fusion | flops 12 | bytes 48 | tf_op jit(solution)/shard_map/concatenate | solution.py:570
  14.3 0.0 copy-start
  14.3 0.9 %copy-done = bf16[2,128,256]{2,1,0:T(8,128)(2,1)S(1)} copy-done((bf16[2,128,256]{2,1,0:T(8,128)(2,1)S(1)}, bf16[2,128,256]{2,1,0:T(8,128)(2,1)}, u32[]{:S(2)}) %copy-start) | copy-done | bytes 131096
  15.2 0.0 copy-start.2
  15.2 0.9 %copy-done.2 = bf16[2,128,256]{2,1,0:T(8,128)(2,1)S(1)} copy-done((bf16[2,128,256]{2,1,0:T(8,128)(2,1)S(1)}, bf16[2,128,256]{2,1,0:T(8,128)(2,1)}, u32[]{:S(2)}) %copy-start.2) | copy-done | bytes 131096
  16.1 1.2 %tables_0.1 = (f32[128,512]{1,0:T(8,128)S(1)}, f32[128,512]{1,0:T(8,128)S(1)}, f32[128,512]{1,0:T(8,128)S(1)}, f32[128,512]{1,0:T(8,128)S(1)}, bf16[4,128,256]{2,1,0:T(8,128)(2,1)S(1)}) custom-call(s32[6]{0:T(128)S(1)} %pad_add_fusion.info_ref, bf16[2,128,256]{2,1,0:T(8,128)(2,1)S(1)} %copy-done.2, bf16[2,128,256]{2,1,0:T(8,128)(2,1)S(1)} %copy-done), custom_call_target="tpu_custom_call" | custom-call | bytes 2960000 | tf_op jit(solution)/shard_map/tables_0/pallas_call | solution.py:422
  17.4 5.6 %all-to-all-done = f32[128,1,128]{2,1,0:T(1,128)S(1)} async-done(((f32[128,1,128]{2,1,0:T(1,128)}), f32[128,1,128]{2,1,0:T(1,128)S(1)}, u32[]{:S(2)}, u32[]{:S(2)}) %all-to-all-start) | async-done | bytes 65568 | tf_op jit(solution)/shard_map/all_to_all | solution.py:572
  23.0 2.6 %prepare.1 = (bf16[256,4096]{1,0:T(8,128)(2,1)S(1)}, f32[32,4,32,128]{3,2,1,0:T(8,128)S(1)}, f32[32,2,16,128]{3,2,1,0:T(8,128)S(1)}) custom-call(s32[6]{0:T(128)S(1)} %pad_add_fusion.info_ref, f32[128,128]{1,0:T(8,128)S(1)} %bitcast.7, bf16[4,128,256]{2,1,0:T(8,128)(2,1)S(1)} %get-tuple-element.19.rest_0_.mix_ref), custom_call_target="tpu_custom_call" | custom-call | bytes 7400000 | tf_op jit(solution)/shard_map/prepare/pallas_call | solution.py:227
  25.6 4.4 %leaf_0.1.rest_0_.own_ref = f32[128,512]{1,0:T(8,128)S(1)} custom-call(bf16[256,4096]{1,0:T(8,128)(2,1)S(1)} %get-tuple-element.20.l_ref, f32[32,4,32,128]{3,2,1,0:T(8,128)S(1)} %get-tuple-element.21.q_ref, f32[32,2,16,128]{3,2,1,0:T(8,128)S(1)} %get-tuple-element.22.z_ref), custom_call_target="tpu_custom_call" | custom-call | bytes 17020000 | tf_op jit(solution)/shard_map/leaf_0/pallas_call | solution.py:295
  30.1 0.0 copy-start.1
  30.1 0.0 copy-start.3
  30.1 0.1 collective-permute-start.4
  30.2 4.4 %leaf_2.1.rest_0_.own_ref = f32[128,512]{1,0:T(8,128)S(1)} custom-call(bf16[256,4096]{1,0:T(8,128)(2,1)S(1)} %get-tuple-element.20.l_ref, f32[32,4,32,128]{3,2,1,0:T(8,128)S(1)} %get-tuple-element.21.q_ref, f32[32,2,16,128]{3,2,1,0:T(8,128)S(1)} %get-tuple-element.22.z_ref, f32[128,512]{1,0:T(8,128)S(1)} %leaf_0.1.rest_0_.own_ref), custom_call_target="tpu_custom_call" | custom-call | bytes 17020000 | tf_op jit(solution)/shard_map/leaf_2/pallas_call | solution.py:295
  34.6 0.6 collective-permute-start
  35.2 0.0 collective-permute-done.4.other_ref
  35.2 0.3 merge_0_0.1.own_ref
  35.5 0.8 %collective-permute-start.5 = (f32[128,512]{1,0:T(8,128)S(1)}, f32[128,512]{1,0:T(8,128)S(1)}, u32[]{:S(2)}, u32[]{:S(2)}) collective-permute-start(f32[128,512]{1,0:T(8,128)S(1)} %merge_0_0.1.own_ref), channel_id=1, source_target_pairs={{0,1},{1,0},{2,3},{3,2},{4,5},{5,4},{6,7},{7,6},{8,9},{9,8},{10,11... | collective-permute-start | bytes 786440 | tf_op jit(solution)/shard_map/ppermute | solution.py:564
  36.3 0.0 copy-done.1
  36.3 0.0 copy-done.3
  36.4 1.2 %tables_1.1 = (f32[128,512]{1,0:T(8,128)S(1)}, f32[128,512]{1,0:T(8,128)S(1)}, f32[128,512]{1,0:T(8,128)S(1)}, f32[128,512]{1,0:T(8,128)S(1)}) custom-call(s32[6]{0:T(128)S(1)} %pad_add_fusion.info_ref, bf16[2,128,256]{2,1,0:T(8,128)(2,1)S(1)} %copy-done.3, bf16[2,128,256]{2,1,0:T(8,128)(2,1)S(1)} %copy-done.1, f32[128,512]{1,0:T(8,128)S(1)} %leaf_2.1.rest_0_.own_ref), custom_call_target="tpu_custom_call" | custom-call | bytes 2960000 | tf_op jit(solution)/shard_map/tables_1/pallas_call | solution.py:422
  37.6 0.0 collective-permute-done.other_ref
  37.6 0.3 merge_0_2.1.own_ref.rest_0_
  37.9 1.5 %collective-permute-start.1 = (f32[128,512]{1,0:T(8,128)S(1)}, f32[128,512]{1,0:T(8,128)S(1)}, u32[]{:S(2)}, u32[]{:S(2)}) collective-permute-start(f32[128,512]{1,0:T(8,128)S(1)} %merge_0_2.1.own_ref.rest_0_), channel_id=1, source_target_pairs={{0,1},{1,0},{2,3},{3,2},{4,5},{5,4},{6,7},{7,6},{8,9},{9,8},{10,11... | collective-permute-start | bytes 786440 | tf_op jit(solution)/shard_map/ppermute | solution.py:564
  39.4 5.5 %collective-permute-done.5.other_ref = f32[128,512]{1,0:T(8,128)S(1)} collective-permute-done((f32[128,512]{1,0:T(8,128)S(1)}, f32[128,512]{1,0:T(8,128)S(1)}, u32[]{:S(2)}, u32[]{:S(2)}) %collective-permute-start.5) | collective-permute-done | bytes 262176 | tf_op jit(solution)/shard_map/ppermute | solution.py:564
  44.9 0.3 merge_1_0.1.own_ref
  45.2 0.7 %collective-permute-start.6 = (f32[128,512]{1,0:T(8,128)S(1)}, f32[128,512]{1,0:T(8,128)S(1)}, u32[]{:S(2)}, u32[]{:S(2)}) collective-permute-start(f32[128,512]{1,0:T(8,128)S(1)} %merge_1_0.1.own_ref), channel_id=1, source_target_pairs={{0,32},{16,48},{32,0},{48,16},{64,96},{80,112},{96,64},{112,80},{1... | collective-permute-start | bytes 786440 | tf_op jit(solution)/shard_map/ppermute | solution.py:564
  45.9 3.7 %collective-permute-done.1.other_ref = f32[128,512]{1,0:T(8,128)S(1)} collective-permute-done((f32[128,512]{1,0:T(8,128)S(1)}, f32[128,512]{1,0:T(8,128)S(1)}, u32[]{:S(2)}, u32[]{:S(2)}) %collective-permute-start.1) | collective-permute-done | bytes 262176 | tf_op jit(solution)/shard_map/ppermute | solution.py:564
  49.6 0.3 merge_1_2.1.own_ref
  49.9 0.7 %collective-permute-start.2 = (f32[128,512]{1,0:T(8,128)S(1)}, f32[128,512]{1,0:T(8,128)S(1)}, u32[]{:S(2)}, u32[]{:S(2)}) collective-permute-start(f32[128,512]{1,0:T(8,128)S(1)} %merge_1_2.1.own_ref), channel_id=1, source_target_pairs={{0,32},{16,48},{32,0},{48,16},{64,96},{80,112},{96,64},{112,80},{1... | collective-permute-start | bytes 786440 | tf_op jit(solution)/shard_map/ppermute | solution.py:564
  50.6 1.1 %collective-permute-done.6.other_ref = f32[128,512]{1,0:T(8,128)S(1)} collective-permute-done((f32[128,512]{1,0:T(8,128)S(1)}, f32[128,512]{1,0:T(8,128)S(1)}, u32[]{:S(2)}, u32[]{:S(2)}) %collective-permute-start.6) | collective-permute-done | bytes 262176 | tf_op jit(solution)/shard_map/ppermute | solution.py:564
  51.8 0.3 merge_2_0.1.own_ref
  52.0 1.1 %collective-permute-start.7 = (f32[128,512]{1,0:T(8,128)S(1)}, f32[128,512]{1,0:T(8,128)S(1)}, u32[]{:S(2)}, u32[]{:S(2)}) collective-permute-start(f32[128,512]{1,0:T(8,128)S(1)} %merge_2_0.1.own_ref), channel_id=1, source_target_pairs={{0,2},{1,3},{2,0},{3,1},{4,6},{5,7},{6,4},{7,5},{8,10},{9,11},{10,... | collective-permute-start | bytes 786440 | tf_op jit(solution)/shard_map/ppermute | solution.py:564
  53.2 4.2 %collective-permute-done.2.other_ref = f32[128,512]{1,0:T(8,128)S(1)} collective-permute-done((f32[128,512]{1,0:T(8,128)S(1)}, f32[128,512]{1,0:T(8,128)S(1)}, u32[]{:S(2)}, u32[]{:S(2)}) %collective-permute-start.2) | collective-permute-done | bytes 262176 | tf_op jit(solution)/shard_map/ppermute | solution.py:564
  57.4 0.3 merge_2_2.1.own_ref
  57.7 1.1 %collective-permute-start.3 = (f32[128,512]{1,0:T(8,128)S(1)}, f32[128,512]{1,0:T(8,128)S(1)}, u32[]{:S(2)}, u32[]{:S(2)}) collective-permute-start(f32[128,512]{1,0:T(8,128)S(1)} %merge_2_2.1.own_ref), channel_id=1, source_target_pairs={{0,2},{1,3},{2,0},{3,1},{4,6},{5,7},{6,4},{7,5},{8,10},{9,11},{10,... | collective-permute-start | bytes 786440 | tf_op jit(solution)/shard_map/ppermute | solution.py:564
  58.8 1.0 %last.1 = (f32[128,1024]{1,0:T(8,128)S(1)}, bf16[256,256]{1,0:T(8,128)(2,1)S(1)}) custom-call(s32[6]{0:T(128)S(1)} %pad_add_fusion.info_ref, f32[128,512]{1,0:T(8,128)S(1)} %merge_0_2.1.own_ref.rest_0_), custom_call_target="tpu_custom_call" | custom-call | bytes 2960000 | tf_op jit(solution)/shard_map/last/pallas_call | solution.py:465
  59.8 0.2 collective-permute-done.7.other_ref
  60.0 1.3 %finish_0.1.rest_0_ = f32[2,64,1024]{2,1,0:T(8,128)} custom-call(f32[128,512]{1,0:T(8,128)S(1)} %merge_2_0.1.own_ref, f32[128,512]{1,0:T(8,128)S(1)} %collective-permute-done.7.other_ref, f32[128,512]{1,0:T(8,128)S(1)} %get-tuple-element.29.gamma_own_ref, f32[128,512]{1,0:T(8,128)S(1)} %get-tuple-element.30.gamma_other_ref, ...), custom_call_target="tpu_custom_call" | custom-call | bytes 4809999 | tf_op jit(solution)/shard_map/finish_0/pallas_call | solution.py:549
  61.3 4.4 %collective-permute-done.3.other_ref = f32[128,512]{1,0:T(8,128)S(1)} collective-permute-done((f32[128,512]{1,0:T(8,128)S(1)}, f32[128,512]{1,0:T(8,128)S(1)}, u32[]{:S(2)}, u32[]{:S(2)}) %collective-permute-start.3) | collective-permute-done | bytes 262176 | tf_op jit(solution)/shard_map/ppermute | solution.py:564
  65.7 1.3 %finish_2.1 = f32[2,64,1024]{2,1,0:T(8,128)} custom-call(f32[128,512]{1,0:T(8,128)S(1)} %merge_2_2.1.own_ref, f32[128,512]{1,0:T(8,128)S(1)} %collective-permute-done.3.other_ref, f32[128,512]{1,0:T(8,128)S(1)} %get-tuple-element.29.gamma_own_ref, f32[128,512]{1,0:T(8,128)S(1)} %get-tuple-element.30.gamma_other_ref, ...), custom_call_target="tpu_custom_call", output_to_operand_aliasing={{}: (7, {})} | custom-call | bytes 4809999 | tf_op jit(solution)/shard_map/finish_2/pallas_call | solution.py:549
Async XLA Ops:
  2.4 20.6 %all-to-all-start = ((f32[128,1,128]{2,1,0:T(1,128)}), f32[128,1,128]{2,1,0:T(1,128)S(1)}, u32[]{:S(2)}, u32[]{:S(2)}) async-start(f32[128,1,128]{2,1,0:T(1,128)} %bitcast.8), calls=%async_computation | async-start | bytes 131072 | tf_op jit(solution)/shard_map/all_to_all | solution.py:572
  14.3 0.9 %copy-start = (bf16[2,128,256]{2,1,0:T(8,128)(2,1)S(1)}, bf16[2,128,256]{2,1,0:T(8,128)(2,1)}, u32[]{:S(2)}) copy-start(bf16[2,128,256]{2,1,0:T(8,128)(2,1)} %constant.14.clone.mix_second_ref) | copy-start | bytes 393220
  15.2 0.9 %copy-start.2 = (bf16[2,128,256]{2,1,0:T(8,128)(2,1)S(1)}, bf16[2,128,256]{2,1,0:T(8,128)(2,1)}, u32[]{:S(2)}) copy-start(bf16[2,128,256]{2,1,0:T(8,128)(2,1)} %constant.13.clone.mix_first_ref) | copy-start | bytes 393220
  30.1 6.3 %copy-start.1 = (bf16[2,128,256]{2,1,0:T(8,128)(2,1)S(1)}, bf16[2,128,256]{2,1,0:T(8,128)(2,1)}, u32[]{:S(2)}) copy-start(bf16[2,128,256]{2,1,0:T(8,128)(2,1)} %constant.14.clone.mix_second_ref) | copy-start | bytes 393220
  30.1 6.3 %copy-start.3 = (bf16[2,128,256]{2,1,0:T(8,128)(2,1)S(1)}, bf16[2,128,256]{2,1,0:T(8,128)(2,1)}, u32[]{:S(2)}) copy-start(bf16[2,128,256]{2,1,0:T(8,128)(2,1)} %constant.13.clone.mix_first_ref) | copy-start | bytes 393220
  30.1 5.1 %collective-permute-start.4 = (f32[128,512]{1,0:T(8,128)S(1)}, f32[128,512]{1,0:T(8,128)S(1)}, u32[]{:S(2)}, u32[]{:S(2)}) collective-permute-start(f32[128,512]{1,0:T(8,128)S(1)} %leaf_0.1.rest_0_.own_ref), channel_id=1, source_target_pairs={{0,16},{16,0},{32,48},{48,32},{64,80},{80,64},{96,112},{112,96},{1... | collective-permute-start | bytes 786440 | tf_op jit(solution)/shard_map/ppermute | solution.py:564
  34.6 2.9 %collective-permute-start = (f32[128,512]{1,0:T(8,128)S(1)}, f32[128,512]{1,0:T(8,128)S(1)}, u32[]{:S(2)}, u32[]{:S(2)}) collective-permute-start(f32[128,512]{1,0:T(8,128)S(1)} %leaf_2.1.rest_0_.own_ref), channel_id=1, source_target_pairs={{0,16},{16,0},{32,48},{48,32},{64,80},{80,64},{96,112},{112,96},{1... | collective-permute-start | bytes 786440 | tf_op jit(solution)/shard_map/ppermute | solution.py:564
  35.5 9.4 %collective-permute-start.5 = (f32[128,512]{1,0:T(8,128)S(1)}, f32[128,512]{1,0:T(8,128)S(1)}, u32[]{:S(2)}, u32[]{:S(2)}) collective-permute-start(f32[128,512]{1,0:T(8,128)S(1)} %merge_0_0.1.own_ref), channel_id=1, source_target_pairs={{0,1},{1,0},{2,3},{3,2},{4,5},{5,4},{6,7},{7,6},{8,9},{9,8},{10,11... | collective-permute-start | bytes 786440 | tf_op jit(solution)/shard_map/ppermute | solution.py:564
  37.9 11.7 %collective-permute-start.1 = (f32[128,512]{1,0:T(8,128)S(1)}, f32[128,512]{1,0:T(8,128)S(1)}, u32[]{:S(2)}, u32[]{:S(2)}) collective-permute-start(f32[128,512]{1,0:T(8,128)S(1)} %merge_0_2.1.own_ref.rest_0_), channel_id=1, source_target_pairs={{0,1},{1,0},{2,3},{3,2},{4,5},{5,4},{6,7},{7,6},{8,9},{9,8},{10,11... | collective-permute-start | bytes 786440 | tf_op jit(solution)/shard_map/ppermute | solution.py:564
  45.2 6.5 %collective-permute-start.6 = (f32[128,512]{1,0:T(8,128)S(1)}, f32[128,512]{1,0:T(8,128)S(1)}, u32[]{:S(2)}, u32[]{:S(2)}) collective-permute-start(f32[128,512]{1,0:T(8,128)S(1)} %merge_1_0.1.own_ref), channel_id=1, source_target_pairs={{0,32},{16,48},{32,0},{48,16},{64,96},{80,112},{96,64},{112,80},{1... | collective-permute-start | bytes 786440 | tf_op jit(solution)/shard_map/ppermute | solution.py:564
  49.9 7.5 %collective-permute-start.2 = (f32[128,512]{1,0:T(8,128)S(1)}, f32[128,512]{1,0:T(8,128)S(1)}, u32[]{:S(2)}, u32[]{:S(2)}) collective-permute-start(f32[128,512]{1,0:T(8,128)S(1)} %merge_1_2.1.own_ref), channel_id=1, source_target_pairs={{0,32},{16,48},{32,0},{48,16},{64,96},{80,112},{96,64},{112,80},{1... | collective-permute-start | bytes 786440 | tf_op jit(solution)/shard_map/ppermute | solution.py:564
  52.0 8.0 %collective-permute-start.7 = (f32[128,512]{1,0:T(8,128)S(1)}, f32[128,512]{1,0:T(8,128)S(1)}, u32[]{:S(2)}, u32[]{:S(2)}) collective-permute-start(f32[128,512]{1,0:T(8,128)S(1)} %merge_2_0.1.own_ref), channel_id=1, source_target_pairs={{0,2},{1,3},{2,0},{3,1},{4,6},{5,7},{6,4},{7,5},{8,10},{9,11},{10,... | collective-permute-start | bytes 786440 | tf_op jit(solution)/shard_map/ppermute | solution.py:564
  57.7 8.0 %collective-permute-start.3 = (f32[128,512]{1,0:T(8,128)S(1)}, f32[128,512]{1,0:T(8,128)S(1)}, u32[]{:S(2)}, u32[]{:S(2)}) collective-permute-start(f32[128,512]{1,0:T(8,128)S(1)} %merge_2_2.1.own_ref), channel_id=1, source_target_pairs={{0,2},{1,3},{2,0},{3,1},{4,6},{5,7},{6,4},{7,5},{8,10},{9,11},{10,... | collective-permute-start | bytes 786440 | tf_op jit(solution)/shard_map/ppermute | solution.py:564

commit v5 on v4

--- a/solution.py
+++ b/solution.py
@@ -13,7 +13,7 @@
 ORDER = 8
 TGT = 32
 CAP = 32
-CHUNKS = ((0, 2), (2, 2))
+CHUNKS = ((0, 1), (1, 1), (2, 1), (3, 1))
 STEP = 8
 NODES = ORDER * ORDER
 TARGETS = TGT * TGT
@@ -27,36 +27,6 @@
 def node_table():
     counting = np.arange(ORDER) * 1.0
     return 0.5 - 0.5 * np.cos(np.pi * (2.0 * counting + 1.0) / (2.0 * ORDER))
-
-
-def child_matrix(side):
-    nodes = node_table()
-    points = 0.5 * (side + nodes)
-    rows = []
-    for target in range(ORDER):
-        factor = np.ones(ORDER)
-        for source in range(ORDER):
-            if source != target:
-                factor = factor * (points - nodes[source]) / (nodes[target] - nodes[source])
-        rows.append(factor)
-    return np.stack(rows)
-
-
-def merge_tables(along):
-    eye = np.eye(ORDER)
-    both = []
-    for bit in range(2):
-        parts = []
-        for side in (bit, 1 - bit):
-            matrix = child_matrix(side)
-            parts.append(np.kron(matrix, eye) if along == 1 else np.kron(eye, matrix))
-        full = np.concatenate(parts, axis=1)
-        high = full.astype(np.float32).astype(BF16)
-        low = (full - high.astype(np.float64)).astype(np.float32).astype(BF16)
-        top = np.concatenate([high, high], axis=1)
-        bottom = np.concatenate([low, np.zeros_like(low)], axis=1)
-        both.append(np.concatenate([top, bottom], axis=0))
-    return np.stack(both)
 
 
 def horner(coefs, x):
@@ -161,18 +131,16 @@
     return total
 
 
-def prepare_body(info_ref, rx_ref, *rest):
+def prepare_body(rx_ref, speed_ref, *rest):
     l_ref, q_ref, z_ref, xt_ref, trig_ref = rest[-5:]
     width_first, width_second = float(N // 8), float(N // 16)
-    corner_first = info_ref[4].astype(F32) * width_first
-    corner_second = info_ref[5].astype(F32) * width_second
+    corner_first = lax.axis_index("bx").astype(F32) * width_first
+    corner_second = lax.axis_index("by").astype(F32) * width_second
     xt_ref[...] = rx_ref[...].T
 
     order = iota((TGT, 128), 0)
-    klass = (order % 16) * 2 + order // 16
-    _, wave = turn((klass.astype(F32) + 1.5) * (1.0 / 32.0))
-    speed_first = (32.0 + info_ref[0].astype(F32) + info_ref[1].astype(F32) * wave) * (1.0 / 4096.0)
-    speed_second = (32.0 + info_ref[2].astype(F32) + info_ref[3].astype(F32) * wave) * (1.0 / 4096.0)
+    speed_first = speed_ref[0]
+    speed_second = speed_ref[1]
     lin_first = (order // 16 * 2 + 1).astype(F32) * (1.0 / 4096.0)
     lin_second = (order % 16 * 4 + 34).astype(F32) * (1.0 / 4096.0)
     power = iota((16, 128), 0).astype(F32) * (1.0 / 1024.0)
@@ -223,7 +191,7 @@
                 l_ref[128 + base : 128 + base + 16, cols] = low
 
 
-def prepare(info, arrived, after):
+def prepare(arrived, speed):
     return pl.pallas_call(
         prepare_body,
         out_shape=(
@@ -231,13 +199,13 @@
             jax.ShapeDtypeStruct((CAP, 4, TGT, 128), F32),
             jax.ShapeDtypeStruct((CAP, 2, 16, 128), F32),
         ),
-        in_specs=[pl.BlockSpec(memory_space=pltpu.SMEM)] + vmem(1) + anywhere(len(after)),
+        in_specs=vmem(2),
         out_specs=vmem(3),
         scratch_shapes=[pltpu.VMEM((128, 128), F32), pltpu.VMEM((4, CAP, 128), F32)],
         name="prepare",
         compiler_params=SMALL,
         cost_estimate=cost(2.0),
-    )(info, arrived, *after)
+    )(arrived, speed)
 
 
 def leaf_body(chunk, l_ref, q_ref, z_ref, *rest):
@@ -357,10 +325,37 @@
     out_ref[...] = moved[:rows] + moved[rows : 2 * rows] + moved[2 * rows :]
 
 
-def tables_body(pair, info_ref, mix_first_ref, mix_second_ref, *rest):
-    gamma_refs = [rest[-5 + k] for k in range(4)] if pair == 0 else [rest[-4 + k] for k in range(4)]
-    index_x = info_ref[4]
-    index_y = info_ref[5]
+def mix_of(number):
+    along, level = LEVELS[number]
+    bit = (lax.axis_index("bx" if along == 1 else "by") >> level) & 1
+    nodes = node_table()
+    lane = iota((1, 128), 1)
+    who = lane // NODES
+    first = lane // ORDER % ORDER
+    second = lane % ORDER
+    source = first if along == 1 else second
+    at = jnp.zeros((1, 128), F32)
+    for t in range(ORDER):
+        at = jnp.where(source == t, float(nodes[t]), at)
+    side = jnp.where(who == 0, bit, 1 - bit).astype(F32)
+    rows = basis_rows((at + side) * 0.5)
+    row = iota((ORDER, 128), 0)
+    full = []
+    for t in range(ORDER):
+        if along == 1:
+            full.append(jnp.where(row == second, rows[t : t + 1], 0.0))
+        else:
+            full.append(jnp.where(first == t, rows, 0.0))
+    high, low = split(jnp.concatenate(full, axis=0))
+    top = jnp.concatenate([high, high], axis=1)
+    bottom = jnp.concatenate([low, jnp.zeros_like(low)], axis=1)
+    return jnp.concatenate([top, bottom], axis=0)
+
+
+def tables_body(pair, info_ref, *rest):
+    gamma_refs = [rest[-6 + k] for k in range(4)] if pair == 0 else [rest[-4 + k] for k in range(4)]
+    index_x = lax.axis_index("bx")
+    index_y = lax.axis_index("by")
     z_first, z_second = node_columns((NODES, 128))
     lane = iota((1, 128), 1)
     klass = (lane % TGT).astype(F32)
@@ -409,31 +404,38 @@
     for k in range(4):
         spread(values, gamma_refs[k], k)
     if pair == 0:
-        mix_ref = rest[-1]
-        for number, (along, level) in enumerate(LEVELS):
-            index_d = index_x if along == 1 else index_y
-            mix_ref[number] = (mix_first_ref if along == 1 else mix_second_ref)[(index_d >> level) & 1]
+        mix_ref, speed_ref = rest[-2:]
+        order = iota((TGT, 128), 0)
+        klass = (order % 16) * 2 + order // 16
+        _, wave = turn((klass.astype(F32) + 1.5) * (1.0 / 32.0))
+        speed_first = (32.0 + info_ref[0].astype(F32) + info_ref[1].astype(F32) * wave) * (1.0 / 4096.0)
+        speed_second = (32.0 + info_ref[2].astype(F32) + info_ref[3].astype(F32) * wave) * (1.0 / 4096.0)
+        speed_ref[0] = speed_first
+        speed_ref[1] = speed_second
+        for number in range(4):
+            mix_ref[number] = mix_of(number)
 
 
 def tables(info, pair, after=()):
     shapes = [jax.ShapeDtypeStruct((2 * NODES, 512), F32)] * 4
     if pair == 0:
         shapes.append(jax.ShapeDtypeStruct((4, 128, 256), BF16))
+        shapes.append(jax.ShapeDtypeStruct((2, TGT, 128), F32))
     return pl.pallas_call(
         functools.partial(tables_body, pair),
         out_shape=tuple(shapes),
-        in_specs=[pl.BlockSpec(memory_space=pltpu.SMEM)] + vmem(2) + anywhere(len(after)),
+        in_specs=[pl.BlockSpec(memory_space=pltpu.SMEM)] + anywhere(len(after)),
         out_specs=vmem(len(shapes)),
         name="tables_%d" % pair,
         compiler_params=SMALL,
         cost_estimate=cost(0.8),
-    )(info, jnp.asarray(merge_tables(1)), jnp.asarray(merge_tables(2)), *after)
+    )(info, *after)
 
 
 def last_body(info_ref, *rest):
     last_ref, order_ref = rest[-2:]
-    index_x = info_ref[4]
-    index_y = info_ref[5]
+    index_x = lax.axis_index("bx")
+    index_y = lax.axis_index("by")
     z_first, z_second = node_columns((NODES, 128))
     width_first = float(N // 8 * 4)
     width_second = float(N // 16 * 4)
@@ -566,23 +568,36 @@
 
 def on_device(point_box, point_offset, point_value, coef):
     owners = lax.axis_size("bx") * lax.axis_size("by")
-    place_on = jnp.stack([lax.axis_index("bx"), lax.axis_index("by")]).astype(jnp.int32)
-    info = jnp.concatenate([coef, place_on])
+    info = coef
     sent = pack(point_box.reshape(-1, 128), point_offset, point_value)
     arrived = lax.all_to_all(sent.reshape(owners, 1, -1), ("bx", "by"), split_axis=0, concat_axis=0, tiled=True)
-    *gammas, mix = tables(info, 0)
-    prepared = prepare(info, arrived.reshape(owners, -1), (mix,))
-    leaf_a = leaf(CHUNKS[0], prepared, ())
-    other = swap(leaf_a, *LEVELS[0])
-    first = merge(0, CHUNKS[0], leaf_a, other, gammas[:2], mix)
-    leaf_b = leaf(CHUNKS[1], prepared, (leaf_a,))
-    gammas += tables(info, 1, (leaf_b,))
-    second = merge(0, CHUNKS[1], leaf_b, swap(leaf_b, *LEVELS[0]), gammas[:2], mix, (gammas[4],))
-    holding = [first, second]
-    lasts = last_tables(info, (second,))
-    for number in (1, 2):
-        pair = gammas[2 * number : 2 * number + 2]
-        holding = [merge(number, c, x, swap(x, *LEVELS[number]), pair, mix) for c, x in zip(CHUNKS, holding)]
+    *gammas, mix, speed = tables(info, 0)
+    prepared = prepare(arrived.reshape(owners, -1), speed)
+
+    def exchange(number, c, x):
+        return swap(x, *LEVELS[number])
+
+    def join(number, c, x, y, after=()):
+        return merge(number, c, x, y, gammas[2 * number : 2 * number + 2], mix, after)
+
+    c0, c1, c2, c3 = CHUNKS
+    leaf0 = leaf(c0, prepared, ())
+    leaf1 = leaf(c1, prepared, (leaf0,))
+    one0 = join(0, c0, leaf0, exchange(0, c0, leaf0))
+    leaf2 = leaf(c2, prepared, (one0,))
+    one1 = join(0, c1, leaf1, exchange(0, c1, leaf1))
+    got0 = exchange(1, c0, one0)
+    leaf3 = leaf(c3, prepared, (one1, got0))
+    one2 = join(0, c2, leaf2, exchange(0, c2, leaf2))
+    got1 = exchange(1, c1, one1)
+    gammas += tables(info, 1, (leaf3, got1))
+    one3 = join(0, c3, leaf3, exchange(0, c3, leaf3), (gammas[4],))
+    ones = [one0, one1, one2, one3]
+    lasts = last_tables(info, (one0,))
+    swapped = [got0, got1, exchange(1, c2, one2), exchange(1, c3, one3)]
+
+    late = [join(1, c, x, y) for c, x, y in zip(CHUNKS, ones, swapped)]
+    holding = [join(2, c, x, exchange(2, c, x)) for c, x in zip(CHUNKS, late)]
     out = None
     for c, x in zip(CHUNKS, holding):
         out = finish(c, x, swap(x, *LEVELS[3]), gammas[6:], mix, lasts, out)

time: 67.4 us -> 65.6 us (0.973)
  waiting for transfers between devices: 24.9 us -> 13.8 us
  starting transfers between devices: 17.8 us -> 25.9 us
  Pallas kernels: 21.6 us -> 24.5 us
  local copies, waits for them, and re-layouts: 1.82 us -> 0.66 us
  other arithmetic: 0.73 us -> 0 us
    ppermute x8 -> x16, waiting for transfers between devices: 19.3 us -> 6.31 us  [swap(): lax.ppermute(value, axis, [(i, i ^ 1 << level) for i in range(lax.axis_si...]
    ppermute x8 -> x16, starting transfers between devices: 6.68 us -> 14.8 us  [swap(): lax.ppermute(value, axis, [(i, i ^ 1 << level) for i in range(lax.axis_si...]
    all_to_all x1, waiting for transfers between devices: 5.64 us -> 7.44 us  [on_device(): lax.all_to_all(sent.reshape(owners, 1, -1), ('bx', 'by'), split_axis=0, c...]
    pallas_call x2 -> x4, Pallas kernels: 2.53 us -> 4.27 us  [finish(): pl.pallas_call(functools.partial(finish_body, chunk), out_shape=jax.Shape...]
    unnamed x8 -> x4, local copies, waits for them, and re-layouts: 1.82 us -> 0.66 us
    pallas_call x6 -> x12, Pallas kernels: 1.71 us -> 2.56 us  [merge(): pl.pallas_call(functools.partial(merge_body, number, chunk), out_shape=ja...]
    pallas_call x2 -> x4, Pallas kernels: 8.87 us -> 9.71 us  [leaf(): pl.pallas_call(functools.partial(leaf_body, chunk), out_shape=jax.ShapeDt...]
    concatenate x1 -> x0, other arithmetic: 0.73 us -> none  [on_device(): info = jnp.concatenate([coef, place_on])]
  transfers between devices with their start and end apart: 9 -> 17, of which waited for: 7 -> 8; matrix products, arithmetic and copies ran while one was open for 1% -> 0% of each run, Pallas kernels for 16% -> 25%
where the time goes in v5:
time: 65.6 us; the launch traced here: 65.3 us
  starting transfers between devices  25.9 us (39%)
  Pallas kernels  24.5 us (37%)
  waiting for transfers between devices  13.8 us (21%)
  local copies, waits for them, and re-layouts  0.66 us (1%)
    ppermute x16, starting transfers between devices, swap(): lax.ppermute(value, axis, [(i, i ^ 1 << level) for i in range(lax.axis_si...  14.8 us
    all_to_all x1, starting transfers between devices, on_device(): lax.all_to_all(sent.reshape(owners, 1, -1), ('bx', 'by'), split_axis=0, c...  11.1 us
    pallas_call x4, Pallas kernels, leaf(): pl.pallas_call(functools.partial(leaf_body, chunk), out_shape=jax.ShapeDt...  9.71 us
    all_to_all x1, waiting for transfers between devices, on_device(): lax.all_to_all(sent.reshape(owners, 1, -1), ('bx', 'by'), split_axis=0, c...  7.44 us
    ppermute x16, waiting for transfers between devices, swap(): lax.ppermute(value, axis, [(i, i ^ 1 << level) for i in range(lax.axis_si...  6.31 us
    pallas_call x4, Pallas kernels, finish(): pl.pallas_call(functools.partial(finish_body, chunk), out_shape=jax.Shape...  4.27 us
    pallas_call x12, Pallas kernels, merge(): pl.pallas_call(functools.partial(merge_body, number, chunk), out_shape=ja...  2.56 us
    pallas_call x2, Pallas kernels, tables(): pl.pallas_call(functools.partial(tables_body, pair), out_shape=tuple(shap...  2.52 us
  transfers between devices with their start and end apart: 17, of which 8 were waited for; matrix products, arithmetic and copies ran while one was open for 0% of the time, Pallas kernels for 25%

profile of v5, /device:TPU:0, one launch (start us, length us, event | category | flops | bytes accessed | tf_op | source)
XLA Modules:
  0.0 65.3 jit_solution(17497192323356000566)
XLA Ops:
  0.0 2.4 %pack.1 = f32[128,128]{1,0:T(8,128)} custom-call(s32[16,128]{1,0:T(8,128)} %bitcast.7, s32[2,2048]{1,0:T(2,128)} %off_ref.1, f32[2,2048]{1,0:T(2,128)} %val_ref.1), custom_call_target="tpu_custom_call" | custom-call | bytes 7400000 | tf_op jit(solution)/shard_map/pack/pallas_call | solution.py:108
  2.4 11.1 %all-to-all-start = ((f32[128,1,128]{2,1,0:T(1,128)}), f32[128,1,128]{2,1,0:T(1,128)S(1)}, u32[]{:S(2)}, u32[]{:S(2)}) async-start(f32[128,1,128]{2,1,0:T(1,128)} %bitcast.6), calls=%async_computation | async-start | bytes 131072 | tf_op jit(solution)/shard_map/all_to_all | solution.py:573
  13.6 0.0 copy-start
  13.6 0.6 copy-done
  14.2 1.3 %tables_0.1 = (f32[128,512]{1,0:T(8,128)S(1)}, f32[128,512]{1,0:T(8,128)S(1)}, f32[128,512]{1,0:T(8,128)S(1)}, f32[128,512]{1,0:T(8,128)S(1)}, bf16[4,128,256]{2...) custom-call(s32[4]{0:T(128)S(1)} %copy-done), custom_call_target="tpu_custom_call" | custom-call | bytes 2960000 | tf_op jit(solution)/shard_map/tables_0/pallas_call | solution.py:424
  15.6 7.4 %all-to-all-done = f32[128,1,128]{2,1,0:T(1,128)S(1)} async-done(((f32[128,1,128]{2,1,0:T(1,128)}), f32[128,1,128]{2,1,0:T(1,128)S(1)}, u32[]{:S(2)}, u32[]{:S(2)}) %all-to-all-start) | async-done | bytes 65568 | tf_op jit(solution)/shard_map/all_to_all | solution.py:573
  23.0 2.1 %prepare.1 = (bf16[256,4096]{1,0:T(8,128)(2,1)S(1)}, f32[32,4,32,128]{3,2,1,0:T(8,128)S(1)}, f32[32,2,16,128]{3,2,1,0:T(8,128)S(1)}) custom-call(f32[128,128]{1,0:T(8,128)S(1)} %bitcast.5, f32[2,32,128]{2,1,0:T(8,128)S(1)} %get-tuple-element.20.speed_ref), custom_call_target="tpu_custom_call" | custom-call | bytes 7400000 | tf_op jit(solution)/shard_map/prepare/pallas_call | solution.py:195
  25.1 2.4 %leaf_0.1.rest_0_.own_ref = f32[128,256]{1,0:T(8,128)S(1)} custom-call(bf16[256,4096]{1,0:T(8,128)(2,1)S(1)} %get-tuple-element.21.l_ref, f32[32,4,32,128]{3,2,1,0:T(8,128)S(1)} %get-tuple-element.22.q_ref, f32[32,2,16,128]{3,2,1,0:T(8,128)S(1)} %get-tuple-element.23.z_ref), custom_call_target="tpu_custom_call" | custom-call | bytes 8510000 | tf_op jit(solution)/shard_map/leaf_0/pallas_call | solution.py:263
  27.5 0.1 collective-permute-start.1
  27.6 2.4 %leaf_1.1.own_ref = f32[128,256]{1,0:T(8,128)S(1)} custom-call(bf16[256,4096]{1,0:T(8,128)(2,1)S(1)} %get-tuple-element.21.l_ref, f32[32,4,32,128]{3,2,1,0:T(8,128)S(1)} %get-tuple-element.22.q_ref, f32[32,2,16,128]{3,2,1,0:T(8,128)S(1)} %get-tuple-element.23.z_ref, f32[128,256]{1,0:T(8,128)S(1)} %leaf_0.1.rest_0_.own_ref), custom_call_target="tpu_custom_call" | custom-call | bytes 8510000 | tf_op jit(solution)/shard_map/leaf_1/pallas_call | solution.py:263
  30.0 0.6 collective-permute-start
  30.6 0.0 collective-permute-done.1.other_ref
  30.6 0.2 merge_0_0.1.rest_0_.own_ref
  30.8 0.7 %collective-permute-start.2 = (f32[128,256]{1,0:T(8,128)S(1)}, f32[128,256]{1,0:T(8,128)S(1)}, u32[]{:S(2)}, u32[]{:S(2)}) collective-permute-start(f32[128,256]{1,0:T(8,128)S(1)} %merge_0_0.1.rest_0_.own_ref), channel_id=1, source_target_pairs={{0,1},{1,0},{2,3},{3,2},{4,5},{5,4},{6,7},{7,6},{8,9},{9,8},{10,11... | collective-permute-start | bytes 393224 | tf_op jit(solution)/shard_map/ppermute | solution.py:566
  31.5 2.4 %leaf_2.1.own_ref = f32[128,256]{1,0:T(8,128)S(1)} custom-call(bf16[256,4096]{1,0:T(8,128)(2,1)S(1)} %get-tuple-element.21.l_ref, f32[32,4,32,128]{3,2,1,0:T(8,128)S(1)} %get-tuple-element.22.q_ref, f32[32,2,16,128]{3,2,1,0:T(8,128)S(1)} %get-tuple-element.23.z_ref, f32[128,256]{1,0:T(8,128)S(1)} %merge_0_0.1.rest_0_.own_ref), custom_call_target="tpu_custom_call" | custom-call | bytes 8510000 | tf_op jit(solution)/shard_map/leaf_2/pallas_call | solution.py:263
  33.9 0.1 collective-permute-start.8
  34.0 0.0 collective-permute-done.other_ref
  34.0 0.2 merge_0_1.1.rest_0_.own_ref
  34.3 0.0 copy-start.1
  34.3 1.7 %collective-permute-start.4 = (f32[128,256]{1,0:T(8,128)S(1)}, f32[128,256]{1,0:T(8,128)S(1)}, u32[]{:S(2)}, u32[]{:S(2)}) collective-permute-start(f32[128,256]{1,0:T(8,128)S(1)} %merge_0_1.1.rest_0_.own_ref), channel_id=1, source_target_pairs={{0,1},{1,0},{2,3},{3,2},{4,5},{5,4},{6,7},{7,6},{8,9},{9,8},{10,11... | collective-permute-start | bytes 393224 | tf_op jit(solution)/shard_map/ppermute | solution.py:566
  36.0 0.4 collective-permute-done.2.rest_1_.other_ref
  36.3 2.4 %leaf_3.1.rest_0_.own_ref = f32[128,256]{1,0:T(8,128)S(1)} custom-call(bf16[256,4096]{1,0:T(8,128)(2,1)S(1)} %get-tuple-element.21.l_ref, f32[32,4,32,128]{3,2,1,0:T(8,128)S(1)} %get-tuple-element.22.q_ref, f32[32,2,16,128]{3,2,1,0:T(8,128)S(1)} %get-tuple-element.23.z_ref, f32[128,256]{1,0:T(8,128)S(1)} %merge_0_1.1.rest_0_.own_ref, ...), custom_call_target="tpu_custom_call" | custom-call | bytes 8510000 | tf_op jit(solution)/shard_map/leaf_3/pallas_call | solution.py:263
  38.8 0.1 collective-permute-start.3
  38.9 0.0 collective-permute-done.8.other_ref
  38.9 0.2 merge_0_2.1.own_ref
  39.1 0.7 %collective-permute-start.9 = (f32[128,256]{1,0:T(8,128)S(1)}, f32[128,256]{1,0:T(8,128)S(1)}, u32[]{:S(2)}, u32[]{:S(2)}) collective-permute-start(f32[128,256]{1,0:T(8,128)S(1)} %merge_0_2.1.own_ref), channel_id=1, source_target_pairs={{0,1},{1,0},{2,3},{3,2},{4,5},{5,4},{6,7},{7,6},{8,9},{9,8},{10,11... | collective-permute-start | bytes 393224 | tf_op jit(solution)/shard_map/ppermute | solution.py:566
  39.8 0.7 collective-permute-done.4.rest_1_.other_ref
  40.4 0.0 copy-done.1
  40.4 1.2 %tables_1.1 = (f32[128,512]{1,0:T(8,128)S(1)}, f32[128,512]{1,0:T(8,128)S(1)}, f32[128,512]{1,0:T(8,128)S(1)}, f32[128,512]{1,0:T(8,128)S(1)}) custom-call(s32[4]{0:T(128)S(1)} %copy-done.1, f32[128,256]{1,0:T(8,128)S(1)} %leaf_3.1.rest_0_.own_ref, f32[128,256]{1,0:T(8,128)S(1)} %collective-permute-done.4.rest_1_.other_ref), custom_call_target="tpu_custom_call" | custom-call | bytes 2960000 | tf_op jit(solution)/shard_map/tables_1/pallas_call | solution.py:424
  41.6 0.0 collective-permute-done.3.other_ref
  41.7 0.2 merge_0_3.1.own_ref
  41.9 1.5 %collective-permute-start.5 = (f32[128,256]{1,0:T(8,128)S(1)}, f32[128,256]{1,0:T(8,128)S(1)}, u32[]{:S(2)}, u32[]{:S(2)}) collective-permute-start(f32[128,256]{1,0:T(8,128)S(1)} %merge_0_3.1.own_ref), channel_id=1, source_target_pairs={{0,1},{1,0},{2,3},{3,2},{4,5},{5,4},{6,7},{7,6},{8,9},{9,8},{10,11... | collective-permute-start | bytes 393224 | tf_op jit(solution)/shard_map/ppermute | solution.py:566
  43.4 0.2 merge_1_0.1.own_ref
  43.6 0.7 %collective-permute-start.14 = (f32[128,256]{1,0:T(8,128)S(1)}, f32[128,256]{1,0:T(8,128)S(1)}, u32[]{:S(2)}, u32[]{:S(2)}) collective-permute-start(f32[128,256]{1,0:T(8,128)S(1)} %merge_1_0.1.own_ref), channel_id=1, source_target_pairs={{0,32},{16,48},{32,0},{48,16},{64,96},{80,112},{96,64},{112,80},{1... | collective-permute-start | bytes 393224 | tf_op jit(solution)/shard_map/ppermute | solution.py:566
  44.3 0.2 merge_1_1.1.own_ref
  44.6 1.5 %collective-permute-start.12 = (f32[128,256]{1,0:T(8,128)S(1)}, f32[128,256]{1,0:T(8,128)S(1)}, u32[]{:S(2)}, u32[]{:S(2)}) collective-permute-start(f32[128,256]{1,0:T(8,128)S(1)} %merge_1_1.1.own_ref), channel_id=1, source_target_pairs={{0,32},{16,48},{32,0},{48,16},{64,96},{80,112},{96,64},{112,80},{1... | collective-permute-start | bytes 393224 | tf_op jit(solution)/shard_map/ppermute | solution.py:566
  46.0 0.0 collective-permute-done.9.other_ref
  46.0 0.2 merge_1_2.1.own_ref
  46.3 0.7 %collective-permute-start.10 = (f32[128,256]{1,0:T(8,128)S(1)}, f32[128,256]{1,0:T(8,128)S(1)}, u32[]{:S(2)}, u32[]{:S(2)}) collective-permute-start(f32[128,256]{1,0:T(8,128)S(1)} %merge_1_2.1.own_ref), channel_id=1, source_target_pairs={{0,32},{16,48},{32,0},{48,16},{64,96},{80,112},{96,64},{112,80},{1... | collective-permute-start | bytes 393224 | tf_op jit(solution)/shard_map/ppermute | solution.py:566
  47.0 0.9 %collective-permute-done.5.other_ref = f32[128,256]{1,0:T(8,128)S(1)} collective-permute-done((f32[128,256]{1,0:T(8,128)S(1)}, f32[128,256]{1,0:T(8,128)S(1)}, u32[]{:S(2)}, u32[]{:S(2)}) %collective-permute-start.5) | collective-permute-done | bytes 131104 | tf_op jit(solution)/shard_map/ppermute | solution.py:566
  47.9 0.2 merge_1_3.1.own_ref
  48.1 0.7 %collective-permute-start.6 = (f32[128,256]{1,0:T(8,128)S(1)}, f32[128,256]{1,0:T(8,128)S(1)}, u32[]{:S(2)}, u32[]{:S(2)}) collective-permute-start(f32[128,256]{1,0:T(8,128)S(1)} %merge_1_3.1.own_ref), channel_id=1, source_target_pairs={{0,32},{16,48},{32,0},{48,16},{64,96},{80,112},{96,64},{112,80},{1... | collective-permute-start | bytes 393224 | tf_op jit(solution)/shard_map/ppermute | solution.py:566
  48.8 1.3 %collective-permute-done.14.other_ref = f32[128,256]{1,0:T(8,128)S(1)} collective-permute-done((f32[128,256]{1,0:T(8,128)S(1)}, f32[128,256]{1,0:T(8,128)S(1)}, u32[]{:S(2)}, u32[]{:S(2)}) %collective-permute-start.14) | collective-permute-done | bytes 131104 | tf_op jit(solution)/shard_map/ppermute | solution.py:566
  50.1 0.2 merge_2_0.1.own_ref
  50.3 1.0 %collective-permute-start.15 = (f32[128,256]{1,0:T(8,128)S(1)}, f32[128,256]{1,0:T(8,128)S(1)}, u32[]{:S(2)}, u32[]{:S(2)}) collective-permute-start(f32[128,256]{1,0:T(8,128)S(1)} %merge_2_0.1.own_ref), channel_id=1, source_target_pairs={{0,2},{1,3},{2,0},{3,1},{4,6},{5,7},{6,4},{7,5},{8,10},{9,11},{10,... | collective-permute-start | bytes 393224 | tf_op jit(solution)/shard_map/ppermute | solution.py:566
  51.4 1.6 %collective-permute-done.12.other_ref = f32[128,256]{1,0:T(8,128)S(1)} collective-permute-done((f32[128,256]{1,0:T(8,128)S(1)}, f32[128,256]{1,0:T(8,128)S(1)}, u32[]{:S(2)}, u32[]{:S(2)}) %collective-permute-start.12) | collective-permute-done | bytes 131104 | tf_op jit(solution)/shard_map/ppermute | solution.py:566
  52.9 0.2 merge_2_1.1.own_ref
  53.2 1.1 %collective-permute-start.13 = (f32[128,256]{1,0:T(8,128)S(1)}, f32[128,256]{1,0:T(8,128)S(1)}, u32[]{:S(2)}, u32[]{:S(2)}) collective-permute-start(f32[128,256]{1,0:T(8,128)S(1)} %merge_2_1.1.own_ref), channel_id=1, source_target_pairs={{0,2},{1,3},{2,0},{3,1},{4,6},{5,7},{6,4},{7,5},{8,10},{9,11},{10,... | collective-permute-start | bytes 393224 | tf_op jit(solution)/shard_map/ppermute | solution.py:566
  54.3 1.3 %collective-permute-done.10.other_ref = f32[128,256]{1,0:T(8,128)S(1)} collective-permute-done((f32[128,256]{1,0:T(8,128)S(1)}, f32[128,256]{1,0:T(8,128)S(1)}, u32[]{:S(2)}, u32[]{:S(2)}) %collective-permute-start.10) | collective-permute-done | bytes 131104 | tf_op jit(solution)/shard_map/ppermute | solution.py:566
  55.6 0.2 merge_2_2.1.own_ref
  55.8 1.3 %collective-permute-start.11 = (f32[128,256]{1,0:T(8,128)S(1)}, f32[128,256]{1,0:T(8,128)S(1)}, u32[]{:S(2)}, u32[]{:S(2)}) collective-permute-start(f32[128,256]{1,0:T(8,128)S(1)} %merge_2_2.1.own_ref), channel_id=1, source_target_pairs={{0,2},{1,3},{2,0},{3,1},{4,6},{5,7},{6,4},{7,5},{8,10},{9,11},{10,... | collective-permute-start | bytes 393224 | tf_op jit(solution)/shard_map/ppermute | solution.py:566
  57.1 0.0 collective-permute-done.6.other_ref
  57.1 0.2 merge_2_3.1.own_ref
  57.3 2.4 %collective-permute-start.7 = (f32[128,256]{1,0:T(8,128)S(1)}, f32[128,256]{1,0:T(8,128)S(1)}, u32[]{:S(2)}, u32[]{:S(2)}) collective-permute-start(f32[128,256]{1,0:T(8,128)S(1)} %merge_2_3.1.own_ref), channel_id=1, source_target_pairs={{0,2},{1,3},{2,0},{3,1},{4,6},{5,7},{6,4},{7,5},{8,10},{9,11},{10,... | collective-permute-start | bytes 393224 | tf_op jit(solution)/shard_map/ppermute | solution.py:566
  59.7 1.0 %last.1 = (f32[128,1024]{1,0:T(8,128)S(1)}, bf16[256,256]{1,0:T(8,128)(2,1)S(1)}) custom-call(s32[4]{0:T(128)S(1)} %copy-done.1, f32[128,256]{1,0:T(8,128)S(1)} %merge_0_0.1.rest_0_.own_ref), custom_call_target="tpu_custom_call" | custom-call | bytes 2960000 | tf_op jit(solution)/shard_map/last/pallas_call | solution.py:467
  60.7 0.0 collective-permute-done.15.other_ref
  60.7 1.1 %finish_0.1.rest_0_ = f32[2,64,1024]{2,1,0:T(8,128)} custom-call(f32[128,256]{1,0:T(8,128)S(1)} %merge_2_0.1.own_ref, f32[128,256]{1,0:T(8,128)S(1)} %collective-permute-done.15.other_ref, f32[128,512]{1,0:T(8,128)S(1)} %get-tuple-element.31.gamma_own_ref, f32[128,512]{1,0:T(8,128)S(1)} %get-tuple-element.32.gamma_other_ref, ...), custom_call_target="tpu_custom_call" | custom-call | bytes 3700000 | tf_op jit(solution)/shard_map/finish_0/pallas_call | solution.py:551
  61.7 0.0 collective-permute-done.13.other_ref
  61.7 1.1 %finish_1.1.rest_0_ = f32[2,64,1024]{2,1,0:T(8,128)} custom-call(f32[128,256]{1,0:T(8,128)S(1)} %merge_2_1.1.own_ref, f32[128,256]{1,0:T(8,128)S(1)} %collective-permute-done.13.other_ref, f32[128,512]{1,0:T(8,128)S(1)} %get-tuple-element.31.gamma_own_ref, f32[128,512]{1,0:T(8,128)S(1)} %get-tuple-element.32.gamma_other_ref, ...), custom_call_target="tpu_custom_call", output_to_operand_aliasing={{}: (7, {})} | custom-call | bytes 3700000 | tf_op jit(solution)/shard_map/finish_1/pallas_call | solution.py:551
  62.8 0.0 collective-permute-done.11.other_ref
  62.8 1.1 %finish_2.1.rest_0_ = f32[2,64,1024]{2,1,0:T(8,128)} custom-call(f32[128,256]{1,0:T(8,128)S(1)} %merge_2_2.1.own_ref, f32[128,256]{1,0:T(8,128)S(1)} %collective-permute-done.11.other_ref, f32[128,512]{1,0:T(8,128)S(1)} %get-tuple-element.31.gamma_own_ref, f32[128,512]{1,0:T(8,128)S(1)} %get-tuple-element.32.gamma_other_ref, ...), custom_call_target="tpu_custom_call", output_to_operand_aliasing={{}: (7, {})} | custom-call | bytes 3700000 | tf_op jit(solution)/shard_map/finish_2/pallas_call | solution.py:551
  63.9 0.2 collective-permute-done.7.other_ref
  64.1 1.1 %finish_3.1 = f32[2,64,1024]{2,1,0:T(8,128)} custom-call(f32[128,256]{1,0:T(8,128)S(1)} %merge_2_3.1.own_ref, f32[128,256]{1,0:T(8,128)S(1)} %collective-permute-done.7.other_ref, f32[128,512]{1,0:T(8,128)S(1)} %get-tuple-element.31.gamma_own_ref, f32[128,512]{1,0:T(8,128)S(1)} %get-tuple-element.32.gamma_other_ref, ...), custom_call_target="tpu_custom_call", output_to_operand_aliasing={{}: (7, {})} | custom-call | bytes 3700000 | tf_op jit(solution)/shard_map/finish_3/pallas_call | solution.py:551
Async XLA Ops:
  2.4 20.6 %all-to-all-start = ((f32[128,1,128]{2,1,0:T(1,128)}), f32[128,1,128]{2,1,0:T(1,128)S(1)}, u32[]{:S(2)}, u32[]{:S(2)}) async-start(f32[128,1,128]{2,1,0:T(1,128)} %bitcast.6), calls=%async_computation | async-start | bytes 131072 | tf_op jit(solution)/shard_map/all_to_all | solution.py:573
  13.6 0.7 %copy-start = (s32[4]{0:T(128)S(1)}, s32[4]{0:T(128)}, u32[]{:S(2)}) copy-start(s32[4]{0:T(128)} %info_ref.5) | copy-start | bytes 52
  27.5 3.1 %collective-permute-start.1 = (f32[128,256]{1,0:T(8,128)S(1)}, f32[128,256]{1,0:T(8,128)S(1)}, u32[]{:S(2)}, u32[]{:S(2)}) collective-permute-start(f32[128,256]{1,0:T(8,128)S(1)} %leaf_0.1.rest_0_.own_ref), channel_id=1, source_target_pairs={{0,16},{16,0},{32,48},{48,32},{64,80},{80,64},{96,112},{112,96},{1... | collective-permute-start | bytes 393224 | tf_op jit(solution)/shard_map/ppermute | solution.py:566
  30.0 4.0 %collective-permute-start = (f32[128,256]{1,0:T(8,128)S(1)}, f32[128,256]{1,0:T(8,128)S(1)}, u32[]{:S(2)}, u32[]{:S(2)}) collective-permute-start(f32[128,256]{1,0:T(8,128)S(1)} %leaf_1.1.own_ref), channel_id=1, source_target_pairs={{0,16},{16,0},{32,48},{48,32},{64,80},{80,64},{96,112},{112,96},{1... | collective-permute-start | bytes 393224 | tf_op jit(solution)/shard_map/ppermute | solution.py:566
  30.8 5.5 %collective-permute-start.2 = (f32[128,256]{1,0:T(8,128)S(1)}, f32[128,256]{1,0:T(8,128)S(1)}, u32[]{:S(2)}, u32[]{:S(2)}) collective-permute-start(f32[128,256]{1,0:T(8,128)S(1)} %merge_0_0.1.rest_0_.own_ref), channel_id=1, source_target_pairs={{0,1},{1,0},{2,3},{3,2},{4,5},{5,4},{6,7},{7,6},{8,9},{9,8},{10,11... | collective-permute-start | bytes 393224 | tf_op jit(solution)/shard_map/ppermute | solution.py:566
  33.9 4.9 %collective-permute-start.8 = (f32[128,256]{1,0:T(8,128)S(1)}, f32[128,256]{1,0:T(8,128)S(1)}, u32[]{:S(2)}, u32[]{:S(2)}) collective-permute-start(f32[128,256]{1,0:T(8,128)S(1)} %leaf_2.1.own_ref), channel_id=1, source_target_pairs={{0,16},{16,0},{32,48},{48,32},{64,80},{80,64},{96,112},{112,96},{1... | collective-permute-start | bytes 393224 | tf_op jit(solution)/shard_map/ppermute | solution.py:566
  34.3 6.2 %copy-start.1 = (s32[4]{0:T(128)S(1)}, s32[4]{0:T(128)}, u32[]{:S(2)}) copy-start(s32[4]{0:T(128)} %info_ref.5) | copy-start | bytes 52
  34.3 6.1 %collective-permute-start.4 = (f32[128,256]{1,0:T(8,128)S(1)}, f32[128,256]{1,0:T(8,128)S(1)}, u32[]{:S(2)}, u32[]{:S(2)}) collective-permute-start(f32[128,256]{1,0:T(8,128)S(1)} %merge_0_1.1.rest_0_.own_ref), channel_id=1, source_target_pairs={{0,1},{1,0},{2,3},{3,2},{4,5},{5,4},{6,7},{7,6},{8,9},{9,8},{10,11... | collective-permute-start | bytes 393224 | tf_op jit(solution)/shard_map/ppermute | solution.py:566
  38.8 2.9 %collective-permute-start.3 = (f32[128,256]{1,0:T(8,128)S(1)}, f32[128,256]{1,0:T(8,128)S(1)}, u32[]{:S(2)}, u32[]{:S(2)}) collective-permute-start(f32[128,256]{1,0:T(8,128)S(1)} %leaf_3.1.rest_0_.own_ref), channel_id=1, source_target_pairs={{0,16},{16,0},{32,48},{48,32},{64,80},{80,64},{96,112},{112,96},{1... | collective-permute-start | bytes 393224 | tf_op jit(solution)/shard_map/ppermute | solution.py:566
  39.1 6.9 %collective-permute-start.9 = (f32[128,256]{1,0:T(8,128)S(1)}, f32[128,256]{1,0:T(8,128)S(1)}, u32[]{:S(2)}, u32[]{:S(2)}) collective-permute-start(f32[128,256]{1,0:T(8,128)S(1)} %merge_0_2.1.own_ref), channel_id=1, source_target_pairs={{0,1},{1,0},{2,3},{3,2},{4,5},{5,4},{6,7},{7,6},{8,9},{9,8},{10,11... | collective-permute-start | bytes 393224 | tf_op jit(solution)/shard_map/ppermute | solution.py:566
  41.9 6.0 %collective-permute-start.5 = (f32[128,256]{1,0:T(8,128)S(1)}, f32[128,256]{1,0:T(8,128)S(1)}, u32[]{:S(2)}, u32[]{:S(2)}) collective-permute-start(f32[128,256]{1,0:T(8,128)S(1)} %merge_0_3.1.own_ref), channel_id=1, source_target_pairs={{0,1},{1,0},{2,3},{3,2},{4,5},{5,4},{6,7},{7,6},{8,9},{9,8},{10,11... | collective-permute-start | bytes 393224 | tf_op jit(solution)/shard_map/ppermute | solution.py:566
  43.6 6.5 %collective-permute-start.14 = (f32[128,256]{1,0:T(8,128)S(1)}, f32[128,256]{1,0:T(8,128)S(1)}, u32[]{:S(2)}, u32[]{:S(2)}) collective-permute-start(f32[128,256]{1,0:T(8,128)S(1)} %merge_1_0.1.own_ref), channel_id=1, source_target_pairs={{0,32},{16,48},{32,0},{48,16},{64,96},{80,112},{96,64},{112,80},{1... | collective-permute-start | bytes 393224 | tf_op jit(solution)/shard_map/ppermute | solution.py:566
  44.6 8.4 %collective-permute-start.12 = (f32[128,256]{1,0:T(8,128)S(1)}, f32[128,256]{1,0:T(8,128)S(1)}, u32[]{:S(2)}, u32[]{:S(2)}) collective-permute-start(f32[128,256]{1,0:T(8,128)S(1)} %merge_1_1.1.own_ref), channel_id=1, source_target_pairs={{0,32},{16,48},{32,0},{48,16},{64,96},{80,112},{96,64},{112,80},{1... | collective-permute-start | bytes 393224 | tf_op jit(solution)/shard_map/ppermute | solution.py:566
  46.3 9.3 %collective-permute-start.10 = (f32[128,256]{1,0:T(8,128)S(1)}, f32[128,256]{1,0:T(8,128)S(1)}, u32[]{:S(2)}, u32[]{:S(2)}) collective-permute-start(f32[128,256]{1,0:T(8,128)S(1)} %merge_1_2.1.own_ref), channel_id=1, source_target_pairs={{0,32},{16,48},{32,0},{48,16},{64,96},{80,112},{96,64},{112,80},{1... | collective-permute-start | bytes 393224 | tf_op jit(solution)/shard_map/ppermute | solution.py:566
  48.1 9.0 %collective-permute-start.6 = (f32[128,256]{1,0:T(8,128)S(1)}, f32[128,256]{1,0:T(8,128)S(1)}, u32[]{:S(2)}, u32[]{:S(2)}) collective-permute-start(f32[128,256]{1,0:T(8,128)S(1)} %merge_1_3.1.own_ref), channel_id=1, source_target_pairs={{0,32},{16,48},{32,0},{48,16},{64,96},{80,112},{96,64},{112,80},{1... | collective-permute-start | bytes 393224 | tf_op jit(solution)/shard_map/ppermute | solution.py:566
  50.3 10.3 %collective-permute-start.15 = (f32[128,256]{1,0:T(8,128)S(1)}, f32[128,256]{1,0:T(8,128)S(1)}, u32[]{:S(2)}, u32[]{:S(2)}) collective-permute-start(f32[128,256]{1,0:T(8,128)S(1)} %merge_2_0.1.own_ref), channel_id=1, source_target_pairs={{0,2},{1,3},{2,0},{3,1},{4,6},{5,7},{6,4},{7,5},{8,10},{9,11},{10,... | collective-permute-start | bytes 393224 | tf_op jit(solution)/shard_map/ppermute | solution.py:566
  53.2 8.6 %collective-permute-start.13 = (f32[128,256]{1,0:T(8,128)S(1)}, f32[128,256]{1,0:T(8,128)S(1)}, u32[]{:S(2)}, u32[]{:S(2)}) collective-permute-start(f32[128,256]{1,0:T(8,128)S(1)} %merge_2_1.1.own_ref), channel_id=1, source_target_pairs={{0,2},{1,3},{2,0},{3,1},{4,6},{5,7},{6,4},{7,5},{8,10},{9,11},{10,... | collective-permute-start | bytes 393224 | tf_op jit(solution)/shard_map/ppermute | solution.py:566
  55.8 7.1 %collective-permute-start.11 = (f32[128,256]{1,0:T(8,128)S(1)}, f32[128,256]{1,0:T(8,128)S(1)}, u32[]{:S(2)}, u32[]{:S(2)}) collective-permute-start(f32[128,256]{1,0:T(8,128)S(1)} %merge_2_2.1.own_ref), channel_id=1, source_target_pairs={{0,2},{1,3},{2,0},{3,1},{4,6},{5,7},{6,4},{7,5},{8,10},{9,11},{10,... | collective-permute-start | bytes 393224 | tf_op jit(solution)/shard_map/ppermute | solution.py:566
  57.3 6.8 %collective-permute-start.7 = (f32[128,256]{1,0:T(8,128)S(1)}, f32[128,256]{1,0:T(8,128)S(1)}, u32[]{:S(2)}, u32[]{:S(2)}) collective-permute-start(f32[128,256]{1,0:T(8,128)S(1)} %merge_2_3.1.own_ref), channel_id=1, source_target_pairs={{0,2},{1,3},{2,0},{3,1},{4,6},{5,7},{6,4},{7,5},{8,10},{9,11},{10,... | collective-permute-start | bytes 393224 | tf_op jit(solution)/shard_map/ppermute | solution.py:566

commit v6 on v5

--- a/solution.py
+++ b/solution.py
@@ -587,20 +587,27 @@
     leaf2 = leaf(c2, prepared, (one0,))
     one1 = join(0, c1, leaf1, exchange(0, c1, leaf1))
     got0 = exchange(1, c0, one0)
+    two0 = join(1, c0, one0, got0)
     leaf3 = leaf(c3, prepared, (one1, got0))
     one2 = join(0, c2, leaf2, exchange(0, c2, leaf2))
-    got1 = exchange(1, c1, one1)
-    gammas += tables(info, 1, (leaf3, got1))
-    one3 = join(0, c3, leaf3, exchange(0, c3, leaf3), (gammas[4],))
-    ones = [one0, one1, one2, one3]
+    one3 = join(0, c3, leaf3, exchange(0, c3, leaf3), (two0, one2))
+    two1 = join(1, c1, one1, exchange(1, c1, one1))
+    gammas += tables(info, 1, (one3, two1))
+    y0 = exchange(2, c0, two0)
+    y1 = exchange(2, c1, two1)
+    three0 = join(2, c0, two0, y0)
+    x0 = exchange(3, c0, three0)
+    two2 = join(1, c2, one2, exchange(1, c2, one2), (three0,))
+    three1 = join(2, c1, two1, y1)
+    x1 = exchange(3, c1, three1)
+    two3 = join(1, c3, one3, exchange(1, c3, one3), (three1,))
+    three2 = join(2, c2, two2, exchange(2, c2, two2), (x0,))
+    x2 = exchange(3, c2, three2)
+    three3 = join(2, c3, two3, exchange(2, c3, two3), (x0, x1))
     lasts = last_tables(info, (one0,))
-    swapped = [got0, got1, exchange(1, c2, one2), exchange(1, c3, one3)]
-
-    late = [join(1, c, x, y) for c, x, y in zip(CHUNKS, ones, swapped)]
-    holding = [join(2, c, x, exchange(2, c, x)) for c, x in zip(CHUNKS, late)]
     out = None
-    for c, x in zip(CHUNKS, holding):
-        out = finish(c, x, swap(x, *LEVELS[3]), gammas[6:], mix, lasts, out)
+    for c, x, y in zip(CHUNKS, (three0, three1, three2, three3), (x0, x1, x2, exchange(3, c3, three3))):
+        out = finish(c, x, y, gammas[6:], mix, lasts, out)
     return out
 
 

time: 65.6 us -> 63.9 us (0.974)
  waiting for transfers between devices: 13.8 us -> 9.31 us
  starting transfers between devices: 25.9 us -> 29 us
    ppermute x16, waiting for transfers between devices: 6.31 us -> 1.87 us  [swap(): lax.ppermute(value, axis, [(i, i ^ 1 << level) for i in range(lax.axis_si...]
    ppermute x16, starting transfers between devices: 14.8 us -> 17.8 us  [swap(): lax.ppermute(value, axis, [(i, i ^ 1 << level) for i in range(lax.axis_si...]
  transfers between devices with their start and end apart: 17 -> 17, of which waited for: 8 -> 6; matrix products, arithmetic and copies ran while one was open for 0% -> 0% of each run, Pallas kernels for 25% -> 26%
where the time goes in v6:
time: 63.9 us; the launch traced here: 63.6 us
  starting transfers between devices  29 us (45%)
  Pallas kernels  24.2 us (38%)
  waiting for transfers between devices  9.31 us (15%)
  local copies, waits for them, and re-layouts  0.66 us (1%)
    ppermute x16, starting transfers between devices, swap(): lax.ppermute(value, axis, [(i, i ^ 1 << level) for i in range(lax.axis_si...  17.8 us
    all_to_all x1, starting transfers between devices, on_device(): lax.all_to_all(sent.reshape(owners, 1, -1), ('bx', 'by'), split_axis=0, c...  11.1 us
    pallas_call x4, Pallas kernels, leaf(): pl.pallas_call(functools.partial(leaf_body, chunk), out_shape=jax.ShapeDt...  9.43 us
    all_to_all x1, waiting for transfers between devices, on_device(): lax.all_to_all(sent.reshape(owners, 1, -1), ('bx', 'by'), split_axis=0, c...  7.44 us
    pallas_call x4, Pallas kernels, finish(): pl.pallas_call(functools.partial(finish_body, chunk), out_shape=jax.Shape...  4.27 us
    pallas_call x12, Pallas kernels, merge(): pl.pallas_call(functools.partial(merge_body, number, chunk), out_shape=ja...  2.53 us
    pallas_call x2, Pallas kernels, tables(): pl.pallas_call(functools.partial(tables_body, pair), out_shape=tuple(shap...  2.53 us
    pallas_call x1, Pallas kernels, pack(): pl.pallas_call(pack_body, out_shape=jax.ShapeDtypeStruct((128, 4 * CAP),...  2.43 us
  transfers between devices with their start and end apart: 17, of which 6 were waited for; matrix products, arithmetic and copies ran while one was open for 0% of the time, Pallas kernels for 26%

profile of v6, /device:TPU:0, one launch (start us, length us, event | category | flops | bytes accessed | tf_op | source)
XLA Modules:
  0.0 63.6 jit_solution(18233566352521147463)
XLA Ops:
  0.0 2.4 %pack.1 = f32[128,128]{1,0:T(8,128)} custom-call(s32[16,128]{1,0:T(8,128)} %bitcast.7, s32[2,2048]{1,0:T(2,128)} %off_ref.1, f32[2,2048]{1,0:T(2,128)} %val_ref.1), custom_call_target="tpu_custom_call" | custom-call | bytes 7400000 | tf_op jit(solution)/shard_map/pack/pallas_call | solution.py:108
  2.4 11.1 %all-to-all-start = ((f32[128,1,128]{2,1,0:T(1,128)}), f32[128,1,128]{2,1,0:T(1,128)S(1)}, u32[]{:S(2)}, u32[]{:S(2)}) async-start(f32[128,1,128]{2,1,0:T(1,128)} %bitcast.6), calls=%async_computation | async-start | bytes 131072 | tf_op jit(solution)/shard_map/all_to_all | solution.py:573
  13.6 0.0 copy-start
  13.6 0.6 %copy-done = s32[4]{0:T(128)S(1)} copy-done((s32[4]{0:T(128)S(1)}, s32[4]{0:T(128)}, u32[]{:S(2)}) %copy-start) | copy-done | bytes 40
  14.2 1.3 %tables_0.1 = (f32[128,512]{1,0:T(8,128)S(1)}, f32[128,512]{1,0:T(8,128)S(1)}, f32[128,512]{1,0:T(8,128)S(1)}, f32[128,512]{1,0:T(8,128)S(1)}, bf16[4,128,256]{2...) custom-call(s32[4]{0:T(128)S(1)} %copy-done), custom_call_target="tpu_custom_call" | custom-call | bytes 2960000 | tf_op jit(solution)/shard_map/tables_0/pallas_call | solution.py:424
  15.6 7.4 %all-to-all-done = f32[128,1,128]{2,1,0:T(1,128)S(1)} async-done(((f32[128,1,128]{2,1,0:T(1,128)}), f32[128,1,128]{2,1,0:T(1,128)S(1)}, u32[]{:S(2)}, u32[]{:S(2)}) %all-to-all-start) | async-done | bytes 65568 | tf_op jit(solution)/shard_map/all_to_all | solution.py:573
  23.0 2.1 %prepare.1 = (bf16[256,4096]{1,0:T(8,128)(2,1)S(1)}, f32[32,4,32,128]{3,2,1,0:T(8,128)S(1)}, f32[32,2,16,128]{3,2,1,0:T(8,128)S(1)}) custom-call(f32[128,128]{1,0:T(8,128)S(1)} %bitcast.5, f32[2,32,128]{2,1,0:T(8,128)S(1)} %get-tuple-element.20.speed_ref), custom_call_target="tpu_custom_call" | custom-call | bytes 7400000 | tf_op jit(solution)/shard_map/prepare/pallas_call | solution.py:195
  25.1 2.4 %leaf_0.1.rest_0_.own_ref = f32[128,256]{1,0:T(8,128)S(1)} custom-call(bf16[256,4096]{1,0:T(8,128)(2,1)S(1)} %get-tuple-element.21.l_ref, f32[32,4,32,128]{3,2,1,0:T(8,128)S(1)} %get-tuple-element.22.q_ref, f32[32,2,16,128]{3,2,1,0:T(8,128)S(1)} %get-tuple-element.23.z_ref), custom_call_target="tpu_custom_call" | custom-call | bytes 8510000 | tf_op jit(solution)/shard_map/leaf_0/pallas_call | solution.py:263
  27.4 0.1 collective-permute-start.1
  27.5 2.4 %leaf_1.1.own_ref = f32[128,256]{1,0:T(8,128)S(1)} custom-call(bf16[256,4096]{1,0:T(8,128)(2,1)S(1)} %get-tuple-element.21.l_ref, f32[32,4,32,128]{3,2,1,0:T(8,128)S(1)} %get-tuple-element.22.q_ref, f32[32,2,16,128]{3,2,1,0:T(8,128)S(1)} %get-tuple-element.23.z_ref, f32[128,256]{1,0:T(8,128)S(1)} %leaf_0.1.rest_0_.own_ref), custom_call_target="tpu_custom_call" | custom-call | bytes 8510000 | tf_op jit(solution)/shard_map/leaf_1/pallas_call | solution.py:263
  29.9 0.6 collective-permute-start
  30.5 0.0 collective-permute-done.1.other_ref
  30.5 0.2 merge_0_0.1.own_ref.rest_0_
  30.7 0.7 %collective-permute-start.2 = (f32[128,256]{1,0:T(8,128)S(1)}, f32[128,256]{1,0:T(8,128)S(1)}, u32[]{:S(2)}, u32[]{:S(2)}) collective-permute-start(f32[128,256]{1,0:T(8,128)S(1)} %merge_0_0.1.own_ref.rest_0_), channel_id=1, source_target_pairs={{0,1},{1,0},{2,3},{3,2},{4,5},{5,4},{6,7},{7,6},{8,9},{9,8},{10,11... | collective-permute-start | bytes 393224 | tf_op jit(solution)/shard_map/ppermute | solution.py:566
  31.4 2.4 %leaf_2.1.own_ref = f32[128,256]{1,0:T(8,128)S(1)} custom-call(bf16[256,4096]{1,0:T(8,128)(2,1)S(1)} %get-tuple-element.21.l_ref, f32[32,4,32,128]{3,2,1,0:T(8,128)S(1)} %get-tuple-element.22.q_ref, f32[32,2,16,128]{3,2,1,0:T(8,128)S(1)} %get-tuple-element.23.z_ref, f32[128,256]{1,0:T(8,128)S(1)} %merge_0_0.1.own_ref.rest_0_), custom_call_target="tpu_custom_call" | custom-call | bytes 8510000 | tf_op jit(solution)/shard_map/leaf_2/pallas_call | solution.py:263
  33.7 0.1 collective-permute-start.4
  33.8 0.0 collective-permute-done.other_ref
  33.8 0.2 merge_0_1.1.rest_0_.own_ref
  34.0 1.7 %collective-permute-start.6 = (f32[128,256]{1,0:T(8,128)S(1)}, f32[128,256]{1,0:T(8,128)S(1)}, u32[]{:S(2)}, u32[]{:S(2)}) collective-permute-start(f32[128,256]{1,0:T(8,128)S(1)} %merge_0_1.1.rest_0_.own_ref), channel_id=1, source_target_pairs={{0,1},{1,0},{2,3},{3,2},{4,5},{5,4},{6,7},{7,6},{8,9},{9,8},{10,11... | collective-permute-start | bytes 393224 | tf_op jit(solution)/shard_map/ppermute | solution.py:566
  35.7 0.4 collective-permute-done.2.rest_1_.other_ref
  36.2 2.4 %leaf_3.1.own_ref = f32[128,256]{1,0:T(8,128)S(1)} custom-call(bf16[256,4096]{1,0:T(8,128)(2,1)S(1)} %get-tuple-element.21.l_ref, f32[32,4,32,128]{3,2,1,0:T(8,128)S(1)} %get-tuple-element.22.q_ref, f32[32,2,16,128]{3,2,1,0:T(8,128)S(1)} %get-tuple-element.23.z_ref, f32[128,256]{1,0:T(8,128)S(1)} %merge_0_1.1.rest_0_.own_ref, ...), custom_call_target="tpu_custom_call" | custom-call | bytes 8510000 | tf_op jit(solution)/shard_map/leaf_3/pallas_call | solution.py:263
  38.6 0.1 collective-permute-start.3
  38.7 0.2 merge_1_0.1.rest_0_.own_ref
  38.9 0.0 copy-start.1
  38.9 0.7 %collective-permute-start.9 = (f32[128,256]{1,0:T(8,128)S(1)}, f32[128,256]{1,0:T(8,128)S(1)}, u32[]{:S(2)}, u32[]{:S(2)}) collective-permute-start(f32[128,256]{1,0:T(8,128)S(1)} %merge_1_0.1.rest_0_.own_ref), channel_id=1, source_target_pairs={{0,32},{16,48},{32,0},{48,16},{64,96},{80,112},{96,64},{112,80},{1... | collective-permute-start | bytes 393224 | tf_op jit(solution)/shard_map/ppermute | solution.py:566
  39.6 0.0 collective-permute-done.4.other_ref
  39.6 0.2 merge_0_2.1.rest_1_.own_ref
  39.8 0.7 %collective-permute-start.13 = (f32[128,256]{1,0:T(8,128)S(1)}, f32[128,256]{1,0:T(8,128)S(1)}, u32[]{:S(2)}, u32[]{:S(2)}) collective-permute-start(f32[128,256]{1,0:T(8,128)S(1)} %merge_0_2.1.rest_1_.own_ref), channel_id=1, source_target_pairs={{0,1},{1,0},{2,3},{3,2},{4,5},{5,4},{6,7},{7,6},{8,9},{9,8},{10,11... | collective-permute-start | bytes 393224 | tf_op jit(solution)/shard_map/ppermute | solution.py:566
  40.5 0.0 collective-permute-done.6.other_ref
  40.5 0.2 merge_1_1.1.rest_1_.own_ref
  40.7 1.5 %collective-permute-start.7 = (f32[128,256]{1,0:T(8,128)S(1)}, f32[128,256]{1,0:T(8,128)S(1)}, u32[]{:S(2)}, u32[]{:S(2)}) collective-permute-start(f32[128,256]{1,0:T(8,128)S(1)} %merge_1_1.1.rest_1_.own_ref), channel_id=1, source_target_pairs={{0,32},{16,48},{32,0},{48,16},{64,96},{80,112},{96,64},{112,80},{1... | collective-permute-start | bytes 393224 | tf_op jit(solution)/shard_map/ppermute | solution.py:566
  42.2 0.0 collective-permute-done.3.other_ref
  42.2 0.2 merge_0_3.1.rest_0_.own_ref
  42.4 1.5 %collective-permute-start.5 = (f32[128,256]{1,0:T(8,128)S(1)}, f32[128,256]{1,0:T(8,128)S(1)}, u32[]{:S(2)}, u32[]{:S(2)}) collective-permute-start(f32[128,256]{1,0:T(8,128)S(1)} %merge_0_3.1.rest_0_.own_ref), channel_id=1, source_target_pairs={{0,1},{1,0},{2,3},{3,2},{4,5},{5,4},{6,7},{7,6},{8,9},{9,8},{10,11... | collective-permute-start | bytes 393224 | tf_op jit(solution)/shard_map/ppermute | solution.py:566
  43.9 0.0 copy-done.1
  43.9 1.2 %tables_1.1 = (f32[128,512]{1,0:T(8,128)S(1)}, f32[128,512]{1,0:T(8,128)S(1)}, f32[128,512]{1,0:T(8,128)S(1)}, f32[128,512]{1,0:T(8,128)S(1)}) custom-call(s32[4]{0:T(128)S(1)} %copy-done.1, f32[128,256]{1,0:T(8,128)S(1)} %merge_0_3.1.rest_0_.own_ref, f32[128,256]{1,0:T(8,128)S(1)} %merge_1_1.1.rest_1_.own_ref), custom_call_target="tpu_custom_call" | custom-call | bytes 2960000 | tf_op jit(solution)/shard_map/tables_1/pallas_call | solution.py:424
  45.2 0.1 collective-permute-done.9.other_ref
  45.3 0.2 merge_2_0.1.rest_0_.own_ref
  45.5 1.1 %collective-permute-start.10 = (f32[128,256]{1,0:T(8,128)S(1)}, f32[128,256]{1,0:T(8,128)S(1)}, u32[]{:S(2)}, u32[]{:S(2)}) collective-permute-start(f32[128,256]{1,0:T(8,128)S(1)} %merge_2_0.1.rest_0_.own_ref), channel_id=1, source_target_pairs={{0,2},{1,3},{2,0},{3,1},{4,6},{5,7},{6,4},{7,5},{8,10},{9,11},{10,... | collective-permute-start | bytes 393224 | tf_op jit(solution)/shard_map/ppermute | solution.py:566
  46.5 0.0 collective-permute-done.13.other_ref
  46.5 0.2 merge_1_2.1.own_ref
  46.8 1.2 %collective-permute-start.14 = (f32[128,256]{1,0:T(8,128)S(1)}, f32[128,256]{1,0:T(8,128)S(1)}, u32[]{:S(2)}, u32[]{:S(2)}) collective-permute-start(f32[128,256]{1,0:T(8,128)S(1)} %merge_1_2.1.own_ref), channel_id=1, source_target_pairs={{0,32},{16,48},{32,0},{48,16},{64,96},{80,112},{96,64},{112,80},{1... | collective-permute-start | bytes 393224 | tf_op jit(solution)/shard_map/ppermute | solution.py:566
  47.9 0.0 collective-permute-done.7.other_ref
  47.9 0.2 merge_2_1.1.rest_0_.own_ref
  48.2 2.2 %collective-permute-start.11 = (f32[128,256]{1,0:T(8,128)S(1)}, f32[128,256]{1,0:T(8,128)S(1)}, u32[]{:S(2)}, u32[]{:S(2)}) collective-permute-start(f32[128,256]{1,0:T(8,128)S(1)} %merge_2_1.1.rest_0_.own_ref), channel_id=1, source_target_pairs={{0,2},{1,3},{2,0},{3,1},{4,6},{5,7},{6,4},{7,5},{8,10},{9,11},{10,... | collective-permute-start | bytes 393224 | tf_op jit(solution)/shard_map/ppermute | solution.py:566
  50.3 0.0 collective-permute-done.5.other_ref
  50.3 0.2 merge_1_3.1.own_ref
  50.5 1.5 %collective-permute-start.8 = (f32[128,256]{1,0:T(8,128)S(1)}, f32[128,256]{1,0:T(8,128)S(1)}, u32[]{:S(2)}, u32[]{:S(2)}) collective-permute-start(f32[128,256]{1,0:T(8,128)S(1)} %merge_1_3.1.own_ref), channel_id=1, source_target_pairs={{0,32},{16,48},{32,0},{48,16},{64,96},{80,112},{96,64},{112,80},{1... | collective-permute-start | bytes 393224 | tf_op jit(solution)/shard_map/ppermute | solution.py:566
  52.0 0.2 collective-permute-done.10.rest_0_.other_ref
  52.2 0.0 collective-permute-done.14.other_ref
  52.3 0.2 merge_2_2.1.own_ref
  52.5 2.7 %collective-permute-start.15 = (f32[128,256]{1,0:T(8,128)S(1)}, f32[128,256]{1,0:T(8,128)S(1)}, u32[]{:S(2)}, u32[]{:S(2)}) collective-permute-start(f32[128,256]{1,0:T(8,128)S(1)} %merge_2_2.1.own_ref), channel_id=1, source_target_pairs={{0,2},{1,3},{2,0},{3,1},{4,6},{5,7},{6,4},{7,5},{8,10},{9,11},{10,... | collective-permute-start | bytes 393224 | tf_op jit(solution)/shard_map/ppermute | solution.py:566
  55.2 0.0 collective-permute-done.11.rest_1_.other_ref
  55.2 0.4 collective-permute-done.8.other_ref
  55.6 0.2 merge_2_3.1.own_ref
  55.8 1.7 %collective-permute-start.12 = (f32[128,256]{1,0:T(8,128)S(1)}, f32[128,256]{1,0:T(8,128)S(1)}, u32[]{:S(2)}, u32[]{:S(2)}) collective-permute-start(f32[128,256]{1,0:T(8,128)S(1)} %merge_2_3.1.own_ref), channel_id=1, source_target_pairs={{0,2},{1,3},{2,0},{3,1},{4,6},{5,7},{6,4},{7,5},{8,10},{9,11},{10,... | collective-permute-start | bytes 393224 | tf_op jit(solution)/shard_map/ppermute | solution.py:566
  57.5 1.0 %last.1 = (f32[128,1024]{1,0:T(8,128)S(1)}, bf16[256,256]{1,0:T(8,128)(2,1)S(1)}) custom-call(s32[4]{0:T(128)S(1)} %copy-done.1, f32[128,256]{1,0:T(8,128)S(1)} %merge_0_0.1.own_ref.rest_0_), custom_call_target="tpu_custom_call" | custom-call | bytes 2960000 | tf_op jit(solution)/shard_map/last/pallas_call | solution.py:467
  58.4 1.1 %finish_0.1.rest_0_ = f32[2,64,1024]{2,1,0:T(8,128)} custom-call(f32[128,256]{1,0:T(8,128)S(1)} %merge_2_0.1.rest_0_.own_ref, f32[128,256]{1,0:T(8,128)S(1)} %collective-permute-done.10.rest_0_.other_ref, f32[128,512]{1,0:T(8,128)S(1)} %get-tuple-element.31.gamma_own_ref, f32[128,512]{1,0:T(8,128)S(1)} %get-tuple-element.32.gamma_other_ref, ...), custom_call_target="tpu_custom_call" | custom-call | bytes 3700000 | tf_op jit(solution)/shard_map/finish_0/pallas_call | solution.py:551
  59.5 1.1 %finish_1.1.rest_0_ = f32[2,64,1024]{2,1,0:T(8,128)} custom-call(f32[128,256]{1,0:T(8,128)S(1)} %merge_2_1.1.rest_0_.own_ref, f32[128,256]{1,0:T(8,128)S(1)} %collective-permute-done.11.rest_1_.other_ref, f32[128,512]{1,0:T(8,128)S(1)} %get-tuple-element.31.gamma_own_ref, ...), custom_call_target="tpu_custom_call", output_to_operand_aliasing={{}: (7, {})} | custom-call | bytes 3700000 | tf_op jit(solution)/shard_map/finish_1/pallas_call | solution.py:551
  60.6 0.0 collective-permute-done.15.other_ref
  60.6 1.1 %finish_2.1.rest_0_ = f32[2,64,1024]{2,1,0:T(8,128)} custom-call(f32[128,256]{1,0:T(8,128)S(1)} %merge_2_2.1.own_ref, f32[128,256]{1,0:T(8,128)S(1)} %collective-permute-done.15.other_ref, f32[128,512]{1,0:T(8,128)S(1)} %get-tuple-element.31.gamma_own_ref, f32[128,512]{1,0:T(8,128)S(1)} %get-tuple-element.32.gamma_other_ref, ...), custom_call_target="tpu_custom_call", output_to_operand_aliasing={{}: (7, {})} | custom-call | bytes 3700000 | tf_op jit(solution)/shard_map/finish_2/pallas_call | solution.py:551
  61.7 0.7 %collective-permute-done.12.other_ref = f32[128,256]{1,0:T(8,128)S(1)} collective-permute-done((f32[128,256]{1,0:T(8,128)S(1)}, f32[128,256]{1,0:T(8,128)S(1)}, u32[]{:S(2)}, u32[]{:S(2)}) %collective-permute-start.12) | collective-permute-done | bytes 131104 | tf_op jit(solution)/shard_map/ppermute | solution.py:566
  62.4 1.1 %finish_3.1 = f32[2,64,1024]{2,1,0:T(8,128)} custom-call(f32[128,256]{1,0:T(8,128)S(1)} %merge_2_3.1.own_ref, f32[128,256]{1,0:T(8,128)S(1)} %collective-permute-done.12.other_ref, f32[128,512]{1,0:T(8,128)S(1)} %get-tuple-element.31.gamma_own_ref, f32[128,512]{1,0:T(8,128)S(1)} %get-tuple-element.32.gamma_other_ref, ...), custom_call_target="tpu_custom_call", output_to_operand_aliasing={{}: (7, {})} | custom-call | bytes 3700000 | tf_op jit(solution)/shard_map/finish_3/pallas_call | solution.py:551
Async XLA Ops:
  2.4 20.6 %all-to-all-start = ((f32[128,1,128]{2,1,0:T(1,128)}), f32[128,1,128]{2,1,0:T(1,128)S(1)}, u32[]{:S(2)}, u32[]{:S(2)}) async-start(f32[128,1,128]{2,1,0:T(1,128)} %bitcast.6), calls=%async_computation | async-start | bytes 131072 | tf_op jit(solution)/shard_map/all_to_all | solution.py:573
  13.6 0.7 %copy-start = (s32[4]{0:T(128)S(1)}, s32[4]{0:T(128)}, u32[]{:S(2)}) copy-start(s32[4]{0:T(128)} %info_ref.5) | copy-start | bytes 52
  27.4 3.0 %collective-permute-start.1 = (f32[128,256]{1,0:T(8,128)S(1)}, f32[128,256]{1,0:T(8,128)S(1)}, u32[]{:S(2)}, u32[]{:S(2)}) collective-permute-start(f32[128,256]{1,0:T(8,128)S(1)} %leaf_0.1.rest_0_.own_ref), channel_id=1, source_target_pairs={{0,16},{16,0},{32,48},{48,32},{64,80},{80,64},{96,112},{112,96},{1... | collective-permute-start | bytes 393224 | tf_op jit(solution)/shard_map/ppermute | solution.py:566
  29.9 3.9 %collective-permute-start = (f32[128,256]{1,0:T(8,128)S(1)}, f32[128,256]{1,0:T(8,128)S(1)}, u32[]{:S(2)}, u32[]{:S(2)}) collective-permute-start(f32[128,256]{1,0:T(8,128)S(1)} %leaf_1.1.own_ref), channel_id=1, source_target_pairs={{0,16},{16,0},{32,48},{48,32},{64,80},{80,64},{96,112},{112,96},{1... | collective-permute-start | bytes 393224 | tf_op jit(solution)/shard_map/ppermute | solution.py:566
  30.7 5.5 %collective-permute-start.2 = (f32[128,256]{1,0:T(8,128)S(1)}, f32[128,256]{1,0:T(8,128)S(1)}, u32[]{:S(2)}, u32[]{:S(2)}) collective-permute-start(f32[128,256]{1,0:T(8,128)S(1)} %merge_0_0.1.own_ref.rest_0_), channel_id=1, source_target_pairs={{0,1},{1,0},{2,3},{3,2},{4,5},{5,4},{6,7},{7,6},{8,9},{9,8},{10,11... | collective-permute-start | bytes 393224 | tf_op jit(solution)/shard_map/ppermute | solution.py:566
  33.7 5.9 %collective-permute-start.4 = (f32[128,256]{1,0:T(8,128)S(1)}, f32[128,256]{1,0:T(8,128)S(1)}, u32[]{:S(2)}, u32[]{:S(2)}) collective-permute-start(f32[128,256]{1,0:T(8,128)S(1)} %leaf_2.1.own_ref), channel_id=1, source_target_pairs={{0,16},{16,0},{32,48},{48,32},{64,80},{80,64},{96,112},{112,96},{1... | collective-permute-start | bytes 393224 | tf_op jit(solution)/shard_map/ppermute | solution.py:566
  34.0 6.4 %collective-permute-start.6 = (f32[128,256]{1,0:T(8,128)S(1)}, f32[128,256]{1,0:T(8,128)S(1)}, u32[]{:S(2)}, u32[]{:S(2)}) collective-permute-start(f32[128,256]{1,0:T(8,128)S(1)} %merge_0_1.1.rest_0_.own_ref), channel_id=1, source_target_pairs={{0,1},{1,0},{2,3},{3,2},{4,5},{5,4},{6,7},{7,6},{8,9},{9,8},{10,11... | collective-permute-start | bytes 393224 | tf_op jit(solution)/shard_map/ppermute | solution.py:566
  38.6 3.6 %collective-permute-start.3 = (f32[128,256]{1,0:T(8,128)S(1)}, f32[128,256]{1,0:T(8,128)S(1)}, u32[]{:S(2)}, u32[]{:S(2)}) collective-permute-start(f32[128,256]{1,0:T(8,128)S(1)} %leaf_3.1.own_ref), channel_id=1, source_target_pairs={{0,16},{16,0},{32,48},{48,32},{64,80},{80,64},{96,112},{112,96},{1... | collective-permute-start | bytes 393224 | tf_op jit(solution)/shard_map/ppermute | solution.py:566
  38.9 5.0 %copy-start.1 = (s32[4]{0:T(128)S(1)}, s32[4]{0:T(128)}, u32[]{:S(2)}) copy-start(s32[4]{0:T(128)} %info_ref.5) | copy-start | bytes 52
  38.9 6.4 %collective-permute-start.9 = (f32[128,256]{1,0:T(8,128)S(1)}, f32[128,256]{1,0:T(8,128)S(1)}, u32[]{:S(2)}, u32[]{:S(2)}) collective-permute-start(f32[128,256]{1,0:T(8,128)S(1)} %merge_1_0.1.rest_0_.own_ref), channel_id=1, source_target_pairs={{0,32},{16,48},{32,0},{48,16},{64,96},{80,112},{96,64},{112,80},{1... | collective-permute-start | bytes 393224 | tf_op jit(solution)/shard_map/ppermute | solution.py:566
  39.8 6.7 %collective-permute-start.13 = (f32[128,256]{1,0:T(8,128)S(1)}, f32[128,256]{1,0:T(8,128)S(1)}, u32[]{:S(2)}, u32[]{:S(2)}) collective-permute-start(f32[128,256]{1,0:T(8,128)S(1)} %merge_0_2.1.rest_1_.own_ref), channel_id=1, source_target_pairs={{0,1},{1,0},{2,3},{3,2},{4,5},{5,4},{6,7},{7,6},{8,9},{9,8},{10,11... | collective-permute-start | bytes 393224 | tf_op jit(solution)/shard_map/ppermute | solution.py:566
  40.7 7.2 %collective-permute-start.7 = (f32[128,256]{1,0:T(8,128)S(1)}, f32[128,256]{1,0:T(8,128)S(1)}, u32[]{:S(2)}, u32[]{:S(2)}) collective-permute-start(f32[128,256]{1,0:T(8,128)S(1)} %merge_1_1.1.rest_1_.own_ref), channel_id=1, source_target_pairs={{0,32},{16,48},{32,0},{48,16},{64,96},{80,112},{96,64},{112,80},{1... | collective-permute-start | bytes 393224 | tf_op jit(solution)/shard_map/ppermute | solution.py:566
  42.4 7.9 %collective-permute-start.5 = (f32[128,256]{1,0:T(8,128)S(1)}, f32[128,256]{1,0:T(8,128)S(1)}, u32[]{:S(2)}, u32[]{:S(2)}) collective-permute-start(f32[128,256]{1,0:T(8,128)S(1)} %merge_0_3.1.rest_0_.own_ref), channel_id=1, source_target_pairs={{0,1},{1,0},{2,3},{3,2},{4,5},{5,4},{6,7},{7,6},{8,9},{9,8},{10,11... | collective-permute-start | bytes 393224 | tf_op jit(solution)/shard_map/ppermute | solution.py:566
  45.5 6.8 %collective-permute-start.10 = (f32[128,256]{1,0:T(8,128)S(1)}, f32[128,256]{1,0:T(8,128)S(1)}, u32[]{:S(2)}, u32[]{:S(2)}) collective-permute-start(f32[128,256]{1,0:T(8,128)S(1)} %merge_2_0.1.rest_0_.own_ref), channel_id=1, source_target_pairs={{0,2},{1,3},{2,0},{3,1},{4,6},{5,7},{6,4},{7,5},{8,10},{9,11},{10,... | collective-permute-start | bytes 393224 | tf_op jit(solution)/shard_map/ppermute | solution.py:566
  46.8 5.5 %collective-permute-start.14 = (f32[128,256]{1,0:T(8,128)S(1)}, f32[128,256]{1,0:T(8,128)S(1)}, u32[]{:S(2)}, u32[]{:S(2)}) collective-permute-start(f32[128,256]{1,0:T(8,128)S(1)} %merge_1_2.1.own_ref), channel_id=1, source_target_pairs={{0,32},{16,48},{32,0},{48,16},{64,96},{80,112},{96,64},{112,80},{1... | collective-permute-start | bytes 393224 | tf_op jit(solution)/shard_map/ppermute | solution.py:566
  48.2 7.1 %collective-permute-start.11 = (f32[128,256]{1,0:T(8,128)S(1)}, f32[128,256]{1,0:T(8,128)S(1)}, u32[]{:S(2)}, u32[]{:S(2)}) collective-permute-start(f32[128,256]{1,0:T(8,128)S(1)} %merge_2_1.1.rest_0_.own_ref), channel_id=1, source_target_pairs={{0,2},{1,3},{2,0},{3,1},{4,6},{5,7},{6,4},{7,5},{8,10},{9,11},{10,... | collective-permute-start | bytes 393224 | tf_op jit(solution)/shard_map/ppermute | solution.py:566
  50.5 5.0 %collective-permute-start.8 = (f32[128,256]{1,0:T(8,128)S(1)}, f32[128,256]{1,0:T(8,128)S(1)}, u32[]{:S(2)}, u32[]{:S(2)}) collective-permute-start(f32[128,256]{1,0:T(8,128)S(1)} %merge_1_3.1.own_ref), channel_id=1, source_target_pairs={{0,32},{16,48},{32,0},{48,16},{64,96},{80,112},{96,64},{112,80},{1... | collective-permute-start | bytes 393224 | tf_op jit(solution)/shard_map/ppermute | solution.py:566
  52.5 8.1 %collective-permute-start.15 = (f32[128,256]{1,0:T(8,128)S(1)}, f32[128,256]{1,0:T(8,128)S(1)}, u32[]{:S(2)}, u32[]{:S(2)}) collective-permute-start(f32[128,256]{1,0:T(8,128)S(1)} %merge_2_2.1.own_ref), channel_id=1, source_target_pairs={{0,2},{1,3},{2,0},{3,1},{4,6},{5,7},{6,4},{7,5},{8,10},{9,11},{10,... | collective-permute-start | bytes 393224 | tf_op jit(solution)/shard_map/ppermute | solution.py:566
  55.8 6.6 %collective-permute-start.12 = (f32[128,256]{1,0:T(8,128)S(1)}, f32[128,256]{1,0:T(8,128)S(1)}, u32[]{:S(2)}, u32[]{:S(2)}) collective-permute-start(f32[128,256]{1,0:T(8,128)S(1)} %merge_2_3.1.own_ref), channel_id=1, source_target_pairs={{0,2},{1,3},{2,0},{3,1},{4,6},{5,7},{6,4},{7,5},{8,10},{9,11},{10,... | collective-permute-start | bytes 393224 | tf_op jit(solution)/shard_map/ppermute | solution.py:566

commit v7 on v6

--- a/solution.py
+++ b/solution.py
@@ -14,7 +14,7 @@
 TGT = 32
 CAP = 32
 CHUNKS = ((0, 1), (1, 1), (2, 1), (3, 1))
-STEP = 8
+STEP = 1
 NODES = ORDER * ORDER
 TARGETS = TGT * TGT
 F32 = jnp.float32
@@ -588,7 +588,7 @@
     one1 = join(0, c1, leaf1, exchange(0, c1, leaf1))
     got0 = exchange(1, c0, one0)
     two0 = join(1, c0, one0, got0)
-    leaf3 = leaf(c3, prepared, (one1, got0))
+    leaf3 = leaf(c3, prepared, (one1,))
     one2 = join(0, c2, leaf2, exchange(0, c2, leaf2))
     one3 = join(0, c3, leaf3, exchange(0, c3, leaf3), (two0, one2))
     two1 = join(1, c1, one1, exchange(1, c1, one1))

time: 63.9 us -> 60.5 us (0.947)
  Pallas kernels: 24.2 us -> 20.5 us
    pallas_call x4, Pallas kernels: 9.43 us -> 5.72 us  [leaf(): pl.pallas_call(functools.partial(leaf_body, chunk), out_shape=jax.ShapeDt...]
  transfers between devices with their start and end apart: 17 -> 17, of which waited for: 6 -> 5; matrix products, arithmetic and copies ran while one was open for 0% -> 0% of each run, Pallas kernels for 26% -> 22%
where the time goes in v7:
time: 60.5 us; the launch traced here: 60.2 us
  starting transfers between devices  28.8 us (48%)
  Pallas kernels  20.5 us (34%)
  waiting for transfers between devices  9.81 us (16%)
  local copies, waits for them, and re-layouts  0.66 us (1%)
    ppermute x16, starting transfers between devices, swap(): lax.ppermute(value, axis, [(i, i ^ 1 << level) for i in range(lax.axis_si...  17.7 us
    all_to_all x1, starting transfers between devices, on_device(): lax.all_to_all(sent.reshape(owners, 1, -1), ('bx', 'by'), split_axis=0, c...  11.1 us
    all_to_all x1, waiting for transfers between devices, on_device(): lax.all_to_all(sent.reshape(owners, 1, -1), ('bx', 'by'), split_axis=0, c...  7.44 us
    pallas_call x4, Pallas kernels, leaf(): pl.pallas_call(functools.partial(leaf_body, chunk), out_shape=jax.ShapeDt...  5.72 us
    pallas_call x4, Pallas kernels, finish(): pl.pallas_call(functools.partial(finish_body, chunk), out_shape=jax.Shape...  4.27 us
    pallas_call x12, Pallas kernels, merge(): pl.pallas_call(functools.partial(merge_body, number, chunk), out_shape=ja...  2.53 us
    pallas_call x2, Pallas kernels, tables(): pl.pallas_call(functools.partial(tables_body, pair), out_shape=tuple(shap...  2.53 us
    pallas_call x1, Pallas kernels, pack(): pl.pallas_call(pack_body, out_shape=jax.ShapeDtypeStruct((128, 4 * CAP),...  2.43 us
  transfers between devices with their start and end apart: 17, of which 5 were waited for; matrix products, arithmetic and copies ran while one was open for 0% of the time, Pallas kernels for 22%

profile of v7, /device:TPU:0, one launch (start us, length us, event | category | flops | bytes accessed | tf_op | source)
XLA Modules:
  0.0 60.2 jit_solution(3554430073463203737)
XLA Ops:
  0.0 2.4 %pack.1 = f32[128,128]{1,0:T(8,128)} custom-call(s32[16,128]{1,0:T(8,128)} %bitcast.7, s32[2,2048]{1,0:T(2,128)} %off_ref.1, f32[2,2048]{1,0:T(2,128)} %val_ref.1), custom_call_target="tpu_custom_call" | custom-call | bytes 7400000 | tf_op jit(solution)/shard_map/pack/pallas_call | solution.py:108
  2.4 11.1 %all-to-all-start = ((f32[128,1,128]{2,1,0:T(1,128)}), f32[128,1,128]{2,1,0:T(1,128)S(1)}, u32[]{:S(2)}, u32[]{:S(2)}) async-start(f32[128,1,128]{2,1,0:T(1,128)} %bitcast.6), calls=%async_computation | async-start | bytes 131072 | tf_op jit(solution)/shard_map/all_to_all | solution.py:573
  13.6 0.0 copy-start
  13.6 0.6 %copy-done = s32[4]{0:T(128)S(1)} copy-done((s32[4]{0:T(128)S(1)}, s32[4]{0:T(128)}, u32[]{:S(2)}) %copy-start) | copy-done | bytes 40
  14.2 1.3 %tables_0.1 = (f32[128,512]{1,0:T(8,128)S(1)}, f32[128,512]{1,0:T(8,128)S(1)}, f32[128,512]{1,0:T(8,128)S(1)}, f32[128,512]{1,0:T(8,128)S(1)}, bf16[4,128,256]{2...) custom-call(s32[4]{0:T(128)S(1)} %copy-done), custom_call_target="tpu_custom_call" | custom-call | bytes 2960000 | tf_op jit(solution)/shard_map/tables_0/pallas_call | solution.py:424
  15.6 7.4 %all-to-all-done = f32[128,1,128]{2,1,0:T(1,128)S(1)} async-done(((f32[128,1,128]{2,1,0:T(1,128)}), f32[128,1,128]{2,1,0:T(1,128)S(1)}, u32[]{:S(2)}, u32[]{:S(2)}) %all-to-all-start) | async-done | bytes 65568 | tf_op jit(solution)/shard_map/all_to_all | solution.py:573
  23.0 2.1 %prepare.1 = (bf16[256,4096]{1,0:T(8,128)(2,1)S(1)}, f32[32,4,32,128]{3,2,1,0:T(8,128)S(1)}, f32[32,2,16,128]{3,2,1,0:T(8,128)S(1)}) custom-call(f32[128,128]{1,0:T(8,128)S(1)} %bitcast.5, f32[2,32,128]{2,1,0:T(8,128)S(1)} %get-tuple-element.20.speed_ref), custom_call_target="tpu_custom_call" | custom-call | bytes 7400000 | tf_op jit(solution)/shard_map/prepare/pallas_call | solution.py:195
  25.1 1.4 %leaf_0.1.rest_0_.own_ref = f32[128,256]{1,0:T(8,128)S(1)} custom-call(bf16[256,4096]{1,0:T(8,128)(2,1)S(1)} %get-tuple-element.21.l_ref, f32[32,4,32,128]{3,2,1,0:T(8,128)S(1)} %get-tuple-element.22.q_ref, f32[32,2,16,128]{3,2,1,0:T(8,128)S(1)} %get-tuple-element.23.z_ref), custom_call_target="tpu_custom_call" | custom-call | bytes 8510000 | tf_op jit(solution)/shard_map/leaf_0/pallas_call | solution.py:263
  26.5 0.1 collective-permute-start.2
  26.6 1.4 %leaf_1.1.own_ref = f32[128,256]{1,0:T(8,128)S(1)} custom-call(bf16[256,4096]{1,0:T(8,128)(2,1)S(1)} %get-tuple-element.21.l_ref, f32[32,4,32,128]{3,2,1,0:T(8,128)S(1)} %get-tuple-element.22.q_ref, f32[32,2,16,128]{3,2,1,0:T(8,128)S(1)} %get-tuple-element.23.z_ref, f32[128,256]{1,0:T(8,128)S(1)} %leaf_0.1.rest_0_.own_ref), custom_call_target="tpu_custom_call" | custom-call | bytes 8510000 | tf_op jit(solution)/shard_map/leaf_1/pallas_call | solution.py:263
  28.0 0.6 collective-permute-start
  28.6 0.0 collective-permute-done.2.other_ref
  28.6 0.2 merge_0_0.1.own_ref.rest_0_
  28.8 0.7 %collective-permute-start.3 = (f32[128,256]{1,0:T(8,128)S(1)}, f32[128,256]{1,0:T(8,128)S(1)}, u32[]{:S(2)}, u32[]{:S(2)}) collective-permute-start(f32[128,256]{1,0:T(8,128)S(1)} %merge_0_0.1.own_ref.rest_0_), channel_id=1, source_target_pairs={{0,1},{1,0},{2,3},{3,2},{4,5},{5,4},{6,7},{7,6},{8,9},{9,8},{10,11... | collective-permute-start | bytes 393224 | tf_op jit(solution)/shard_map/ppermute | solution.py:566
  29.5 1.4 %leaf_2.1.own_ref = f32[128,256]{1,0:T(8,128)S(1)} custom-call(bf16[256,4096]{1,0:T(8,128)(2,1)S(1)} %get-tuple-element.21.l_ref, f32[32,4,32,128]{3,2,1,0:T(8,128)S(1)} %get-tuple-element.22.q_ref, f32[32,2,16,128]{3,2,1,0:T(8,128)S(1)} %get-tuple-element.23.z_ref, f32[128,256]{1,0:T(8,128)S(1)} %merge_0_0.1.own_ref.rest_0_), custom_call_target="tpu_custom_call" | custom-call | bytes 8510000 | tf_op jit(solution)/shard_map/leaf_2/pallas_call | solution.py:263
  31.0 0.1 collective-permute-start.4
  31.0 0.0 collective-permute-done.other_ref
  31.1 0.2 merge_0_1.1.rest_0_.own_ref
  31.3 1.5 %collective-permute-start.6 = (f32[128,256]{1,0:T(8,128)S(1)}, f32[128,256]{1,0:T(8,128)S(1)}, u32[]{:S(2)}, u32[]{:S(2)}) collective-permute-start(f32[128,256]{1,0:T(8,128)S(1)} %merge_0_1.1.rest_0_.own_ref), channel_id=1, source_target_pairs={{0,1},{1,0},{2,3},{3,2},{4,5},{5,4},{6,7},{7,6},{8,9},{9,8},{10,11... | collective-permute-start | bytes 393224 | tf_op jit(solution)/shard_map/ppermute | solution.py:566
  32.8 1.4 %leaf_3.1.own_ref = f32[128,256]{1,0:T(8,128)S(1)} custom-call(bf16[256,4096]{1,0:T(8,128)(2,1)S(1)} %get-tuple-element.21.l_ref, f32[32,4,32,128]{3,2,1,0:T(8,128)S(1)} %get-tuple-element.22.q_ref, f32[32,2,16,128]{3,2,1,0:T(8,128)S(1)} %get-tuple-element.23.z_ref, f32[128,256]{1,0:T(8,128)S(1)} %merge_0_1.1.rest_0_.own_ref), custom_call_target="tpu_custom_call" | custom-call | bytes 8510000 | tf_op jit(solution)/shard_map/leaf_3/pallas_call | solution.py:263
  34.2 0.3 collective-permute-start.1
  34.5 0.0 collective-permute-done.3.other_ref
  34.5 0.2 merge_1_0.1.rest_0_.own_ref
  34.7 0.0 copy-start.1
  34.8 0.7 %collective-permute-start.9 = (f32[128,256]{1,0:T(8,128)S(1)}, f32[128,256]{1,0:T(8,128)S(1)}, u32[]{:S(2)}, u32[]{:S(2)}) collective-permute-start(f32[128,256]{1,0:T(8,128)S(1)} %merge_1_0.1.rest_0_.own_ref), channel_id=1, source_target_pairs={{0,32},{16,48},{32,0},{48,16},{64,96},{80,112},{96,64},{112,80},{1... | collective-permute-start | bytes 393224 | tf_op jit(solution)/shard_map/ppermute | solution.py:566
  35.5 0.0 collective-permute-done.4.other_ref
  35.5 0.2 merge_0_2.1.rest_1_.own_ref
  35.7 0.8 %collective-permute-start.13 = (f32[128,256]{1,0:T(8,128)S(1)}, f32[128,256]{1,0:T(8,128)S(1)}, u32[]{:S(2)}, u32[]{:S(2)}) collective-permute-start(f32[128,256]{1,0:T(8,128)S(1)} %merge_0_2.1.rest_1_.own_ref), channel_id=1, source_target_pairs={{0,1},{1,0},{2,3},{3,2},{4,5},{5,4},{6,7},{7,6},{8,9},{9,8},{10,11... | collective-permute-start | bytes 393224 | tf_op jit(solution)/shard_map/ppermute | solution.py:566
  36.5 0.7 %collective-permute-done.6.other_ref = f32[128,256]{1,0:T(8,128)S(1)} collective-permute-done((f32[128,256]{1,0:T(8,128)S(1)}, f32[128,256]{1,0:T(8,128)S(1)}, u32[]{:S(2)}, u32[]{:S(2)}) %collective-permute-start.6) | collective-permute-done | bytes 131104 | tf_op jit(solution)/shard_map/ppermute | solution.py:566
  37.2 0.2 merge_1_1.1.rest_1_.own_ref
  37.5 0.8 %collective-permute-start.7 = (f32[128,256]{1,0:T(8,128)S(1)}, f32[128,256]{1,0:T(8,128)S(1)}, u32[]{:S(2)}, u32[]{:S(2)}) collective-permute-start(f32[128,256]{1,0:T(8,128)S(1)} %merge_1_1.1.rest_1_.own_ref), channel_id=1, source_target_pairs={{0,32},{16,48},{32,0},{48,16},{64,96},{80,112},{96,64},{112,80},{1... | collective-permute-start | bytes 393224 | tf_op jit(solution)/shard_map/ppermute | solution.py:566
  38.2 0.0 collective-permute-done.1.other_ref
  38.2 0.2 merge_0_3.1.rest_0_.own_ref
  38.5 1.5 %collective-permute-start.5 = (f32[128,256]{1,0:T(8,128)S(1)}, f32[128,256]{1,0:T(8,128)S(1)}, u32[]{:S(2)}, u32[]{:S(2)}) collective-permute-start(f32[128,256]{1,0:T(8,128)S(1)} %merge_0_3.1.rest_0_.own_ref), channel_id=1, source_target_pairs={{0,1},{1,0},{2,3},{3,2},{4,5},{5,4},{6,7},{7,6},{8,9},{9,8},{10,11... | collective-permute-start | bytes 393224 | tf_op jit(solution)/shard_map/ppermute | solution.py:566
  40.0 0.0 copy-done.1
  40.0 1.2 %tables_1.1 = (f32[128,512]{1,0:T(8,128)S(1)}, f32[128,512]{1,0:T(8,128)S(1)}, f32[128,512]{1,0:T(8,128)S(1)}, f32[128,512]{1,0:T(8,128)S(1)}) custom-call(s32[4]{0:T(128)S(1)} %copy-done.1, f32[128,256]{1,0:T(8,128)S(1)} %merge_0_3.1.rest_0_.own_ref, f32[128,256]{1,0:T(8,128)S(1)} %merge_1_1.1.rest_1_.own_ref), custom_call_target="tpu_custom_call" | custom-call | bytes 2960000 | tf_op jit(solution)/shard_map/tables_1/pallas_call | solution.py:424
  41.2 0.0 collective-permute-done.9.other_ref
  41.2 0.2 merge_2_0.1.rest_0_.own_ref
  41.4 1.1 %collective-permute-start.10 = (f32[128,256]{1,0:T(8,128)S(1)}, f32[128,256]{1,0:T(8,128)S(1)}, u32[]{:S(2)}, u32[]{:S(2)}) collective-permute-start(f32[128,256]{1,0:T(8,128)S(1)} %merge_2_0.1.rest_0_.own_ref), channel_id=1, source_target_pairs={{0,2},{1,3},{2,0},{3,1},{4,6},{5,7},{6,4},{7,5},{8,10},{9,11},{10,... | collective-permute-start | bytes 393224 | tf_op jit(solution)/shard_map/ppermute | solution.py:566
  42.5 0.0 collective-permute-done.13.other_ref
  42.5 0.2 merge_1_2.1.own_ref
  42.7 1.5 %collective-permute-start.14 = (f32[128,256]{1,0:T(8,128)S(1)}, f32[128,256]{1,0:T(8,128)S(1)}, u32[]{:S(2)}, u32[]{:S(2)}) collective-permute-start(f32[128,256]{1,0:T(8,128)S(1)} %merge_1_2.1.own_ref), channel_id=1, source_target_pairs={{0,32},{16,48},{32,0},{48,16},{64,96},{80,112},{96,64},{112,80},{1... | collective-permute-start | bytes 393224 | tf_op jit(solution)/shard_map/ppermute | solution.py:566
  44.2 0.0 collective-permute-done.7.other_ref
  44.2 0.2 merge_2_1.1.rest_0_.own_ref
  44.4 2.5 %collective-permute-start.11 = (f32[128,256]{1,0:T(8,128)S(1)}, f32[128,256]{1,0:T(8,128)S(1)}, u32[]{:S(2)}, u32[]{:S(2)}) collective-permute-start(f32[128,256]{1,0:T(8,128)S(1)} %merge_2_1.1.rest_0_.own_ref), channel_id=1, source_target_pairs={{0,2},{1,3},{2,0},{3,1},{4,6},{5,7},{6,4},{7,5},{8,10},{9,11},{10,... | collective-permute-start | bytes 393224 | tf_op jit(solution)/shard_map/ppermute | solution.py:566
  47.0 0.0 collective-permute-done.5.other_ref
  47.0 0.2 merge_1_3.1.own_ref
  47.2 0.8 %collective-permute-start.8 = (f32[128,256]{1,0:T(8,128)S(1)}, f32[128,256]{1,0:T(8,128)S(1)}, u32[]{:S(2)}, u32[]{:S(2)}) collective-permute-start(f32[128,256]{1,0:T(8,128)S(1)} %merge_1_3.1.own_ref), channel_id=1, source_target_pairs={{0,32},{16,48},{32,0},{48,16},{64,96},{80,112},{96,64},{112,80},{1... | collective-permute-start | bytes 393224 | tf_op jit(solution)/shard_map/ppermute | solution.py:566
  48.0 0.7 %collective-permute-done.10.rest_0_.other_ref = f32[128,256]{1,0:T(8,128)S(1)} collective-permute-done((f32[128,256]{1,0:T(8,128)S(1)}, f32[128,256]{1,0:T(8,128)S(1)}, u32[]{:S(2)}, u32[]{:S(2)}) %collective-permute-start.10) | collective-permute-done | bytes 131104 | tf_op jit(solution)/shard_map/ppermute | solution.py:566
  48.6 0.0 collective-permute-done.14.other_ref
  48.6 0.2 merge_2_2.1.own_ref
  48.9 2.7 %collective-permute-start.15 = (f32[128,256]{1,0:T(8,128)S(1)}, f32[128,256]{1,0:T(8,128)S(1)}, u32[]{:S(2)}, u32[]{:S(2)}) collective-permute-start(f32[128,256]{1,0:T(8,128)S(1)} %merge_2_2.1.own_ref), channel_id=1, source_target_pairs={{0,2},{1,3},{2,0},{3,1},{4,6},{5,7},{6,4},{7,5},{8,10},{9,11},{10,... | collective-permute-start | bytes 393224 | tf_op jit(solution)/shard_map/ppermute | solution.py:566
  51.6 0.0 collective-permute-done.11.rest_1_.other_ref
  51.6 0.7 %collective-permute-done.8.other_ref = f32[128,256]{1,0:T(8,128)S(1)} collective-permute-done((f32[128,256]{1,0:T(8,128)S(1)}, f32[128,256]{1,0:T(8,128)S(1)}, u32[]{:S(2)}, u32[]{:S(2)}) %collective-permute-start.8) | collective-permute-done | bytes 131104 | tf_op jit(solution)/shard_map/ppermute | solution.py:566
  52.2 0.2 merge_2_3.1.own_ref
  52.5 2.0 %collective-permute-start.12 = (f32[128,256]{1,0:T(8,128)S(1)}, f32[128,256]{1,0:T(8,128)S(1)}, u32[]{:S(2)}, u32[]{:S(2)}) collective-permute-start(f32[128,256]{1,0:T(8,128)S(1)} %merge_2_3.1.own_ref), channel_id=1, source_target_pairs={{0,2},{1,3},{2,0},{3,1},{4,6},{5,7},{6,4},{7,5},{8,10},{9,11},{10,... | collective-permute-start | bytes 393224 | tf_op jit(solution)/shard_map/ppermute | solution.py:566
  54.5 1.0 %last.1 = (f32[128,1024]{1,0:T(8,128)S(1)}, bf16[256,256]{1,0:T(8,128)(2,1)S(1)}) custom-call(s32[4]{0:T(128)S(1)} %copy-done.1, f32[128,256]{1,0:T(8,128)S(1)} %merge_0_0.1.own_ref.rest_0_), custom_call_target="tpu_custom_call" | custom-call | bytes 2960000 | tf_op jit(solution)/shard_map/last/pallas_call | solution.py:467
  55.5 1.1 %finish_0.1.rest_0_ = f32[2,64,1024]{2,1,0:T(8,128)} custom-call(f32[128,256]{1,0:T(8,128)S(1)} %merge_2_0.1.rest_0_.own_ref, f32[128,256]{1,0:T(8,128)S(1)} %collective-permute-done.10.rest_0_.other_ref, f32[128,512]{1,0:T(8,128)S(1)} %get-tuple-element.31.gamma_own_ref, f32[128,512]{1,0:T(8,128)S(1)} %get-tuple-element.32.gamma_other_ref, ...), custom_call_target="tpu_custom_call" | custom-call | bytes 3700000 | tf_op jit(solution)/shard_map/finish_0/pallas_call | solution.py:551
  56.5 1.1 %finish_1.1.rest_0_ = f32[2,64,1024]{2,1,0:T(8,128)} custom-call(f32[128,256]{1,0:T(8,128)S(1)} %merge_2_1.1.rest_0_.own_ref, f32[128,256]{1,0:T(8,128)S(1)} %collective-permute-done.11.rest_1_.other_ref, f32[128,512]{1,0:T(8,128)S(1)} %get-tuple-element.31.gamma_own_ref, ...), custom_call_target="tpu_custom_call", output_to_operand_aliasing={{}: (7, {})} | custom-call | bytes 3700000 | tf_op jit(solution)/shard_map/finish_1/pallas_call | solution.py:551
  57.6 0.0 collective-permute-done.15.other_ref
  57.6 1.1 %finish_2.1.rest_0_ = f32[2,64,1024]{2,1,0:T(8,128)} custom-call(f32[128,256]{1,0:T(8,128)S(1)} %merge_2_2.1.own_ref, f32[128,256]{1,0:T(8,128)S(1)} %collective-permute-done.15.other_ref, f32[128,512]{1,0:T(8,128)S(1)} %get-tuple-element.31.gamma_own_ref, f32[128,512]{1,0:T(8,128)S(1)} %get-tuple-element.32.gamma_other_ref, ...), custom_call_target="tpu_custom_call", output_to_operand_aliasing={{}: (7, {})} | custom-call | bytes 3700000 | tf_op jit(solution)/shard_map/finish_2/pallas_call | solution.py:551
  58.7 0.3 collective-permute-done.12.other_ref
  59.0 1.1 %finish_3.1 = f32[2,64,1024]{2,1,0:T(8,128)} custom-call(f32[128,256]{1,0:T(8,128)S(1)} %merge_2_3.1.own_ref, f32[128,256]{1,0:T(8,128)S(1)} %collective-permute-done.12.other_ref, f32[128,512]{1,0:T(8,128)S(1)} %get-tuple-element.31.gamma_own_ref, f32[128,512]{1,0:T(8,128)S(1)} %get-tuple-element.32.gamma_other_ref, ...), custom_call_target="tpu_custom_call", output_to_operand_aliasing={{}: (7, {})} | custom-call | bytes 3700000 | tf_op jit(solution)/shard_map/finish_3/pallas_call | solution.py:551
Async XLA Ops:
  2.4 20.6 %all-to-all-start = ((f32[128,1,128]{2,1,0:T(1,128)}), f32[128,1,128]{2,1,0:T(1,128)S(1)}, u32[]{:S(2)}, u32[]{:S(2)}) async-start(f32[128,1,128]{2,1,0:T(1,128)} %bitcast.6), calls=%async_computation | async-start | bytes 131072 | tf_op jit(solution)/shard_map/all_to_all | solution.py:573
  13.6 0.7 %copy-start = (s32[4]{0:T(128)S(1)}, s32[4]{0:T(128)}, u32[]{:S(2)}) copy-start(s32[4]{0:T(128)} %info_ref.5) | copy-start | bytes 52
  26.5 2.1 %collective-permute-start.2 = (f32[128,256]{1,0:T(8,128)S(1)}, f32[128,256]{1,0:T(8,128)S(1)}, u32[]{:S(2)}, u32[]{:S(2)}) collective-permute-start(f32[128,256]{1,0:T(8,128)S(1)} %leaf_0.1.rest_0_.own_ref), channel_id=1, source_target_pairs={{0,16},{16,0},{32,48},{48,32},{64,80},{80,64},{96,112},{112,96},{1... | collective-permute-start | bytes 393224 | tf_op jit(solution)/shard_map/ppermute | solution.py:566
  28.0 3.0 %collective-permute-start = (f32[128,256]{1,0:T(8,128)S(1)}, f32[128,256]{1,0:T(8,128)S(1)}, u32[]{:S(2)}, u32[]{:S(2)}) collective-permute-start(f32[128,256]{1,0:T(8,128)S(1)} %leaf_1.1.own_ref), channel_id=1, source_target_pairs={{0,16},{16,0},{32,48},{48,32},{64,80},{80,64},{96,112},{112,96},{1... | collective-permute-start | bytes 393224 | tf_op jit(solution)/shard_map/ppermute | solution.py:566
  28.8 5.7 %collective-permute-start.3 = (f32[128,256]{1,0:T(8,128)S(1)}, f32[128,256]{1,0:T(8,128)S(1)}, u32[]{:S(2)}, u32[]{:S(2)}) collective-permute-start(f32[128,256]{1,0:T(8,128)S(1)} %merge_0_0.1.own_ref.rest_0_), channel_id=1, source_target_pairs={{0,1},{1,0},{2,3},{3,2},{4,5},{5,4},{6,7},{7,6},{8,9},{9,8},{10,11... | collective-permute-start | bytes 393224 | tf_op jit(solution)/shard_map/ppermute | solution.py:566
  31.0 4.5 %collective-permute-start.4 = (f32[128,256]{1,0:T(8,128)S(1)}, f32[128,256]{1,0:T(8,128)S(1)}, u32[]{:S(2)}, u32[]{:S(2)}) collective-permute-start(f32[128,256]{1,0:T(8,128)S(1)} %leaf_2.1.own_ref), channel_id=1, source_target_pairs={{0,16},{16,0},{32,48},{48,32},{64,80},{80,64},{96,112},{112,96},{1... | collective-permute-start | bytes 393224 | tf_op jit(solution)/shard_map/ppermute | solution.py:566
  31.3 6.0 %collective-permute-start.6 = (f32[128,256]{1,0:T(8,128)S(1)}, f32[128,256]{1,0:T(8,128)S(1)}, u32[]{:S(2)}, u32[]{:S(2)}) collective-permute-start(f32[128,256]{1,0:T(8,128)S(1)} %merge_0_1.1.rest_0_.own_ref), channel_id=1, source_target_pairs={{0,1},{1,0},{2,3},{3,2},{4,5},{5,4},{6,7},{7,6},{8,9},{9,8},{10,11... | collective-permute-start | bytes 393224 | tf_op jit(solution)/shard_map/ppermute | solution.py:566
  34.2 4.0 %collective-permute-start.1 = (f32[128,256]{1,0:T(8,128)S(1)}, f32[128,256]{1,0:T(8,128)S(1)}, u32[]{:S(2)}, u32[]{:S(2)}) collective-permute-start(f32[128,256]{1,0:T(8,128)S(1)} %leaf_3.1.own_ref), channel_id=1, source_target_pairs={{0,16},{16,0},{32,48},{48,32},{64,80},{80,64},{96,112},{112,96},{1... | collective-permute-start | bytes 393224 | tf_op jit(solution)/shard_map/ppermute | solution.py:566
  34.7 5.2 %copy-start.1 = (s32[4]{0:T(128)S(1)}, s32[4]{0:T(128)}, u32[]{:S(2)}) copy-start(s32[4]{0:T(128)} %info_ref.5) | copy-start | bytes 52
  34.8 6.4 %collective-permute-start.9 = (f32[128,256]{1,0:T(8,128)S(1)}, f32[128,256]{1,0:T(8,128)S(1)}, u32[]{:S(2)}, u32[]{:S(2)}) collective-permute-start(f32[128,256]{1,0:T(8,128)S(1)} %merge_1_0.1.rest_0_.own_ref), channel_id=1, source_target_pairs={{0,32},{16,48},{32,0},{48,16},{64,96},{80,112},{96,64},{112,80},{1... | collective-permute-start | bytes 393224 | tf_op jit(solution)/shard_map/ppermute | solution.py:566
  35.7 6.8 %collective-permute-start.13 = (f32[128,256]{1,0:T(8,128)S(1)}, f32[128,256]{1,0:T(8,128)S(1)}, u32[]{:S(2)}, u32[]{:S(2)}) collective-permute-start(f32[128,256]{1,0:T(8,128)S(1)} %merge_0_2.1.rest_1_.own_ref), channel_id=1, source_target_pairs={{0,1},{1,0},{2,3},{3,2},{4,5},{5,4},{6,7},{7,6},{8,9},{9,8},{10,11... | collective-permute-start | bytes 393224 | tf_op jit(solution)/shard_map/ppermute | solution.py:566
  37.5 6.8 %collective-permute-start.7 = (f32[128,256]{1,0:T(8,128)S(1)}, f32[128,256]{1,0:T(8,128)S(1)}, u32[]{:S(2)}, u32[]{:S(2)}) collective-permute-start(f32[128,256]{1,0:T(8,128)S(1)} %merge_1_1.1.rest_1_.own_ref), channel_id=1, source_target_pairs={{0,32},{16,48},{32,0},{48,16},{64,96},{80,112},{96,64},{112,80},{1... | collective-permute-start | bytes 393224 | tf_op jit(solution)/shard_map/ppermute | solution.py:566
  38.5 8.5 %collective-permute-start.5 = (f32[128,256]{1,0:T(8,128)S(1)}, f32[128,256]{1,0:T(8,128)S(1)}, u32[]{:S(2)}, u32[]{:S(2)}) collective-permute-start(f32[128,256]{1,0:T(8,128)S(1)} %merge_0_3.1.rest_0_.own_ref), channel_id=1, source_target_pairs={{0,1},{1,0},{2,3},{3,2},{4,5},{5,4},{6,7},{7,6},{8,9},{9,8},{10,11... | collective-permute-start | bytes 393224 | tf_op jit(solution)/shard_map/ppermute | solution.py:566
  41.4 7.2 %collective-permute-start.10 = (f32[128,256]{1,0:T(8,128)S(1)}, f32[128,256]{1,0:T(8,128)S(1)}, u32[]{:S(2)}, u32[]{:S(2)}) collective-permute-start(f32[128,256]{1,0:T(8,128)S(1)} %merge_2_0.1.rest_0_.own_ref), channel_id=1, source_target_pairs={{0,2},{1,3},{2,0},{3,1},{4,6},{5,7},{6,4},{7,5},{8,10},{9,11},{10,... | collective-permute-start | bytes 393224 | tf_op jit(solution)/shard_map/ppermute | solution.py:566
  42.7 5.9 %collective-permute-start.14 = (f32[128,256]{1,0:T(8,128)S(1)}, f32[128,256]{1,0:T(8,128)S(1)}, u32[]{:S(2)}, u32[]{:S(2)}) collective-permute-start(f32[128,256]{1,0:T(8,128)S(1)} %merge_1_2.1.own_ref), channel_id=1, source_target_pairs={{0,32},{16,48},{32,0},{48,16},{64,96},{80,112},{96,64},{112,80},{1... | collective-permute-start | bytes 393224 | tf_op jit(solution)/shard_map/ppermute | solution.py:566
  44.4 7.1 %collective-permute-start.11 = (f32[128,256]{1,0:T(8,128)S(1)}, f32[128,256]{1,0:T(8,128)S(1)}, u32[]{:S(2)}, u32[]{:S(2)}) collective-permute-start(f32[128,256]{1,0:T(8,128)S(1)} %merge_2_1.1.rest_0_.own_ref), channel_id=1, source_target_pairs={{0,2},{1,3},{2,0},{3,1},{4,6},{5,7},{6,4},{7,5},{8,10},{9,11},{10,... | collective-permute-start | bytes 393224 | tf_op jit(solution)/shard_map/ppermute | solution.py:566
  47.2 5.0 %collective-permute-start.8 = (f32[128,256]{1,0:T(8,128)S(1)}, f32[128,256]{1,0:T(8,128)S(1)}, u32[]{:S(2)}, u32[]{:S(2)}) collective-permute-start(f32[128,256]{1,0:T(8,128)S(1)} %merge_1_3.1.own_ref), channel_id=1, source_target_pairs={{0,32},{16,48},{32,0},{48,16},{64,96},{80,112},{96,64},{112,80},{1... | collective-permute-start | bytes 393224 | tf_op jit(solution)/shard_map/ppermute | solution.py:566
  48.9 8.8 %collective-permute-start.15 = (f32[128,256]{1,0:T(8,128)S(1)}, f32[128,256]{1,0:T(8,128)S(1)}, u32[]{:S(2)}, u32[]{:S(2)}) collective-permute-start(f32[128,256]{1,0:T(8,128)S(1)} %merge_2_2.1.own_ref), channel_id=1, source_target_pairs={{0,2},{1,3},{2,0},{3,1},{4,6},{5,7},{6,4},{7,5},{8,10},{9,11},{10,... | collective-permute-start | bytes 393224 | tf_op jit(solution)/shard_map/ppermute | solution.py:566
  52.5 6.6 %collective-permute-start.12 = (f32[128,256]{1,0:T(8,128)S(1)}, f32[128,256]{1,0:T(8,128)S(1)}, u32[]{:S(2)}, u32[]{:S(2)}) collective-permute-start(f32[128,256]{1,0:T(8,128)S(1)} %merge_2_3.1.own_ref), channel_id=1, source_target_pairs={{0,2},{1,3},{2,0},{3,1},{4,6},{5,7},{6,4},{7,5},{8,10},{9,11},{10,... | collective-permute-start | bytes 393224 | tf_op jit(solution)/shard_map/ppermute | solution.py:566

commit v8 on v7

--- a/solution.py
+++ b/solution.py
@@ -294,10 +294,10 @@
     return first, second
 
 
-def speeds(info_ref, klass, at):
+def speeds(coefs, klass, at):
     _, wave = turn((klass + at) * (1.0 / 32.0))
-    one = (32.0 + info_ref[0].astype(F32) + info_ref[1].astype(F32) * wave) * (1.0 / 4096.0)
-    two = (32.0 + info_ref[2].astype(F32) + info_ref[3].astype(F32) * wave) * (1.0 / 4096.0)
+    one = (32.0 + coefs[0] + coefs[1] * wave) * (1.0 / 4096.0)
+    two = (32.0 + coefs[2] + coefs[3] * wave) * (1.0 / 4096.0)
     return one, two
 
 
@@ -352,8 +352,9 @@
     return jnp.concatenate([top, bottom], axis=0)
 
 
-def tables_body(pair, info_ref, *rest):
-    gamma_refs = [rest[-6 + k] for k in range(4)] if pair == 0 else [rest[-4 + k] for k in range(4)]
+def tables_body(pair, coef_ref, *rest):
+    gamma_refs = [rest[-7 + k] for k in range(4)] if pair == 0 else [rest[-4 + k] for k in range(4)]
+    coefs = [coef_ref[k].astype(F32) for k in range(4)] if pair == 0 else [coef_ref[k : k + 1] for k in range(4)]
     index_x = lax.axis_index("bx")
     index_y = lax.axis_index("by")
     z_first, z_second = node_columns((NODES, 128))
@@ -399,17 +400,20 @@
     first = first_at + first_width * z_first
     second = second_at + second_width * z_second
     moved = first * move_first + second * move_second
-    phase = root_of(speeds(info_ref, klass, new_at), first, second) - root_of(speeds(info_ref, klass, old_at), first, second)
+    phase = root_of(speeds(coefs, klass, new_at), first, second) - root_of(speeds(coefs, klass, old_at), first, second)
     values = exact(jnp.concatenate(turn(phase + moved), axis=0))
     for k in range(4):
         spread(values, gamma_refs[k], k)
     if pair == 0:
-        mix_ref, speed_ref = rest[-2:]
+        mix_ref, speed_ref, copied_ref = rest[-3:]
+        for k in range(4):
+            copied_ref[k : k + 1] = jnp.zeros((1, 128), F32) + coefs[k]
+        copied_ref[4:] = jnp.zeros((4, 128), F32)
         order = iota((TGT, 128), 0)
         klass = (order % 16) * 2 + order // 16
         _, wave = turn((klass.astype(F32) + 1.5) * (1.0 / 32.0))
-        speed_first = (32.0 + info_ref[0].astype(F32) + info_ref[1].astype(F32) * wave) * (1.0 / 4096.0)
-        speed_second = (32.0 + info_ref[2].astype(F32) + info_ref[3].astype(F32) * wave) * (1.0 / 4096.0)
+        speed_first = (32.0 + coefs[0] + coefs[1] * wave) * (1.0 / 4096.0)
+        speed_second = (32.0 + coefs[2] + coefs[3] * wave) * (1.0 / 4096.0)
         speed_ref[0] = speed_first
         speed_ref[1] = speed_second
         for number in range(4):
@@ -421,10 +425,11 @@
     if pair == 0:
         shapes.append(jax.ShapeDtypeStruct((4, 128, 256), BF16))
         shapes.append(jax.ShapeDtypeStruct((2, TGT, 128), F32))
+        shapes.append(jax.ShapeDtypeStruct((ORDER, 128), F32))
     return pl.pallas_call(
         functools.partial(tables_body, pair),
         out_shape=tuple(shapes),
-        in_specs=[pl.BlockSpec(memory_space=pltpu.SMEM)] + anywhere(len(after)),
+        in_specs=[pl.BlockSpec(memory_space=pltpu.SMEM) if pair == 0 else vmem(1)[0]] + anywhere(len(after)),
         out_specs=vmem(len(shapes)),
         name="tables_%d" % pair,
         compiler_params=SMALL,
@@ -432,8 +437,9 @@
     )(info, *after)
 
 
-def last_body(info_ref, *rest):
+def last_body(coef_ref, *rest):
     last_ref, order_ref = rest[-2:]
+    coefs = [coef_ref[k : k + 1] for k in range(4)]
     index_x = lax.axis_index("bx")
     index_y = lax.axis_index("by")
     z_first, z_second = node_columns((NODES, 128))
@@ -447,7 +453,7 @@
     for tile in range(4):
         u = tile * 8 + lane // 16
         klass = ((u + 2 * v) % TGT).astype(F32)
-        root = root_of(speeds(info_ref, klass, new[0] + 2.0 * new[1]), first, second)
+        root = root_of(speeds(coefs, klass, new[0] + 2.0 * new[1]), first, second)
         root = root - jnp.floor(root)
         at_first = first * ((u.astype(F32) + new[0]) * (1.0 / 2048.0))
         at_first = at_first - jnp.floor(at_first) + root
@@ -467,7 +473,7 @@
     return pl.pallas_call(
         last_body,
         out_shape=(jax.ShapeDtypeStruct((2 * NODES, TARGETS), F32), jax.ShapeDtypeStruct((256, 256), BF16)),
-        in_specs=[pl.BlockSpec(memory_space=pltpu.SMEM)] + anywhere(len(after)),
+        in_specs=vmem(1) + anywhere(len(after)),
         out_specs=vmem(2),
         name="last",
         compiler_params=SMALL,
@@ -571,7 +577,7 @@
     info = coef
     sent = pack(point_box.reshape(-1, 128), point_offset, point_value)
     arrived = lax.all_to_all(sent.reshape(owners, 1, -1), ("bx", "by"), split_axis=0, concat_axis=0, tiled=True)
-    *gammas, mix, speed = tables(info, 0)
+    *gammas, mix, speed, copied = tables(info, 0)
     prepared = prepare(arrived.reshape(owners, -1), speed)
 
     def exchange(number, c, x):
@@ -592,7 +598,7 @@
     one2 = join(0, c2, leaf2, exchange(0, c2, leaf2))
     one3 = join(0, c3, leaf3, exchange(0, c3, leaf3), (two0, one2))
     two1 = join(1, c1, one1, exchange(1, c1, one1))
-    gammas += tables(info, 1, (one3, two1))
+    gammas += tables(copied, 1, (one3, two1))
     y0 = exchange(2, c0, two0)
     y1 = exchange(2, c1, two1)
     three0 = join(2, c0, two0, y0)
@@ -604,7 +610,7 @@
     three2 = join(2, c2, two2, exchange(2, c2, two2), (x0,))
     x2 = exchange(3, c2, three2)
     three3 = join(2, c3, two3, exchange(2, c3, two3), (x0, x1))
-    lasts = last_tables(info, (one0,))
+    lasts = last_tables(copied, (one0,))
     out = None
     for c, x, y in zip(CHUNKS, (three0, three1, three2, three3), (x0, x1, x2, exchange(3, c3, three3))):
         out = finish(c, x, y, gammas[6:], mix, lasts, out)

time: 60.5 us -> 60.3 us (level)
  waiting for transfers between devices: 9.81 us -> 10.9 us
    ppermute x16, waiting for transfers between devices: 2.37 us -> 3.5 us  [swap(): lax.ppermute(value, axis, [(i, i ^ 1 << level) for i in range(lax.axis_si...]
    ppermute x16, starting transfers between devices: 17.7 us -> 17.1 us  [swap(): lax.ppermute(value, axis, [(i, i ^ 1 << level) for i in range(lax.axis_si...]
  transfers between devices with their start and end apart: 17 -> 17, of which waited for: 5 -> 7; matrix products, arithmetic and copies ran while one was open for 0% -> 0% of each run, Pallas kernels for 22% -> 21%
where the time goes in v8:
time: 60.3 us; the launch traced here: 60 us
  starting transfers between devices  28.2 us (47%)
  Pallas kernels  19.9 us (33%)
  waiting for transfers between devices  10.9 us (18%)
  local copies, waits for them, and re-layouts  0.65 us (1%)
    ppermute x16, starting transfers between devices, swap(): lax.ppermute(value, axis, [(i, i ^ 1 << level) for i in range(lax.axis_si...  17.1 us
    all_to_all x1, starting transfers between devices, on_device(): lax.all_to_all(sent.reshape(owners, 1, -1), ('bx', 'by'), split_axis=0, c...  11.1 us
    all_to_all x1, waiting for transfers between devices, on_device(): lax.all_to_all(sent.reshape(owners, 1, -1), ('bx', 'by'), split_axis=0, c...  7.45 us
    pallas_call x4, Pallas kernels, leaf(): pl.pallas_call(functools.partial(leaf_body, chunk), out_shape=jax.ShapeDt...  6.16 us
    pallas_call x4, Pallas kernels, finish(): pl.pallas_call(functools.partial(finish_body, chunk), out_shape=jax.Shape...  4.26 us
    ppermute x16, waiting for transfers between devices, swap(): lax.ppermute(value, axis, [(i, i ^ 1 << level) for i in range(lax.axis_si...  3.5 us
    pallas_call x12, Pallas kernels, merge(): pl.pallas_call(functools.partial(merge_body, number, chunk), out_shape=ja...  2.52 us
    pallas_call x1, Pallas kernels, pack(): pl.pallas_call(pack_body, out_shape=jax.ShapeDtypeStruct((128, 4 * CAP),...  2.43 us
  transfers between devices with their start and end apart: 17, of which 7 were waited for; matrix products, arithmetic and copies ran while one was open for 0% of the time, Pallas kernels for 21%

profile of v8, /device:TPU:0, one launch (start us, length us, event | category | flops | bytes accessed | tf_op | source)
XLA Modules:
  0.0 60.0 jit_solution(3889241086812771785)
XLA Ops:
  0.0 2.4 %pack.1 = f32[128,128]{1,0:T(8,128)} custom-call(s32[16,128]{1,0:T(8,128)} %bitcast.7, s32[2,2048]{1,0:T(2,128)} %off_ref.1, f32[2,2048]{1,0:T(2,128)} %val_ref.1), custom_call_target="tpu_custom_call" | custom-call | bytes 7400000 | tf_op jit(solution)/shard_map/pack/pallas_call | solution.py:108
  2.4 11.1 %all-to-all-start = ((f32[128,1,128]{2,1,0:T(1,128)}), f32[128,1,128]{2,1,0:T(1,128)S(1)}, u32[]{:S(2)}, u32[]{:S(2)}) async-start(f32[128,1,128]{2,1,0:T(1,128)} %bitcast.6), calls=%async_computation | async-start | bytes 131072 | tf_op jit(solution)/shard_map/all_to_all | solution.py:579
  13.6 0.0 copy-start
  13.6 0.6 %copy-done = s32[4]{0:T(128)S(1)} copy-done((s32[4]{0:T(128)S(1)}, s32[4]{0:T(128)}, u32[]{:S(2)}) %copy-start) | copy-done | bytes 40
  14.2 1.3 %tables_0.1 = (f32[128,512]{1,0:T(8,128)S(1)}, f32[128,512]{1,0:T(8,128)S(1)}, f32[128,512]{1,0:T(8,128)S(1)}, f32[128,512]{1,0:T(8,128)S(1)}, bf16[4,128,256]{2...) custom-call(s32[4]{0:T(128)S(1)} %copy-done), custom_call_target="tpu_custom_call" | custom-call | bytes 2960000 | tf_op jit(solution)/shard_map/tables_0/pallas_call | solution.py:429
  15.5 7.4 %all-to-all-done = f32[128,1,128]{2,1,0:T(1,128)S(1)} async-done(((f32[128,1,128]{2,1,0:T(1,128)}), f32[128,1,128]{2,1,0:T(1,128)S(1)}, u32[]{:S(2)}, u32[]{:S(2)}) %all-to-all-start) | async-done | bytes 65568 | tf_op jit(solution)/shard_map/all_to_all | solution.py:579
  23.0 2.1 %prepare.1 = (bf16[256,4096]{1,0:T(8,128)(2,1)S(1)}, f32[32,4,32,128]{3,2,1,0:T(8,128)S(1)}, f32[32,2,16,128]{3,2,1,0:T(8,128)S(1)}) custom-call(f32[128,128]{1,0:T(8,128)S(1)} %bitcast.5, f32[2,32,128]{2,1,0:T(8,128)S(1)} %get-tuple-element.21.speed_ref), custom_call_target="tpu_custom_call" | custom-call | bytes 7400000 | tf_op jit(solution)/shard_map/prepare/pallas_call | solution.py:195
  25.1 1.5 %leaf_0.1.rest_0_.own_ref = f32[128,256]{1,0:T(8,128)S(1)} custom-call(bf16[256,4096]{1,0:T(8,128)(2,1)S(1)} %get-tuple-element.22.l_ref, f32[32,4,32,128]{3,2,1,0:T(8,128)S(1)} %get-tuple-element.23.q_ref, f32[32,2,16,128]{3,2,1,0:T(8,128)S(1)} %get-tuple-element.24.z_ref), custom_call_target="tpu_custom_call" | custom-call | bytes 8510000 | tf_op jit(solution)/shard_map/leaf_0/pallas_call | solution.py:263
  26.6 0.1 collective-permute-start.2
  26.7 1.6 %leaf_1.1.own_ref = f32[128,256]{1,0:T(8,128)S(1)} custom-call(bf16[256,4096]{1,0:T(8,128)(2,1)S(1)} %get-tuple-element.22.l_ref, f32[32,4,32,128]{3,2,1,0:T(8,128)S(1)} %get-tuple-element.23.q_ref, f32[32,2,16,128]{3,2,1,0:T(8,128)S(1)} %get-tuple-element.24.z_ref, f32[128,256]{1,0:T(8,128)S(1)} %leaf_0.1.rest_0_.own_ref), custom_call_target="tpu_custom_call" | custom-call | bytes 8510000 | tf_op jit(solution)/shard_map/leaf_1/pallas_call | solution.py:263
  28.3 0.6 collective-permute-start
  28.9 0.0 collective-permute-done.2.other_ref
  28.9 0.2 merge_0_0.1.own_ref.rest_0_
  29.1 0.7 %collective-permute-start.3 = (f32[128,256]{1,0:T(8,128)S(1)}, f32[128,256]{1,0:T(8,128)S(1)}, u32[]{:S(2)}, u32[]{:S(2)}) collective-permute-start(f32[128,256]{1,0:T(8,128)S(1)} %merge_0_0.1.own_ref.rest_0_), channel_id=1, source_target_pairs={{0,1},{1,0},{2,3},{3,2},{4,5},{5,4},{6,7},{7,6},{8,9},{9,8},{10,11... | collective-permute-start | bytes 393224 | tf_op jit(solution)/shard_map/ppermute | solution.py:572
  29.7 1.5 %leaf_2.1.own_ref = f32[128,256]{1,0:T(8,128)S(1)} custom-call(bf16[256,4096]{1,0:T(8,128)(2,1)S(1)} %get-tuple-element.22.l_ref, f32[32,4,32,128]{3,2,1,0:T(8,128)S(1)} %get-tuple-element.23.q_ref, f32[32,2,16,128]{3,2,1,0:T(8,128)S(1)} %get-tuple-element.24.z_ref, f32[128,256]{1,0:T(8,128)S(1)} %merge_0_0.1.own_ref.rest_0_), custom_call_target="tpu_custom_call" | custom-call | bytes 8510000 | tf_op jit(solution)/shard_map/leaf_2/pallas_call | solution.py:263
  31.3 0.1 collective-permute-start.4
  31.4 0.0 collective-permute-done.other_ref
  31.4 0.2 merge_0_1.1.rest_0_.own_ref
  31.6 1.5 %collective-permute-start.6 = (f32[128,256]{1,0:T(8,128)S(1)}, f32[128,256]{1,0:T(8,128)S(1)}, u32[]{:S(2)}, u32[]{:S(2)}) collective-permute-start(f32[128,256]{1,0:T(8,128)S(1)} %merge_0_1.1.rest_0_.own_ref), channel_id=1, source_target_pairs={{0,1},{1,0},{2,3},{3,2},{4,5},{5,4},{6,7},{7,6},{8,9},{9,8},{10,11... | collective-permute-start | bytes 393224 | tf_op jit(solution)/shard_map/ppermute | solution.py:572
  33.1 1.5 %leaf_3.1.own_ref = f32[128,256]{1,0:T(8,128)S(1)} custom-call(bf16[256,4096]{1,0:T(8,128)(2,1)S(1)} %get-tuple-element.22.l_ref, f32[32,4,32,128]{3,2,1,0:T(8,128)S(1)} %get-tuple-element.23.q_ref, f32[32,2,16,128]{3,2,1,0:T(8,128)S(1)} %get-tuple-element.24.z_ref, f32[128,256]{1,0:T(8,128)S(1)} %merge_0_1.1.rest_0_.own_ref), custom_call_target="tpu_custom_call" | custom-call | bytes 8510000 | tf_op jit(solution)/shard_map/leaf_3/pallas_call | solution.py:263
  34.7 0.3 collective-permute-start.1
  35.0 0.0 collective-permute-done.3.other_ref
  35.0 0.2 merge_1_0.1.rest_0_.own_ref
  35.2 0.7 %collective-permute-start.9 = (f32[128,256]{1,0:T(8,128)S(1)}, f32[128,256]{1,0:T(8,128)S(1)}, u32[]{:S(2)}, u32[]{:S(2)}) collective-permute-start(f32[128,256]{1,0:T(8,128)S(1)} %merge_1_0.1.rest_0_.own_ref), channel_id=1, source_target_pairs={{0,32},{16,48},{32,0},{48,16},{64,96},{80,112},{96,64},{112,80},{1... | collective-permute-start | bytes 393224 | tf_op jit(solution)/shard_map/ppermute | solution.py:572
  35.9 0.0 collective-permute-done.4.other_ref
  35.9 0.2 merge_0_2.1.rest_1_.own_ref
  36.1 0.8 %collective-permute-start.13 = (f32[128,256]{1,0:T(8,128)S(1)}, f32[128,256]{1,0:T(8,128)S(1)}, u32[]{:S(2)}, u32[]{:S(2)}) collective-permute-start(f32[128,256]{1,0:T(8,128)S(1)} %merge_0_2.1.rest_1_.own_ref), channel_id=1, source_target_pairs={{0,1},{1,0},{2,3},{3,2},{4,5},{5,4},{6,7},{7,6},{8,9},{9,8},{10,11... | collective-permute-start | bytes 393224 | tf_op jit(solution)/shard_map/ppermute | solution.py:572
  36.9 0.6 %collective-permute-done.6.other_ref = f32[128,256]{1,0:T(8,128)S(1)} collective-permute-done((f32[128,256]{1,0:T(8,128)S(1)}, f32[128,256]{1,0:T(8,128)S(1)}, u32[]{:S(2)}, u32[]{:S(2)}) %collective-permute-start.6) | collective-permute-done | bytes 131104 | tf_op jit(solution)/shard_map/ppermute | solution.py:572
  37.6 0.2 merge_1_1.1.rest_1_.own_ref
  37.8 0.9 %collective-permute-start.7 = (f32[128,256]{1,0:T(8,128)S(1)}, f32[128,256]{1,0:T(8,128)S(1)}, u32[]{:S(2)}, u32[]{:S(2)}) collective-permute-start(f32[128,256]{1,0:T(8,128)S(1)} %merge_1_1.1.rest_1_.own_ref), channel_id=1, source_target_pairs={{0,32},{16,48},{32,0},{48,16},{64,96},{80,112},{96,64},{112,80},{1... | collective-permute-start | bytes 393224 | tf_op jit(solution)/shard_map/ppermute | solution.py:572
  38.6 0.0 collective-permute-done.1.other_ref
  38.7 0.2 merge_0_3.1.rest_0_.own_ref
  38.9 1.5 %collective-permute-start.5 = (f32[128,256]{1,0:T(8,128)S(1)}, f32[128,256]{1,0:T(8,128)S(1)}, u32[]{:S(2)}, u32[]{:S(2)}) collective-permute-start(f32[128,256]{1,0:T(8,128)S(1)} %merge_0_3.1.rest_0_.own_ref), channel_id=1, source_target_pairs={{0,1},{1,0},{2,3},{3,2},{4,5},{5,4},{6,7},{7,6},{8,9},{9,8},{10,11... | collective-permute-start | bytes 393224 | tf_op jit(solution)/shard_map/ppermute | solution.py:572
  40.4 0.7 %tables_1.1 = (f32[128,512]{1,0:T(8,128)S(1)}, f32[128,512]{1,0:T(8,128)S(1)}, f32[128,512]{1,0:T(8,128)S(1)}, f32[128,512]{1,0:T(8,128)S(1)}) custom-call(f32[8,128]{1,0:T(8,128)S(1)} %get-tuple-element.30.coef_ref, f32[128,256]{1,0:T(8,128)S(1)} %merge_0_3.1.rest_0_.own_ref, f32[128,256]{1,0:T(8,128)S(1)} %merge_1_1.1.rest_1_.own_ref), custom_call_target="tpu_custom_call" | custom-call | bytes 2960000 | tf_op jit(solution)/shard_map/tables_1/pallas_call | solution.py:429
  41.1 0.5 collective-permute-done.9.other_ref
  41.6 0.2 merge_2_0.1.rest_0_.own_ref
  41.8 0.5 collective-permute-start.10
  42.3 0.3 collective-permute-done.13.other_ref
  42.6 0.2 merge_1_2.1.own_ref
  42.8 1.6 %collective-permute-start.14 = (f32[128,256]{1,0:T(8,128)S(1)}, f32[128,256]{1,0:T(8,128)S(1)}, u32[]{:S(2)}, u32[]{:S(2)}) collective-permute-start(f32[128,256]{1,0:T(8,128)S(1)} %merge_1_2.1.own_ref), channel_id=1, source_target_pairs={{0,32},{16,48},{32,0},{48,16},{64,96},{80,112},{96,64},{112,80},{1... | collective-permute-start | bytes 393224 | tf_op jit(solution)/shard_map/ppermute | solution.py:572
  44.4 0.0 collective-permute-done.7.other_ref
  44.4 0.2 merge_2_1.1.rest_0_.own_ref
  44.6 2.1 %collective-permute-start.11 = (f32[128,256]{1,0:T(8,128)S(1)}, f32[128,256]{1,0:T(8,128)S(1)}, u32[]{:S(2)}, u32[]{:S(2)}) collective-permute-start(f32[128,256]{1,0:T(8,128)S(1)} %merge_2_1.1.rest_0_.own_ref), channel_id=1, source_target_pairs={{0,2},{1,3},{2,0},{3,1},{4,6},{5,7},{6,4},{7,5},{8,10},{9,11},{10,... | collective-permute-start | bytes 393224 | tf_op jit(solution)/shard_map/ppermute | solution.py:572
  46.8 0.0 collective-permute-done.5.other_ref
  46.8 0.2 merge_1_3.1.own_ref
  47.0 1.4 %collective-permute-start.8 = (f32[128,256]{1,0:T(8,128)S(1)}, f32[128,256]{1,0:T(8,128)S(1)}, u32[]{:S(2)}, u32[]{:S(2)}) collective-permute-start(f32[128,256]{1,0:T(8,128)S(1)} %merge_1_3.1.own_ref), channel_id=1, source_target_pairs={{0,32},{16,48},{32,0},{48,16},{64,96},{80,112},{96,64},{112,80},{1... | collective-permute-start | bytes 393224 | tf_op jit(solution)/shard_map/ppermute | solution.py:572
  48.3 0.7 %collective-permute-done.10.rest_0_.other_ref = f32[128,256]{1,0:T(8,128)S(1)} collective-permute-done((f32[128,256]{1,0:T(8,128)S(1)}, f32[128,256]{1,0:T(8,128)S(1)}, u32[]{:S(2)}, u32[]{:S(2)}) %collective-permute-start.10) | collective-permute-done | bytes 131104 | tf_op jit(solution)/shard_map/ppermute | solution.py:572
  49.1 0.0 collective-permute-done.14.other_ref
  49.1 0.2 merge_2_2.1.own_ref
  49.3 2.7 %collective-permute-start.15 = (f32[128,256]{1,0:T(8,128)S(1)}, f32[128,256]{1,0:T(8,128)S(1)}, u32[]{:S(2)}, u32[]{:S(2)}) collective-permute-start(f32[128,256]{1,0:T(8,128)S(1)} %merge_2_2.1.own_ref), channel_id=1, source_target_pairs={{0,2},{1,3},{2,0},{3,1},{4,6},{5,7},{6,4},{7,5},{8,10},{9,11},{10,... | collective-permute-start | bytes 393224 | tf_op jit(solution)/shard_map/ppermute | solution.py:572
  52.0 0.0 collective-permute-done.11.rest_1_.other_ref
  52.0 0.0 collective-permute-done.8.other_ref
  52.0 0.2 merge_2_3.1.own_ref
  52.3 1.6 %collective-permute-start.12 = (f32[128,256]{1,0:T(8,128)S(1)}, f32[128,256]{1,0:T(8,128)S(1)}, u32[]{:S(2)}, u32[]{:S(2)}) collective-permute-start(f32[128,256]{1,0:T(8,128)S(1)} %merge_2_3.1.own_ref), channel_id=1, source_target_pairs={{0,2},{1,3},{2,0},{3,1},{4,6},{5,7},{6,4},{7,5},{8,10},{9,11},{10,... | collective-permute-start | bytes 393224 | tf_op jit(solution)/shard_map/ppermute | solution.py:572
  53.8 0.4 last.1
  54.3 1.1 %finish_0.1.rest_0_ = f32[2,64,1024]{2,1,0:T(8,128)} custom-call(f32[128,256]{1,0:T(8,128)S(1)} %merge_2_0.1.rest_0_.own_ref, f32[128,256]{1,0:T(8,128)S(1)} %collective-permute-done.10.rest_0_.other_ref, f32[128,512]{1,0:T(8,128)S(1)} %get-tuple-element.33.gamma_own_ref, f32[128,512]{1,0:T(8,128)S(1)} %get-tuple-element.34.gamma_other_ref, ...), custom_call_target="tpu_custom_call" | custom-call | bytes 3700000 | tf_op jit(solution)/shard_map/finish_0/pallas_call | solution.py:557
  55.3 1.1 %finish_1.1.rest_0_ = f32[2,64,1024]{2,1,0:T(8,128)} custom-call(f32[128,256]{1,0:T(8,128)S(1)} %merge_2_1.1.rest_0_.own_ref, f32[128,256]{1,0:T(8,128)S(1)} %collective-permute-done.11.rest_1_.other_ref, f32[128,512]{1,0:T(8,128)S(1)} %get-tuple-element.33.gamma_own_ref, ...), custom_call_target="tpu_custom_call", output_to_operand_aliasing={{}: (7, {})} | custom-call | bytes 3700000 | tf_op jit(solution)/shard_map/finish_1/pallas_call | solution.py:557
  56.4 0.4 collective-permute-done.15.other_ref
  56.8 1.1 %finish_2.1.rest_0_ = f32[2,64,1024]{2,1,0:T(8,128)} custom-call(f32[128,256]{1,0:T(8,128)S(1)} %merge_2_2.1.own_ref, f32[128,256]{1,0:T(8,128)S(1)} %collective-permute-done.15.other_ref, f32[128,512]{1,0:T(8,128)S(1)} %get-tuple-element.33.gamma_own_ref, f32[128,512]{1,0:T(8,128)S(1)} %get-tuple-element.34.gamma_other_ref, ...), custom_call_target="tpu_custom_call", output_to_operand_aliasing={{}: (7, {})} | custom-call | bytes 3700000 | tf_op jit(solution)/shard_map/finish_2/pallas_call | solution.py:557
  57.9 1.0 %collective-permute-done.12.other_ref = f32[128,256]{1,0:T(8,128)S(1)} collective-permute-done((f32[128,256]{1,0:T(8,128)S(1)}, f32[128,256]{1,0:T(8,128)S(1)}, u32[]{:S(2)}, u32[]{:S(2)}) %collective-permute-start.12) | collective-permute-done | bytes 131104 | tf_op jit(solution)/shard_map/ppermute | solution.py:572
  58.8 1.1 %finish_3.1 = f32[2,64,1024]{2,1,0:T(8,128)} custom-call(f32[128,256]{1,0:T(8,128)S(1)} %merge_2_3.1.own_ref, f32[128,256]{1,0:T(8,128)S(1)} %collective-permute-done.12.other_ref, f32[128,512]{1,0:T(8,128)S(1)} %get-tuple-element.33.gamma_own_ref, f32[128,512]{1,0:T(8,128)S(1)} %get-tuple-element.34.gamma_other_ref, ...), custom_call_target="tpu_custom_call", output_to_operand_aliasing={{}: (7, {})} | custom-call | bytes 3700000 | tf_op jit(solution)/shard_map/finish_3/pallas_call | solution.py:557
Async XLA Ops:
  2.4 20.6 %all-to-all-start = ((f32[128,1,128]{2,1,0:T(1,128)}), f32[128,1,128]{2,1,0:T(1,128)S(1)}, u32[]{:S(2)}, u32[]{:S(2)}) async-start(f32[128,1,128]{2,1,0:T(1,128)} %bitcast.6), calls=%async_computation | async-start | bytes 131072 | tf_op jit(solution)/shard_map/all_to_all | solution.py:579
  13.6 0.7 %copy-start = (s32[4]{0:T(128)S(1)}, s32[4]{0:T(128)}, u32[]{:S(2)}) copy-start(s32[4]{0:T(128)} %coef_ref.1) | copy-start | bytes 52
  26.6 2.2 %collective-permute-start.2 = (f32[128,256]{1,0:T(8,128)S(1)}, f32[128,256]{1,0:T(8,128)S(1)}, u32[]{:S(2)}, u32[]{:S(2)}) collective-permute-start(f32[128,256]{1,0:T(8,128)S(1)} %leaf_0.1.rest_0_.own_ref), channel_id=1, source_target_pairs={{0,16},{16,0},{32,48},{48,32},{64,80},{80,64},{96,112},{112,96},{1... | collective-permute-start | bytes 393224 | tf_op jit(solution)/shard_map/ppermute | solution.py:572
  28.3 3.1 %collective-permute-start = (f32[128,256]{1,0:T(8,128)S(1)}, f32[128,256]{1,0:T(8,128)S(1)}, u32[]{:S(2)}, u32[]{:S(2)}) collective-permute-start(f32[128,256]{1,0:T(8,128)S(1)} %leaf_1.1.own_ref), channel_id=1, source_target_pairs={{0,16},{16,0},{32,48},{48,32},{64,80},{80,64},{96,112},{112,96},{1... | collective-permute-start | bytes 393224 | tf_op jit(solution)/shard_map/ppermute | solution.py:572
  29.1 5.9 %collective-permute-start.3 = (f32[128,256]{1,0:T(8,128)S(1)}, f32[128,256]{1,0:T(8,128)S(1)}, u32[]{:S(2)}, u32[]{:S(2)}) collective-permute-start(f32[128,256]{1,0:T(8,128)S(1)} %merge_0_0.1.own_ref.rest_0_), channel_id=1, source_target_pairs={{0,1},{1,0},{2,3},{3,2},{4,5},{5,4},{6,7},{7,6},{8,9},{9,8},{10,11... | collective-permute-start | bytes 393224 | tf_op jit(solution)/shard_map/ppermute | solution.py:572
  31.3 4.6 %collective-permute-start.4 = (f32[128,256]{1,0:T(8,128)S(1)}, f32[128,256]{1,0:T(8,128)S(1)}, u32[]{:S(2)}, u32[]{:S(2)}) collective-permute-start(f32[128,256]{1,0:T(8,128)S(1)} %leaf_2.1.own_ref), channel_id=1, source_target_pairs={{0,16},{16,0},{32,48},{48,32},{64,80},{80,64},{96,112},{112,96},{1... | collective-permute-start | bytes 393224 | tf_op jit(solution)/shard_map/ppermute | solution.py:572
  31.6 6.0 %collective-permute-start.6 = (f32[128,256]{1,0:T(8,128)S(1)}, f32[128,256]{1,0:T(8,128)S(1)}, u32[]{:S(2)}, u32[]{:S(2)}) collective-permute-start(f32[128,256]{1,0:T(8,128)S(1)} %merge_0_1.1.rest_0_.own_ref), channel_id=1, source_target_pairs={{0,1},{1,0},{2,3},{3,2},{4,5},{5,4},{6,7},{7,6},{8,9},{9,8},{10,11... | collective-permute-start | bytes 393224 | tf_op jit(solution)/shard_map/ppermute | solution.py:572
  34.7 4.0 %collective-permute-start.1 = (f32[128,256]{1,0:T(8,128)S(1)}, f32[128,256]{1,0:T(8,128)S(1)}, u32[]{:S(2)}, u32[]{:S(2)}) collective-permute-start(f32[128,256]{1,0:T(8,128)S(1)} %leaf_3.1.own_ref), channel_id=1, source_target_pairs={{0,16},{16,0},{32,48},{48,32},{64,80},{80,64},{96,112},{112,96},{1... | collective-permute-start | bytes 393224 | tf_op jit(solution)/shard_map/ppermute | solution.py:572
  35.2 6.4 %collective-permute-start.9 = (f32[128,256]{1,0:T(8,128)S(1)}, f32[128,256]{1,0:T(8,128)S(1)}, u32[]{:S(2)}, u32[]{:S(2)}) collective-permute-start(f32[128,256]{1,0:T(8,128)S(1)} %merge_1_0.1.rest_0_.own_ref), channel_id=1, source_target_pairs={{0,32},{16,48},{32,0},{48,16},{64,96},{80,112},{96,64},{112,80},{1... | collective-permute-start | bytes 393224 | tf_op jit(solution)/shard_map/ppermute | solution.py:572
  36.1 6.5 %collective-permute-start.13 = (f32[128,256]{1,0:T(8,128)S(1)}, f32[128,256]{1,0:T(8,128)S(1)}, u32[]{:S(2)}, u32[]{:S(2)}) collective-permute-start(f32[128,256]{1,0:T(8,128)S(1)} %merge_0_2.1.rest_1_.own_ref), channel_id=1, source_target_pairs={{0,1},{1,0},{2,3},{3,2},{4,5},{5,4},{6,7},{7,6},{8,9},{9,8},{10,11... | collective-permute-start | bytes 393224 | tf_op jit(solution)/shard_map/ppermute | solution.py:572
  37.8 6.6 %collective-permute-start.7 = (f32[128,256]{1,0:T(8,128)S(1)}, f32[128,256]{1,0:T(8,128)S(1)}, u32[]{:S(2)}, u32[]{:S(2)}) collective-permute-start(f32[128,256]{1,0:T(8,128)S(1)} %merge_1_1.1.rest_1_.own_ref), channel_id=1, source_target_pairs={{0,32},{16,48},{32,0},{48,16},{64,96},{80,112},{96,64},{112,80},{1... | collective-permute-start | bytes 393224 | tf_op jit(solution)/shard_map/ppermute | solution.py:572
  38.9 7.9 %collective-permute-start.5 = (f32[128,256]{1,0:T(8,128)S(1)}, f32[128,256]{1,0:T(8,128)S(1)}, u32[]{:S(2)}, u32[]{:S(2)}) collective-permute-start(f32[128,256]{1,0:T(8,128)S(1)} %merge_0_3.1.rest_0_.own_ref), channel_id=1, source_target_pairs={{0,1},{1,0},{2,3},{3,2},{4,5},{5,4},{6,7},{7,6},{8,9},{9,8},{10,11... | collective-permute-start | bytes 393224 | tf_op jit(solution)/shard_map/ppermute | solution.py:572
  41.8 7.3 %collective-permute-start.10 = (f32[128,256]{1,0:T(8,128)S(1)}, f32[128,256]{1,0:T(8,128)S(1)}, u32[]{:S(2)}, u32[]{:S(2)}) collective-permute-start(f32[128,256]{1,0:T(8,128)S(1)} %merge_2_0.1.rest_0_.own_ref), channel_id=1, source_target_pairs={{0,2},{1,3},{2,0},{3,1},{4,6},{5,7},{6,4},{7,5},{8,10},{9,11},{10,... | collective-permute-start | bytes 393224 | tf_op jit(solution)/shard_map/ppermute | solution.py:572
  42.8 6.3 %collective-permute-start.14 = (f32[128,256]{1,0:T(8,128)S(1)}, f32[128,256]{1,0:T(8,128)S(1)}, u32[]{:S(2)}, u32[]{:S(2)}) collective-permute-start(f32[128,256]{1,0:T(8,128)S(1)} %merge_1_2.1.own_ref), channel_id=1, source_target_pairs={{0,32},{16,48},{32,0},{48,16},{64,96},{80,112},{96,64},{112,80},{1... | collective-permute-start | bytes 393224 | tf_op jit(solution)/shard_map/ppermute | solution.py:572
  44.6 7.4 %collective-permute-start.11 = (f32[128,256]{1,0:T(8,128)S(1)}, f32[128,256]{1,0:T(8,128)S(1)}, u32[]{:S(2)}, u32[]{:S(2)}) collective-permute-start(f32[128,256]{1,0:T(8,128)S(1)} %merge_2_1.1.rest_0_.own_ref), channel_id=1, source_target_pairs={{0,2},{1,3},{2,0},{3,1},{4,6},{5,7},{6,4},{7,5},{8,10},{9,11},{10,... | collective-permute-start | bytes 393224 | tf_op jit(solution)/shard_map/ppermute | solution.py:572
  47.0 5.1 %collective-permute-start.8 = (f32[128,256]{1,0:T(8,128)S(1)}, f32[128,256]{1,0:T(8,128)S(1)}, u32[]{:S(2)}, u32[]{:S(2)}) collective-permute-start(f32[128,256]{1,0:T(8,128)S(1)} %merge_1_3.1.own_ref), channel_id=1, source_target_pairs={{0,32},{16,48},{32,0},{48,16},{64,96},{80,112},{96,64},{112,80},{1... | collective-permute-start | bytes 393224 | tf_op jit(solution)/shard_map/ppermute | solution.py:572
  49.3 7.5 %collective-permute-start.15 = (f32[128,256]{1,0:T(8,128)S(1)}, f32[128,256]{1,0:T(8,128)S(1)}, u32[]{:S(2)}, u32[]{:S(2)}) collective-permute-start(f32[128,256]{1,0:T(8,128)S(1)} %merge_2_2.1.own_ref), channel_id=1, source_target_pairs={{0,2},{1,3},{2,0},{3,1},{4,6},{5,7},{6,4},{7,5},{8,10},{9,11},{10,... | collective-permute-start | bytes 393224 | tf_op jit(solution)/shard_map/ppermute | solution.py:572
  52.3 6.6 %collective-permute-start.12 = (f32[128,256]{1,0:T(8,128)S(1)}, f32[128,256]{1,0:T(8,128)S(1)}, u32[]{:S(2)}, u32[]{:S(2)}) collective-permute-start(f32[128,256]{1,0:T(8,128)S(1)} %merge_2_3.1.own_ref), channel_id=1, source_target_pairs={{0,2},{1,3},{2,0},{3,1},{4,6},{5,7},{6,4},{7,5},{8,10},{9,11},{10,... | collective-permute-start | bytes 393224 | tf_op jit(solution)/shard_map/ppermute | solution.py:572

commit v9 on v8

--- a/solution.py
+++ b/solution.py
@@ -93,15 +93,16 @@
         cols = slice(b * 128, (b + 1) * 128)
         values = [off_ref[0:1, cols].astype(F32), off_ref[1:2, cols].astype(F32), val_ref[0:1, cols], val_ref[1:2, cols]]
         pieces = [[], [], []]
-        for v in values:
+        for index, v in enumerate(values):
             rest = v
-            for piece in pieces:
+            for piece in pieces if index > 1 else pieces[:2]:
                 top = rest.astype(BF16).astype(F32)
                 rest = rest - top
                 piece.append(jnp.where(hit, top, 0.0).astype(BF16))
         wide.append(jnp.concatenate([x for piece in pieces for x in piece], axis=0))
     total = nt(jnp.concatenate(ones, axis=1), jnp.concatenate(wide, axis=1))
-    out_ref[...] = total[:, :128] + total[:, 128:256] + total[:, 256:]
+    out_ref[:, :64] = total[:, :64] + total[:, 128:192]
+    out_ref[:, 64:] = total[:, 64:128] + total[:, 192:256] + total[:, 256:]
 
 
 def pack(box, offsets, values):

time: 60.3 us -> 60.2 us (level)
  no operation moved by 1% of the time
where the time goes in v9:
time: 60.2 us; the launch traced here: 59.9 us
  starting transfers between devices  28.2 us (47%)
  Pallas kernels  19.8 us (33%)
  waiting for transfers between devices  10.9 us (18%)
  local copies, waits for them, and re-layouts  0.65 us (1%)
    ppermute x16, starting transfers between devices, swap(): lax.ppermute(value, axis, [(i, i ^ 1 << level) for i in range(lax.axis_si...  17.1 us
    all_to_all x1, starting transfers between devices, on_device(): lax.all_to_all(sent.reshape(owners, 1, -1), ('bx', 'by'), split_axis=0, c...  11.1 us
    all_to_all x1, waiting for transfers between devices, on_device(): lax.all_to_all(sent.reshape(owners, 1, -1), ('bx', 'by'), split_axis=0, c...  7.45 us
    pallas_call x4, Pallas kernels, leaf(): pl.pallas_call(functools.partial(leaf_body, chunk), out_shape=jax.ShapeDt...  6.17 us
    pallas_call x4, Pallas kernels, finish(): pl.pallas_call(functools.partial(finish_body, chunk), out_shape=jax.Shape...  4.26 us
    ppermute x16, waiting for transfers between devices, swap(): lax.ppermute(value, axis, [(i, i ^ 1 << level) for i in range(lax.axis_si...  3.5 us
    pallas_call x12, Pallas kernels, merge(): pl.pallas_call(functools.partial(merge_body, number, chunk), out_shape=ja...  2.52 us
    pallas_call x1, Pallas kernels, pack(): pl.pallas_call(pack_body, out_shape=jax.ShapeDtypeStruct((128, 4 * CAP),...  2.34 us
  transfers between devices with their start and end apart: 17, of which 7 were waited for; matrix products, arithmetic and copies ran while one was open for 0% of the time, Pallas kernels for 21%

profile of v9, /device:TPU:0, one launch (start us, length us, event | category | flops | bytes accessed | tf_op | source)
XLA Modules:
  0.0 59.9 jit_solution(4949817435578975267)
XLA Ops:
  0.0 2.3 %pack.1 = f32[128,128]{1,0:T(8,128)} custom-call(s32[16,128]{1,0:T(8,128)} %bitcast.7, s32[2,2048]{1,0:T(2,128)} %off_ref.1, f32[2,2048]{1,0:T(2,128)} %val_ref.1), custom_call_target="tpu_custom_call" | custom-call | bytes 7400000 | tf_op jit(solution)/shard_map/pack/pallas_call | solution.py:109
  2.3 11.1 %all-to-all-start = ((f32[128,1,128]{2,1,0:T(1,128)}), f32[128,1,128]{2,1,0:T(1,128)S(1)}, u32[]{:S(2)}, u32[]{:S(2)}) async-start(f32[128,1,128]{2,1,0:T(1,128)} %bitcast.6), calls=%async_computation | async-start | bytes 131072 | tf_op jit(solution)/shard_map/all_to_all | solution.py:580
  13.5 0.0 copy-start
  13.5 0.6 %copy-done = s32[4]{0:T(128)S(1)} copy-done((s32[4]{0:T(128)S(1)}, s32[4]{0:T(128)}, u32[]{:S(2)}) %copy-start) | copy-done | bytes 40
  14.1 1.3 %tables_0.1 = (f32[128,512]{1,0:T(8,128)S(1)}, f32[128,512]{1,0:T(8,128)S(1)}, f32[128,512]{1,0:T(8,128)S(1)}, f32[128,512]{1,0:T(8,128)S(1)}, bf16[4,128,256]{2...) custom-call(s32[4]{0:T(128)S(1)} %copy-done), custom_call_target="tpu_custom_call" | custom-call | bytes 2960000 | tf_op jit(solution)/shard_map/tables_0/pallas_call | solution.py:430
  15.4 7.4 %all-to-all-done = f32[128,1,128]{2,1,0:T(1,128)S(1)} async-done(((f32[128,1,128]{2,1,0:T(1,128)}), f32[128,1,128]{2,1,0:T(1,128)S(1)}, u32[]{:S(2)}, u32[]{:S(2)}) %all-to-all-start) | async-done | bytes 65568 | tf_op jit(solution)/shard_map/all_to_all | solution.py:580
  22.9 2.1 %prepare.1 = (bf16[256,4096]{1,0:T(8,128)(2,1)S(1)}, f32[32,4,32,128]{3,2,1,0:T(8,128)S(1)}, f32[32,2,16,128]{3,2,1,0:T(8,128)S(1)}) custom-call(f32[128,128]{1,0:T(8,128)S(1)} %bitcast.5, f32[2,32,128]{2,1,0:T(8,128)S(1)} %get-tuple-element.21.speed_ref), custom_call_target="tpu_custom_call" | custom-call | bytes 7400000 | tf_op jit(solution)/shard_map/prepare/pallas_call | solution.py:196
  25.0 1.5 %leaf_0.1.rest_0_.own_ref = f32[128,256]{1,0:T(8,128)S(1)} custom-call(bf16[256,4096]{1,0:T(8,128)(2,1)S(1)} %get-tuple-element.22.l_ref, f32[32,4,32,128]{3,2,1,0:T(8,128)S(1)} %get-tuple-element.23.q_ref, f32[32,2,16,128]{3,2,1,0:T(8,128)S(1)} %get-tuple-element.24.z_ref), custom_call_target="tpu_custom_call" | custom-call | bytes 8510000 | tf_op jit(solution)/shard_map/leaf_0/pallas_call | solution.py:264
  26.5 0.1 collective-permute-start.2
  26.6 1.6 %leaf_1.1.own_ref = f32[128,256]{1,0:T(8,128)S(1)} custom-call(bf16[256,4096]{1,0:T(8,128)(2,1)S(1)} %get-tuple-element.22.l_ref, f32[32,4,32,128]{3,2,1,0:T(8,128)S(1)} %get-tuple-element.23.q_ref, f32[32,2,16,128]{3,2,1,0:T(8,128)S(1)} %get-tuple-element.24.z_ref, f32[128,256]{1,0:T(8,128)S(1)} %leaf_0.1.rest_0_.own_ref), custom_call_target="tpu_custom_call" | custom-call | bytes 8510000 | tf_op jit(solution)/shard_map/leaf_1/pallas_call | solution.py:264
  28.2 0.6 collective-permute-start
  28.8 0.0 collective-permute-done.2.other_ref
  28.8 0.2 merge_0_0.1.own_ref.rest_0_
  29.0 0.7 %collective-permute-start.3 = (f32[128,256]{1,0:T(8,128)S(1)}, f32[128,256]{1,0:T(8,128)S(1)}, u32[]{:S(2)}, u32[]{:S(2)}) collective-permute-start(f32[128,256]{1,0:T(8,128)S(1)} %merge_0_0.1.own_ref.rest_0_), channel_id=1, source_target_pairs={{0,1},{1,0},{2,3},{3,2},{4,5},{5,4},{6,7},{7,6},{8,9},{9,8},{10,11... | collective-permute-start | bytes 393224 | tf_op jit(solution)/shard_map/ppermute | solution.py:573
  29.6 1.5 %leaf_2.1.own_ref = f32[128,256]{1,0:T(8,128)S(1)} custom-call(bf16[256,4096]{1,0:T(8,128)(2,1)S(1)} %get-tuple-element.22.l_ref, f32[32,4,32,128]{3,2,1,0:T(8,128)S(1)} %get-tuple-element.23.q_ref, f32[32,2,16,128]{3,2,1,0:T(8,128)S(1)} %get-tuple-element.24.z_ref, f32[128,256]{1,0:T(8,128)S(1)} %merge_0_0.1.own_ref.rest_0_), custom_call_target="tpu_custom_call" | custom-call | bytes 8510000 | tf_op jit(solution)/shard_map/leaf_2/pallas_call | solution.py:264
  31.2 0.1 collective-permute-start.4
  31.3 0.0 collective-permute-done.other_ref
  31.3 0.2 merge_0_1.1.rest_0_.own_ref
  31.5 1.5 %collective-permute-start.6 = (f32[128,256]{1,0:T(8,128)S(1)}, f32[128,256]{1,0:T(8,128)S(1)}, u32[]{:S(2)}, u32[]{:S(2)}) collective-permute-start(f32[128,256]{1,0:T(8,128)S(1)} %merge_0_1.1.rest_0_.own_ref), channel_id=1, source_target_pairs={{0,1},{1,0},{2,3},{3,2},{4,5},{5,4},{6,7},{7,6},{8,9},{9,8},{10,11... | collective-permute-start | bytes 393224 | tf_op jit(solution)/shard_map/ppermute | solution.py:573
  33.0 1.5 %leaf_3.1.own_ref = f32[128,256]{1,0:T(8,128)S(1)} custom-call(bf16[256,4096]{1,0:T(8,128)(2,1)S(1)} %get-tuple-element.22.l_ref, f32[32,4,32,128]{3,2,1,0:T(8,128)S(1)} %get-tuple-element.23.q_ref, f32[32,2,16,128]{3,2,1,0:T(8,128)S(1)} %get-tuple-element.24.z_ref, f32[128,256]{1,0:T(8,128)S(1)} %merge_0_1.1.rest_0_.own_ref), custom_call_target="tpu_custom_call" | custom-call | bytes 8510000 | tf_op jit(solution)/shard_map/leaf_3/pallas_call | solution.py:264
  34.6 0.3 collective-permute-start.1
  34.9 0.0 collective-permute-done.3.other_ref
  34.9 0.2 merge_1_0.1.rest_0_.own_ref
  35.1 0.7 %collective-permute-start.9 = (f32[128,256]{1,0:T(8,128)S(1)}, f32[128,256]{1,0:T(8,128)S(1)}, u32[]{:S(2)}, u32[]{:S(2)}) collective-permute-start(f32[128,256]{1,0:T(8,128)S(1)} %merge_1_0.1.rest_0_.own_ref), channel_id=1, source_target_pairs={{0,32},{16,48},{32,0},{48,16},{64,96},{80,112},{96,64},{112,80},{1... | collective-permute-start | bytes 393224 | tf_op jit(solution)/shard_map/ppermute | solution.py:573
  35.8 0.0 collective-permute-done.4.other_ref
  35.8 0.2 merge_0_2.1.rest_1_.own_ref
  36.0 0.8 %collective-permute-start.13 = (f32[128,256]{1,0:T(8,128)S(1)}, f32[128,256]{1,0:T(8,128)S(1)}, u32[]{:S(2)}, u32[]{:S(2)}) collective-permute-start(f32[128,256]{1,0:T(8,128)S(1)} %merge_0_2.1.rest_1_.own_ref), channel_id=1, source_target_pairs={{0,1},{1,0},{2,3},{3,2},{4,5},{5,4},{6,7},{7,6},{8,9},{9,8},{10,11... | collective-permute-start | bytes 393224 | tf_op jit(solution)/shard_map/ppermute | solution.py:573
  36.8 0.6 %collective-permute-done.6.other_ref = f32[128,256]{1,0:T(8,128)S(1)} collective-permute-done((f32[128,256]{1,0:T(8,128)S(1)}, f32[128,256]{1,0:T(8,128)S(1)}, u32[]{:S(2)}, u32[]{:S(2)}) %collective-permute-start.6) | collective-permute-done | bytes 131104 | tf_op jit(solution)/shard_map/ppermute | solution.py:573
  37.5 0.2 merge_1_1.1.rest_1_.own_ref
  37.7 0.9 %collective-permute-start.7 = (f32[128,256]{1,0:T(8,128)S(1)}, f32[128,256]{1,0:T(8,128)S(1)}, u32[]{:S(2)}, u32[]{:S(2)}) collective-permute-start(f32[128,256]{1,0:T(8,128)S(1)} %merge_1_1.1.rest_1_.own_ref), channel_id=1, source_target_pairs={{0,32},{16,48},{32,0},{48,16},{64,96},{80,112},{96,64},{112,80},{1... | collective-permute-start | bytes 393224 | tf_op jit(solution)/shard_map/ppermute | solution.py:573
  38.5 0.0 collective-permute-done.1.other_ref
  38.6 0.2 merge_0_3.1.rest_0_.own_ref
  38.8 1.5 %collective-permute-start.5 = (f32[128,256]{1,0:T(8,128)S(1)}, f32[128,256]{1,0:T(8,128)S(1)}, u32[]{:S(2)}, u32[]{:S(2)}) collective-permute-start(f32[128,256]{1,0:T(8,128)S(1)} %merge_0_3.1.rest_0_.own_ref), channel_id=1, source_target_pairs={{0,1},{1,0},{2,3},{3,2},{4,5},{5,4},{6,7},{7,6},{8,9},{9,8},{10,11... | collective-permute-start | bytes 393224 | tf_op jit(solution)/shard_map/ppermute | solution.py:573
  40.3 0.7 %tables_1.1 = (f32[128,512]{1,0:T(8,128)S(1)}, f32[128,512]{1,0:T(8,128)S(1)}, f32[128,512]{1,0:T(8,128)S(1)}, f32[128,512]{1,0:T(8,128)S(1)}) custom-call(f32[8,128]{1,0:T(8,128)S(1)} %get-tuple-element.30.coef_ref, f32[128,256]{1,0:T(8,128)S(1)} %merge_0_3.1.rest_0_.own_ref, f32[128,256]{1,0:T(8,128)S(1)} %merge_1_1.1.rest_1_.own_ref), custom_call_target="tpu_custom_call" | custom-call | bytes 2960000 | tf_op jit(solution)/shard_map/tables_1/pallas_call | solution.py:430
  41.0 0.5 collective-permute-done.9.other_ref
  41.5 0.2 merge_2_0.1.rest_0_.own_ref
  41.7 0.5 collective-permute-start.10
  42.2 0.3 collective-permute-done.13.other_ref
  42.5 0.2 merge_1_2.1.own_ref
  42.7 1.6 %collective-permute-start.14 = (f32[128,256]{1,0:T(8,128)S(1)}, f32[128,256]{1,0:T(8,128)S(1)}, u32[]{:S(2)}, u32[]{:S(2)}) collective-permute-start(f32[128,256]{1,0:T(8,128)S(1)} %merge_1_2.1.own_ref), channel_id=1, source_target_pairs={{0,32},{16,48},{32,0},{48,16},{64,96},{80,112},{96,64},{112,80},{1... | collective-permute-start | bytes 393224 | tf_op jit(solution)/shard_map/ppermute | solution.py:573
  44.3 0.0 collective-permute-done.7.other_ref
  44.3 0.2 merge_2_1.1.rest_0_.own_ref
  44.5 2.1 %collective-permute-start.11 = (f32[128,256]{1,0:T(8,128)S(1)}, f32[128,256]{1,0:T(8,128)S(1)}, u32[]{:S(2)}, u32[]{:S(2)}) collective-permute-start(f32[128,256]{1,0:T(8,128)S(1)} %merge_2_1.1.rest_0_.own_ref), channel_id=1, source_target_pairs={{0,2},{1,3},{2,0},{3,1},{4,6},{5,7},{6,4},{7,5},{8,10},{9,11},{10,... | collective-permute-start | bytes 393224 | tf_op jit(solution)/shard_map/ppermute | solution.py:573
  46.7 0.0 collective-permute-done.5.other_ref
  46.7 0.2 merge_1_3.1.own_ref
  46.9 1.4 %collective-permute-start.8 = (f32[128,256]{1,0:T(8,128)S(1)}, f32[128,256]{1,0:T(8,128)S(1)}, u32[]{:S(2)}, u32[]{:S(2)}) collective-permute-start(f32[128,256]{1,0:T(8,128)S(1)} %merge_1_3.1.own_ref), channel_id=1, source_target_pairs={{0,32},{16,48},{32,0},{48,16},{64,96},{80,112},{96,64},{112,80},{1... | collective-permute-start | bytes 393224 | tf_op jit(solution)/shard_map/ppermute | solution.py:573
  48.2 0.7 %collective-permute-done.10.rest_0_.other_ref = f32[128,256]{1,0:T(8,128)S(1)} collective-permute-done((f32[128,256]{1,0:T(8,128)S(1)}, f32[128,256]{1,0:T(8,128)S(1)}, u32[]{:S(2)}, u32[]{:S(2)}) %collective-permute-start.10) | collective-permute-done | bytes 131104 | tf_op jit(solution)/shard_map/ppermute | solution.py:573
  49.0 0.0 collective-permute-done.14.other_ref
  49.0 0.2 merge_2_2.1.own_ref
  49.2 2.7 %collective-permute-start.15 = (f32[128,256]{1,0:T(8,128)S(1)}, f32[128,256]{1,0:T(8,128)S(1)}, u32[]{:S(2)}, u32[]{:S(2)}) collective-permute-start(f32[128,256]{1,0:T(8,128)S(1)} %merge_2_2.1.own_ref), channel_id=1, source_target_pairs={{0,2},{1,3},{2,0},{3,1},{4,6},{5,7},{6,4},{7,5},{8,10},{9,11},{10,... | collective-permute-start | bytes 393224 | tf_op jit(solution)/shard_map/ppermute | solution.py:573
  51.9 0.0 collective-permute-done.11.rest_1_.other_ref
  51.9 0.0 collective-permute-done.8.other_ref
  51.9 0.2 merge_2_3.1.own_ref
  52.2 1.6 %collective-permute-start.12 = (f32[128,256]{1,0:T(8,128)S(1)}, f32[128,256]{1,0:T(8,128)S(1)}, u32[]{:S(2)}, u32[]{:S(2)}) collective-permute-start(f32[128,256]{1,0:T(8,128)S(1)} %merge_2_3.1.own_ref), channel_id=1, source_target_pairs={{0,2},{1,3},{2,0},{3,1},{4,6},{5,7},{6,4},{7,5},{8,10},{9,11},{10,... | collective-permute-start | bytes 393224 | tf_op jit(solution)/shard_map/ppermute | solution.py:573
  53.7 0.4 last.1
  54.2 1.1 %finish_0.1.rest_0_ = f32[2,64,1024]{2,1,0:T(8,128)} custom-call(f32[128,256]{1,0:T(8,128)S(1)} %merge_2_0.1.rest_0_.own_ref, f32[128,256]{1,0:T(8,128)S(1)} %collective-permute-done.10.rest_0_.other_ref, f32[128,512]{1,0:T(8,128)S(1)} %get-tuple-element.33.gamma_own_ref, f32[128,512]{1,0:T(8,128)S(1)} %get-tuple-element.34.gamma_other_ref, ...), custom_call_target="tpu_custom_call" | custom-call | bytes 3700000 | tf_op jit(solution)/shard_map/finish_0/pallas_call | solution.py:558
  55.2 1.1 %finish_1.1.rest_0_ = f32[2,64,1024]{2,1,0:T(8,128)} custom-call(f32[128,256]{1,0:T(8,128)S(1)} %merge_2_1.1.rest_0_.own_ref, f32[128,256]{1,0:T(8,128)S(1)} %collective-permute-done.11.rest_1_.other_ref, f32[128,512]{1,0:T(8,128)S(1)} %get-tuple-element.33.gamma_own_ref, ...), custom_call_target="tpu_custom_call", output_to_operand_aliasing={{}: (7, {})} | custom-call | bytes 3700000 | tf_op jit(solution)/shard_map/finish_1/pallas_call | solution.py:558
  56.3 0.4 collective-permute-done.15.other_ref
  56.7 1.1 %finish_2.1.rest_0_ = f32[2,64,1024]{2,1,0:T(8,128)} custom-call(f32[128,256]{1,0:T(8,128)S(1)} %merge_2_2.1.own_ref, f32[128,256]{1,0:T(8,128)S(1)} %collective-permute-done.15.other_ref, f32[128,512]{1,0:T(8,128)S(1)} %get-tuple-element.33.gamma_own_ref, f32[128,512]{1,0:T(8,128)S(1)} %get-tuple-element.34.gamma_other_ref, ...), custom_call_target="tpu_custom_call", output_to_operand_aliasing={{}: (7, {})} | custom-call | bytes 3700000 | tf_op jit(solution)/shard_map/finish_2/pallas_call | solution.py:558
  57.8 1.0 %collective-permute-done.12.other_ref = f32[128,256]{1,0:T(8,128)S(1)} collective-permute-done((f32[128,256]{1,0:T(8,128)S(1)}, f32[128,256]{1,0:T(8,128)S(1)}, u32[]{:S(2)}, u32[]{:S(2)}) %collective-permute-start.12) | collective-permute-done | bytes 131104 | tf_op jit(solution)/shard_map/ppermute | solution.py:573
  58.7 1.1 %finish_3.1 = f32[2,64,1024]{2,1,0:T(8,128)} custom-call(f32[128,256]{1,0:T(8,128)S(1)} %merge_2_3.1.own_ref, f32[128,256]{1,0:T(8,128)S(1)} %collective-permute-done.12.other_ref, f32[128,512]{1,0:T(8,128)S(1)} %get-tuple-element.33.gamma_own_ref, f32[128,512]{1,0:T(8,128)S(1)} %get-tuple-element.34.gamma_other_ref, ...), custom_call_target="tpu_custom_call", output_to_operand_aliasing={{}: (7, {})} | custom-call | bytes 3700000 | tf_op jit(solution)/shard_map/finish_3/pallas_call | solution.py:558
Async XLA Ops:
  2.3 20.6 %all-to-all-start = ((f32[128,1,128]{2,1,0:T(1,128)}), f32[128,1,128]{2,1,0:T(1,128)S(1)}, u32[]{:S(2)}, u32[]{:S(2)}) async-start(f32[128,1,128]{2,1,0:T(1,128)} %bitcast.6), calls=%async_computation | async-start | bytes 131072 | tf_op jit(solution)/shard_map/all_to_all | solution.py:580
  13.5 0.7 %copy-start = (s32[4]{0:T(128)S(1)}, s32[4]{0:T(128)}, u32[]{:S(2)}) copy-start(s32[4]{0:T(128)} %coef_ref.1) | copy-start | bytes 52
  26.5 2.2 %collective-permute-start.2 = (f32[128,256]{1,0:T(8,128)S(1)}, f32[128,256]{1,0:T(8,128)S(1)}, u32[]{:S(2)}, u32[]{:S(2)}) collective-permute-start(f32[128,256]{1,0:T(8,128)S(1)} %leaf_0.1.rest_0_.own_ref), channel_id=1, source_target_pairs={{0,16},{16,0},{32,48},{48,32},{64,80},{80,64},{96,112},{112,96},{1... | collective-permute-start | bytes 393224 | tf_op jit(solution)/shard_map/ppermute | solution.py:573
  28.2 3.1 %collective-permute-start = (f32[128,256]{1,0:T(8,128)S(1)}, f32[128,256]{1,0:T(8,128)S(1)}, u32[]{:S(2)}, u32[]{:S(2)}) collective-permute-start(f32[128,256]{1,0:T(8,128)S(1)} %leaf_1.1.own_ref), channel_id=1, source_target_pairs={{0,16},{16,0},{32,48},{48,32},{64,80},{80,64},{96,112},{112,96},{1... | collective-permute-start | bytes 393224 | tf_op jit(solution)/shard_map/ppermute | solution.py:573
  29.0 5.9 %collective-permute-start.3 = (f32[128,256]{1,0:T(8,128)S(1)}, f32[128,256]{1,0:T(8,128)S(1)}, u32[]{:S(2)}, u32[]{:S(2)}) collective-permute-start(f32[128,256]{1,0:T(8,128)S(1)} %merge_0_0.1.own_ref.rest_0_), channel_id=1, source_target_pairs={{0,1},{1,0},{2,3},{3,2},{4,5},{5,4},{6,7},{7,6},{8,9},{9,8},{10,11... | collective-permute-start | bytes 393224 | tf_op jit(solution)/shard_map/ppermute | solution.py:573
  31.2 4.6 %collective-permute-start.4 = (f32[128,256]{1,0:T(8,128)S(1)}, f32[128,256]{1,0:T(8,128)S(1)}, u32[]{:S(2)}, u32[]{:S(2)}) collective-permute-start(f32[128,256]{1,0:T(8,128)S(1)} %leaf_2.1.own_ref), channel_id=1, source_target_pairs={{0,16},{16,0},{32,48},{48,32},{64,80},{80,64},{96,112},{112,96},{1... | collective-permute-start | bytes 393224 | tf_op jit(solution)/shard_map/ppermute | solution.py:573
  31.5 6.0 %collective-permute-start.6 = (f32[128,256]{1,0:T(8,128)S(1)}, f32[128,256]{1,0:T(8,128)S(1)}, u32[]{:S(2)}, u32[]{:S(2)}) collective-permute-start(f32[128,256]{1,0:T(8,128)S(1)} %merge_0_1.1.rest_0_.own_ref), channel_id=1, source_target_pairs={{0,1},{1,0},{2,3},{3,2},{4,5},{5,4},{6,7},{7,6},{8,9},{9,8},{10,11... | collective-permute-start | bytes 393224 | tf_op jit(solution)/shard_map/ppermute | solution.py:573
  34.6 4.0 %collective-permute-start.1 = (f32[128,256]{1,0:T(8,128)S(1)}, f32[128,256]{1,0:T(8,128)S(1)}, u32[]{:S(2)}, u32[]{:S(2)}) collective-permute-start(f32[128,256]{1,0:T(8,128)S(1)} %leaf_3.1.own_ref), channel_id=1, source_target_pairs={{0,16},{16,0},{32,48},{48,32},{64,80},{80,64},{96,112},{112,96},{1... | collective-permute-start | bytes 393224 | tf_op jit(solution)/shard_map/ppermute | solution.py:573
  35.1 6.4 %collective-permute-start.9 = (f32[128,256]{1,0:T(8,128)S(1)}, f32[128,256]{1,0:T(8,128)S(1)}, u32[]{:S(2)}, u32[]{:S(2)}) collective-permute-start(f32[128,256]{1,0:T(8,128)S(1)} %merge_1_0.1.rest_0_.own_ref), channel_id=1, source_target_pairs={{0,32},{16,48},{32,0},{48,16},{64,96},{80,112},{96,64},{112,80},{1... | collective-permute-start | bytes 393224 | tf_op jit(solution)/shard_map/ppermute | solution.py:573
  36.0 6.5 %collective-permute-start.13 = (f32[128,256]{1,0:T(8,128)S(1)}, f32[128,256]{1,0:T(8,128)S(1)}, u32[]{:S(2)}, u32[]{:S(2)}) collective-permute-start(f32[128,256]{1,0:T(8,128)S(1)} %merge_0_2.1.rest_1_.own_ref), channel_id=1, source_target_pairs={{0,1},{1,0},{2,3},{3,2},{4,5},{5,4},{6,7},{7,6},{8,9},{9,8},{10,11... | collective-permute-start | bytes 393224 | tf_op jit(solution)/shard_map/ppermute | solution.py:573
  37.7 6.6 %collective-permute-start.7 = (f32[128,256]{1,0:T(8,128)S(1)}, f32[128,256]{1,0:T(8,128)S(1)}, u32[]{:S(2)}, u32[]{:S(2)}) collective-permute-start(f32[128,256]{1,0:T(8,128)S(1)} %merge_1_1.1.rest_1_.own_ref), channel_id=1, source_target_pairs={{0,32},{16,48},{32,0},{48,16},{64,96},{80,112},{96,64},{112,80},{1... | collective-permute-start | bytes 393224 | tf_op jit(solution)/shard_map/ppermute | solution.py:573
  38.8 7.9 %collective-permute-start.5 = (f32[128,256]{1,0:T(8,128)S(1)}, f32[128,256]{1,0:T(8,128)S(1)}, u32[]{:S(2)}, u32[]{:S(2)}) collective-permute-start(f32[128,256]{1,0:T(8,128)S(1)} %merge_0_3.1.rest_0_.own_ref), channel_id=1, source_target_pairs={{0,1},{1,0},{2,3},{3,2},{4,5},{5,4},{6,7},{7,6},{8,9},{9,8},{10,11... | collective-permute-start | bytes 393224 | tf_op jit(solution)/shard_map/ppermute | solution.py:573
  41.7 7.3 %collective-permute-start.10 = (f32[128,256]{1,0:T(8,128)S(1)}, f32[128,256]{1,0:T(8,128)S(1)}, u32[]{:S(2)}, u32[]{:S(2)}) collective-permute-start(f32[128,256]{1,0:T(8,128)S(1)} %merge_2_0.1.rest_0_.own_ref), channel_id=1, source_target_pairs={{0,2},{1,3},{2,0},{3,1},{4,6},{5,7},{6,4},{7,5},{8,10},{9,11},{10,... | collective-permute-start | bytes 393224 | tf_op jit(solution)/shard_map/ppermute | solution.py:573
  42.7 6.3 %collective-permute-start.14 = (f32[128,256]{1,0:T(8,128)S(1)}, f32[128,256]{1,0:T(8,128)S(1)}, u32[]{:S(2)}, u32[]{:S(2)}) collective-permute-start(f32[128,256]{1,0:T(8,128)S(1)} %merge_1_2.1.own_ref), channel_id=1, source_target_pairs={{0,32},{16,48},{32,0},{48,16},{64,96},{80,112},{96,64},{112,80},{1... | collective-permute-start | bytes 393224 | tf_op jit(solution)/shard_map/ppermute | solution.py:573
  44.5 7.4 %collective-permute-start.11 = (f32[128,256]{1,0:T(8,128)S(1)}, f32[128,256]{1,0:T(8,128)S(1)}, u32[]{:S(2)}, u32[]{:S(2)}) collective-permute-start(f32[128,256]{1,0:T(8,128)S(1)} %merge_2_1.1.rest_0_.own_ref), channel_id=1, source_target_pairs={{0,2},{1,3},{2,0},{3,1},{4,6},{5,7},{6,4},{7,5},{8,10},{9,11},{10,... | collective-permute-start | bytes 393224 | tf_op jit(solution)/shard_map/ppermute | solution.py:573
  46.9 5.1 %collective-permute-start.8 = (f32[128,256]{1,0:T(8,128)S(1)}, f32[128,256]{1,0:T(8,128)S(1)}, u32[]{:S(2)}, u32[]{:S(2)}) collective-permute-start(f32[128,256]{1,0:T(8,128)S(1)} %merge_1_3.1.own_ref), channel_id=1, source_target_pairs={{0,32},{16,48},{32,0},{48,16},{64,96},{80,112},{96,64},{112,80},{1... | collective-permute-start | bytes 393224 | tf_op jit(solution)/shard_map/ppermute | solution.py:573
  49.2 7.5 %collective-permute-start.15 = (f32[128,256]{1,0:T(8,128)S(1)}, f32[128,256]{1,0:T(8,128)S(1)}, u32[]{:S(2)}, u32[]{:S(2)}) collective-permute-start(f32[128,256]{1,0:T(8,128)S(1)} %merge_2_2.1.own_ref), channel_id=1, source_target_pairs={{0,2},{1,3},{2,0},{3,1},{4,6},{5,7},{6,4},{7,5},{8,10},{9,11},{10,... | collective-permute-start | bytes 393224 | tf_op jit(solution)/shard_map/ppermute | solution.py:573
  52.2 6.6 %collective-permute-start.12 = (f32[128,256]{1,0:T(8,128)S(1)}, f32[128,256]{1,0:T(8,128)S(1)}, u32[]{:S(2)}, u32[]{:S(2)}) collective-permute-start(f32[128,256]{1,0:T(8,128)S(1)} %merge_2_3.1.own_ref), channel_id=1, source_target_pairs={{0,2},{1,3},{2,0},{3,1},{4,6},{5,7},{6,4},{7,5},{8,10},{9,11},{10,... | collective-permute-start | bytes 393224 | tf_op jit(solution)/shard_map/ppermute | solution.py:573
